TPU v7x, 128 devices: a whole 4x4x4 slice. The times are simulated.
128 devices in a mesh: energy: 8 (over y, core), layer: 16 (over x, z).
Axes of the slice: x: 4, y: 4, z: 4, core: 2. Of those that a mesh axis runs over, the one named last changes fastest.
Arguments:
- correlations: bfloat16 [128, 16, 4, 256, 256], P(('energy', 'layer')), may hold values from -6 to 6
- retarded: bfloat16 [128, 16, 2, 256, 256], P(('energy', 'layer')), may hold values from -0.15625 to 0.15625
- coupling: bfloat16 [16, 256, 256], P('layer'), may hold values from -0.375 to 0.375
- phonon_shifts: int32 [4], replicated, may hold values from 1 to 4, as said below
- phonon_coupling: float32 [4], replicated, may hold values from 0.3 to 1.2
- layer_orbitals: int32 [16], P('layer'), may hold values from 128 to 256, as said below
Outputs:
- left_correlations: bfloat16 [128, 16, 4, 256, 256], P('energy', 'layer')
Inputs may be any that keep to these rules, and one draw needn't show every extreme that they name: `phonon_shifts`: one of the offsets equals 4. `layer_orbitals`: some layer has all 256 orbitals live.
All inputs are finite; a program needn't handle non-finite values.
Results may differ from a plain program's by a relative error of at most 0.025.
Values may be sent and summed in bfloat16 or wider, within the bound.
No kernel may reach another device: no remote copies, remote signals or barrier semaphores. Data moves between devices by JAX's collectives and lax.ppermute only.
A program may use at most 128 MiB of HBM per device.

v0:
```python
import jax
import jax.numpy as jnp
from jax import lax
from jax.sharding import PartitionSpec as P

MODES = 4
SHIFT_MAX = 4


bose_ratio = 0.5


def with_halo(block, sides, width):
    for axis, dim in sides:
        count = lax.axis_size(axis)
        forward = [(i, i + 1) for i in range(count - 1)]
        backward = [(target, source) for source, target in forward]
        low = lax.ppermute(
            lax.slice_in_dim(block, block.shape[dim] - width, None, axis=dim), axis, forward
        )
        high = lax.ppermute(lax.slice_in_dim(block, 0, width, axis=dim), axis, backward)
        block = jnp.concatenate([low, block, high], axis=dim)
    return block


def mode_weights(shift_value):
    occupation = 1.0 / (jnp.exp(bose_ratio * shift_value.astype(jnp.float32)) - 1.0)
    lower_weight = jnp.stack([occupation, occupation, occupation + 1.0, occupation + 1.0])
    upper_weight = jnp.stack([occupation + 1.0, occupation + 1.0, occupation, occupation])
    return (lower_weight, upper_weight)


def left_product(matrix, stacked_block):
    return jnp.einsum(
        "...ab,...kbc->...kac", matrix, stacked_block, preferred_element_type=jnp.float32
    )


def right_product(stacked_block, matrix):
    return jnp.einsum(
        "...kab,...cb->...kac", stacked_block, matrix, preferred_element_type=jnp.float32
    )


def advance(previous, sigma_block, green_block, coupling_block):
    halfway = jnp.einsum(
        "...kab,cb->...kac", previous, coupling_block, preferred_element_type=jnp.float32
    ).astype(jnp.bfloat16)
    spread = jnp.einsum(
        "ab,...kbc->...kac", coupling_block, halfway, preferred_element_type=jnp.float32
    )
    source = (sigma_block.astype(jnp.float32) + spread).astype(jnp.bfloat16)
    green_real = green_block[..., 0, :, :]
    green_imag = green_block[..., 1, :, :]
    source_real = source[..., 0::2, :, :]
    source_imag = source[..., 1::2, :, :]
    inner_real = (
        left_product(green_real, source_real) - left_product(green_imag, source_imag)
    ).astype(jnp.bfloat16)
    inner_imag = (
        left_product(green_real, source_imag) + left_product(green_imag, source_real)
    ).astype(jnp.bfloat16)
    outer_real = right_product(inner_real, green_real) + right_product(inner_imag, green_imag)
    outer_imag = right_product(inner_imag, green_real) - right_product(inner_real, green_imag)
    stacked = jnp.stack([outer_real, outer_imag], axis=-3)
    return stacked.reshape(stacked.shape[:-4] + (4,) + stacked.shape[-2:]).astype(jnp.bfloat16)


def body(correlations, retarded, coupling, phonon_shifts, phonon_coupling, layer_orbitals):
    regrouped = lax.all_to_all(correlations, "layer", split_axis=1, concat_axis=0, tiled=True)
    energies_here = regrouped.shape[0]
    orbital_count = regrouped.shape[-1]
    padded = with_halo(regrouped, (("energy", 0),), SHIFT_MAX)
    accumulated = jnp.zeros(regrouped.shape, jnp.float32)
    for mode_index in range(MODES):
        shift_value = phonon_shifts[mode_index]
        lower_weight, upper_weight = mode_weights(shift_value)
        lower_block = lax.dynamic_slice_in_dim(padded, SHIFT_MAX - shift_value, energies_here, 0)
        upper_block = lax.dynamic_slice_in_dim(padded, SHIFT_MAX + shift_value, energies_here, 0)
        accumulated = accumulated + phonon_coupling[mode_index] * (
            lower_weight[:, None, None] * lower_block.astype(jnp.float32)
            + upper_weight[:, None, None] * upper_block.astype(jnp.float32)
        )
    orbital_index = jnp.arange(orbital_count, dtype=jnp.int32)
    live_count = layer_orbitals[:, None, None, None]
    live_mask = (orbital_index[:, None] < live_count) & (orbital_index[None, :] < live_count)
    sigma_blocks = jnp.where(live_mask, accumulated, 0.0).astype(jnp.bfloat16)
    returned = lax.all_to_all(sigma_blocks, "layer", split_axis=0, concat_axis=1, tiled=True)
    couplings = lax.all_gather(coupling, "layer", axis=0, tiled=True)
    layer_total = returned.shape[1]

    def layer_step(layer_index, state):
        previous, finished = state
        current = advance(
            previous,
            lax.dynamic_index_in_dim(returned, layer_index, 1, keepdims=False),
            lax.dynamic_index_in_dim(retarded, layer_index, 1, keepdims=False),
            lax.dynamic_index_in_dim(couplings, layer_index, 0, keepdims=False),
        )
        finished = lax.dynamic_update_index_in_dim(finished, current, layer_index, 1)
        return (current, finished)

    _, finished = lax.fori_loop(
        0, layer_total, layer_step, (correlations[:, 0], jnp.zeros_like(correlations))
    )
    return lax.all_to_all(finished, "layer", split_axis=1, concat_axis=0, tiled=True)


def solution(mesh):
    return jax.shard_map(
        body,
        mesh=mesh,
        in_specs=(
            P(("energy", "layer"), None, None, None, None),
            P(("energy", "layer"), None, None, None, None),
            P("layer", None, None),
            P(),
            P(),
            P("layer"),
        ),
        out_specs=P("energy", "layer", None, None, None),
        check_vma=False,
    )
```

profile of v0, /device:TPU:8, one launch (start us, length us, event | category | flops | bytes accessed | tf_op | source)
XLA Modules:
  0.0 559.1 jit_solution(11851508432102478930)
XLA Ops:
  6.5 12.2 %copy.25 = bf16[1,16,4,256,256]{3,4,2,0,1:T(8,128)(2,1)} copy(bf16[1,16,4,256,256]{4,3,2,1,0:T(8,128)(2,1)} %param.8) | data formatting | bytes 16777216 | tf_op args[0]
  18.8 104.3 %all_to_all.39 = bf16[1,16,4,256,256]{3,4,2,0,1:T(8,128)(2,1)S(1)} all-to-all(bf16[1,16,4,256,256]{3,4,2,0,1:T(8,128)(2,1)} %copy.25), channel_id=1, replica_groups=mesh['energy'=8,'layer'=16] {'layer'}, dimensions={1} | all-to-all | bytes 16777216 | tf_op jit(solution)/shard_map/all_to_all | solution.py:70
  124.7 2.4 copy-done
  128.6 1.9 collective-permute-start.1
  130.6 2.4 collective-permute-start
  148.3 6.1 %collective-permute-done.1 = bf16[4,1,4,256,256]{3,4,2,0,1:T(8,128)(2,1)S(1)} collective-permute-done((bf16[4,1,4,256,256]{3,4,2,0,1:T(8,128)(2,1)}, bf16[4,1,4,256,256]{3,4,2,0,1:T(8,128)(2,1)S(1)}, u32[]{:S(2)}, u32[]{:S(2)}) %collective-permute-start.1) | collective-permute-done | bytes 2097184 | tf_op jit(solution)/shard_map/ppermute | solution.py:21
  154.4 3.8 collective-permute-done
  158.2 6.4 %pad_maximum_fusion = bf16[24,1,4,256,256]{3,4,2,0,1:T(8,128)(2,1)S(1)} fusion(bf16[4,1,4,256,256]{3,4,2,0,1:T(8,128)(2,1)} %copy-done.1, bf16[16,1,4,256,256]{3,4,2,0,1:T(8,128)(2,1)} %bitcast.174, bf16[4,1,4,256,256]{3,4,2,0,1:T(8,128)(2,1)} %collective-permute-done), kind=kLoop, calls=%fused_computation.37 | loop fusion | flops 12582912 | bytes 25165824 | tf_op jit(solution)/shard_map/concatenate | solution.py:22
  164.6 20.0 %fusion.29 = bf16[16,1,4,256,256]{3,4,2,1,0:T(8,128)(2,1)} fusion(bf16[24,1,4,256,256]{3,4,2,0,1:T(8,128)(2,1)S(1)} %pad_maximum_fusion, s32[]{:T(128)S(6)} %select_n.47, f32[4]{0:T(128)S(1)} %get-tuple-element.136, s32[]{:T(128)S(6)} %select_n.46, f32[4]{0:T(128)S(1)} %get-tuple-element.135, f32[]{:T(128)} %bitcast.51, s32[]{:T(128)S(6)} %select_n.45, ...), kind=kLoop, calls=%fused_computation.38 | loop fusion | flops 121634816 | bytes 75563184 | tf_op jit(solution)/shard_map/convert_element_type | solution.py:87
  184.6 4.7 all-to-all-start.1
  191.2 142.2 %all-gather.2.cloned.1.call-done = bf16[16,256,256]{2,1,0:T(8,128)(2,1)} async-done(((bf16[1,256,256]{2,1,0:T(8,128)(2,1)}), bf16[16,256,256]{2,1,0:T(8,128)(2,1)}) %all-gather.2.cloned.1.call-update) | async-done | bytes 2097168 | tf_op jit(solution)/shard_map/all_gather | solution.py:89
  333.4 6.0 %all-to-all-done.1 = bf16[16,1,4,256,256]{3,4,2,1,0:T(8,128)(2,1)} async-done(((bf16[16,1,4,256,256]{3,4,2,1,0:T(8,128)(2,1)}), bf16[16,1,4,256,256]{3,4,2,1,0:T(8,128)(2,1)}, u32[]{:S(2)}, u32[]{:S(2)}) %all-to-all-start.1) | async-done | bytes 8388640 | tf_op jit(solution)/shard_map/all_to_all | solution.py:88
  339.3 92.7 %while.15 = (s32[]{:T(128)}, bf16[1,4,256,256]{3,2,1,0:T(8,128)(2,1)S(1)}, bf16[1,16,4,256,256]{4,3,2,1,0:T(8,128)(2,1)}, bf16[1,16,4,256,256]{3,4,2,1,0:T(8,128...) while((s32[]{:T(128)}, ...), condition=%wide.region_1.2_spmd, body=%wide.region_0.1_spmd.sunk | while | flops 807665664 | bytes 13895261 | solution.py:103
  357.7 1.7 fusion.67
  363.5 1.7 fusion.67
  369.3 1.7 fusion.67
  380.9 1.7 fusion.67
  386.7 1.7 fusion.67
  392.5 1.7 fusion.67
  398.3 1.7 fusion.67
  409.8 1.7 fusion.67
  415.6 1.7 fusion.67
  432.0 112.4 %all_to_all.40 = bf16[1,16,4,256,256]{4,3,2,0,1:T(8,128)(2,1)} all-to-all(bf16[1,16,4,256,256]{4,3,2,0,1:T(8,128)(2,1)} %bitcast.176), channel_id=1, replica_groups=mesh['energy'=8,'layer'=16] {'layer'}, dimensions={1} | all-to-all | bytes 16777216 | tf_op jit(solution)/shard_map/all_to_all | solution.py:106
  544.4 7.8 %copy.49 = bf16[16,1,4,256,256]{4,3,2,1,0:T(8,128)(2,1)} copy(bf16[16,1,4,256,256]{4,3,2,1,0:T(8,128)(2,1)} %bitcast.175) | data formatting | bytes 16777216
  (220 shorter events, 82.8 us)
Async XLA Ops:
  18.8 114.2 %copy-start.2 = (s32[4]{0:T(128)S(1)}, s32[4]{0:T(128)}, u32[]{:S(2)}) copy-start(s32[4]{0:T(128)} %param.11) | copy-start | bytes 52
  18.8 128.8 %copy-start.3 = (f32[4]{0:T(128)S(1)}, f32[4]{0:T(128)}, u32[]{:S(2)}) copy-start(f32[4]{0:T(128)} %param.12) | copy-start | bytes 52
  123.1 4.0 copy-start
  128.6 25.8 %collective-permute-start.1 = (bf16[4,1,4,256,256]{3,4,2,0,1:T(8,128)(2,1)}, bf16[4,1,4,256,256]{3,4,2,0,1:T(8,128)(2,1)S(1)}, u32[]{:S(2)}, u32[]{:S(2)}) collective-permute-start(bf16[4,1,4,256,256]{3,4,2,0,1:T(8,128)(2,1)} %slice_bitcast_fusion.10), channel_id=1, source_target_pairs={{16,0},{32,16},{48,32},{64,48},{80,64},{96,80},{112,96},{17,1},{33... | collective-permute-start | bytes 6291464 | tf_op jit(solution)/shard_map/ppermute | solution.py:21
  130.6 27.7 %collective-permute-start = (bf16[4,1,4,256,256]{3,4,2,0,1:T(8,128)(2,1)}, bf16[4,1,4,256,256]{3,4,2,0,1:T(8,128)(2,1)}, u32[]{:S(2)}, u32[]{:S(2)}) collective-permute-start(bf16[4,1,4,256,256]{3,4,2,0,1:T(8,128)(2,1)} %slice_bitcast_fusion.11), channel_id=1, source_target_pairs={{0,16},{16,32},{32,48},{48,64},{64,80},{80,96},{96,112},{1,17},{17... | collective-permute-start | bytes 6291464 | tf_op jit(solution)/shard_map/ppermute | solution.py:18
  154.4 3.8 copy-start.1
  184.6 154.7 %all-to-all-start.1 = ((bf16[16,1,4,256,256]{3,4,2,1,0:T(8,128)(2,1)}), bf16[16,1,4,256,256]{3,4,2,1,0:T(8,128)(2,1)}, u32[]{:S(2)}, u32[]{:S(2)}) async-start(bf16[16,1,4,256,256]{3,4,2,1,0:T(8,128)(2,1)} %fusion.29), calls=%async_computation.1 | async-start | bytes 16777216 | tf_op jit(solution)/shard_map/all_to_all | solution.py:88
  189.4 144.0 %all-gather.2.cloned.1.call-start = ((), (), s32[]{:S(2)}) async-start(), calls=%async_computation.3 | async-start | bytes 2228224 | tf_op jit(solution)/shard_map/all_gather | solution.py:89
Sparse Core Ops, SparseCore 0:
  192.3 140.9 all-gather.1
where the time goes:
time: 561 us; the launch traced here: 559 us
  blocking collectives  217 us (39%)
  waiting for transfers between devices  159 us (28%)
  matrix products  61.4 us (11%)
  local copies, waits for them, and re-layouts  57.3 us (10%)
  other arithmetic  27.6 us (5%)
  between operations  27 us (5%)
  starting transfers between devices  9.1 us (2%)
    all_gather x1, waiting for transfers between devices, body(): couplings = lax.all_gather(coupling, 'layer', axis=0, tiled=True)  142 us
    all_to_all x1, blocking collectives, body(): lax.all_to_all(finished, 'layer', split_axis=1, concat_axis=0, tiled=True)  112 us
    all_to_all x1, blocking collectives, body(): lax.all_to_all(correlations, 'layer', split_axis=1, concat_axis=0, tiled=...  104 us
    dot_general x16, matrix products, advance(): jnp.einsum('ab,...kbc->...kac', coupling_block, halfway, preferred_elemen...  27.3 us
    unnamed x10, local copies, waits for them, and re-layouts  22.5 us
    convert_element_type x1, other arithmetic, body(): sigma_blocks = jnp.where(live_mask, accumulated, 0.0).astype(jnp.bfloat16)  20 us
    dot_general x64, matrix products, right_product(): jnp.einsum('...kab,...cb->...kac', stacked_block, matrix, preferred_eleme...  17.5 us
    dot_general x64, matrix products, left_product(): jnp.einsum('...ab,...kbc->...kac', matrix, stacked_block, preferred_eleme...  16.5 us
  transfers between devices with their start and end apart: 4, of which 4 were waited for; matrix products, arithmetic and copies ran while one was open for 1% of the time, Pallas kernels for 0%

commit v1 on v0

v1 whole, which is shorter than its diff:
```python
import functools

import jax
import jax.numpy as jnp
from jax import lax
from jax.experimental import pallas as pl
from jax.experimental.pallas import tpu as pltpu
from jax.sharding import PartitionSpec as P

SHIFT_MAX = 4
BOSE_RATIO = 0.5
ROWS = 64


def tap_weights(phonon_shifts, phonon_coupling):
    occupation = 1.0 / (jnp.exp(BOSE_RATIO * phonon_shifts.astype(jnp.float32)) - 1.0)
    distance = jnp.arange(1, SHIFT_MAX + 1, dtype=jnp.int32)
    hit = (phonon_shifts[None, :] == distance[:, None]).astype(jnp.float32)
    absorbed = jnp.sum(hit * (phonon_coupling * occupation)[None, :], axis=1)
    emitted = jnp.sum(hit * (phonon_coupling * (occupation + 1.0))[None, :], axis=1)
    lesser = jnp.concatenate([absorbed[::-1], emitted])
    greater = jnp.concatenate([emitted[::-1], absorbed])
    return jnp.stack([lesser, greater])


def sigma_kernel(pair, weights, live, low, here, high, out):
    energies = here.shape[0]
    rows, columns = here.shape[2], here.shape[3]
    taps = [weights[pair, k] for k in range(2 * SHIFT_MAX)]
    offsets = [k - SHIFT_MAX if k < SHIFT_MAX else k - SHIFT_MAX + 1 for k in range(2 * SHIFT_MAX)]
    first_row = pl.program_id(1) * rows
    step = 16

    def block(position, carry):
        start = pl.multiple_of(position * step, step)
        row = lax.broadcasted_iota(jnp.int32, (step, columns), 0) + (first_row + start)
        column = lax.broadcasted_iota(jnp.int32, (step, columns), 1)
        mask = (row < live[0]) & (column < live[0])

        def load(energy):
            if energy < 0:
                ref, index = low, energy + SHIFT_MAX
            elif energy >= energies:
                ref, index = high, energy - energies
            else:
                ref, index = here, energy
            return ref[index, 0, pl.ds(start, step), :].astype(jnp.float32)

        for energy in range(energies):
            total = taps[0] * load(energy + offsets[0])
            for tap, offset in zip(taps[1:], offsets[1:]):
                total = total + tap * load(energy + offset)
            out[energy, 0, pl.ds(start, step), :] = jnp.where(mask, total, 0.0).astype(jnp.bfloat16)
        return carry

    lax.fori_loop(0, rows // step, block, 0)


def self_energy(pair, weights, live, low, here, high):
    energies, parts, orbitals, _ = here.shape
    halo = pl.BlockSpec((SHIFT_MAX, 1, ROWS, orbitals), lambda c, r: (0, c, r, 0))
    full = pl.BlockSpec((energies, 1, ROWS, orbitals), lambda c, r: (0, c, r, 0))
    scalar = pl.BlockSpec(memory_space=pltpu.SMEM)
    return pl.pallas_call(
        functools.partial(sigma_kernel, pair),
        grid=(parts, orbitals // ROWS),
        in_specs=[scalar, scalar, halo, full, halo],
        out_specs=full,
        out_shape=jax.ShapeDtypeStruct(here.shape, jnp.bfloat16),
        cost_estimate=pl.CostEstimate(
            flops=16 * here.size, bytes_accessed=5 * here.size, transcendentals=0
        ),
        name=f"self_energy_{pair}",
    )(weights, live, low, here, high)


def dot(left, right):
    return jnp.dot(left, right, preferred_element_type=jnp.float32)


def dot_transposed(left, right):
    return lax.dot_general(
        left, right, (((1,), (1,)), ((), ())), preferred_element_type=jnp.float32
    )


def sweep_kernel(lead, sigma, green, coupling, out, held):
    orbitals = green.shape[-1]

    @pl.when(pl.program_id(0) == 0)
    def _():
        held[...] = lead[0].reshape(2 * orbitals, orbitals)

    v = coupling[...].reshape(orbitals, orbitals)
    halfway = dot_transposed(held[...], v).astype(jnp.bfloat16)
    g_real, g_imag = green[0, 0], green[0, 1]
    source_real = (sigma[0, 0].astype(jnp.float32) + dot(v, halfway[:orbitals])).astype(jnp.bfloat16)
    source_imag = (sigma[0, 1].astype(jnp.float32) + dot(v, halfway[orbitals:])).astype(jnp.bfloat16)
    inner_real = (dot(g_real, source_real) - dot(g_imag, source_imag)).astype(jnp.bfloat16)
    inner_imag = (dot(g_real, source_imag) + dot(g_imag, source_real)).astype(jnp.bfloat16)
    outer_real = (dot_transposed(inner_real, g_real) + dot_transposed(inner_imag, g_imag)).astype(jnp.bfloat16)
    outer_imag = (dot_transposed(inner_imag, g_real) - dot_transposed(inner_real, g_imag)).astype(jnp.bfloat16)
    held[:orbitals] = outer_real
    held[orbitals:] = outer_imag
    out[0, 0] = outer_real
    out[0, 1] = outer_imag


def sweep(pair, correlations, sigma, green, coupling):
    layers, _, orbitals, _ = sigma.shape
    parts = coupling.shape[0]
    block = pl.BlockSpec((1, 2, orbitals, orbitals), lambda i: (i, 0, 0, 0))
    return pl.pallas_call(
        sweep_kernel,
        grid=(layers,),
        in_specs=[
            pl.BlockSpec((1, 2, orbitals, orbitals), lambda i: (0, pair, 0, 0)),
            block,
            block,
            pl.BlockSpec((parts, 1, orbitals // parts, orbitals), lambda i: (0, i, 0, 0)),
        ],
        out_specs=block,
        out_shape=jax.ShapeDtypeStruct(sigma.shape, jnp.bfloat16),
        scratch_shapes=[pltpu.VMEM((2 * orbitals, orbitals), jnp.bfloat16)],
        cost_estimate=pl.CostEstimate(
            flops=24 * layers * orbitals**3,
            bytes_accessed=14 * layers * orbitals**2,
            transcendentals=0,
        ),
        name=f"sweep_{pair}",
    )(correlations, sigma, green, coupling)


def exchange(block, axis):
    return lax.all_to_all(block, axis, split_axis=0, concat_axis=0, tiled=True)


def halo_of(block):
    count = lax.axis_size("energy")
    forward = [(i, i + 1) for i in range(count - 1)]
    backward = [(i + 1, i) for i in range(count - 1)]
    low = lax.ppermute(block[-SHIFT_MAX:], "energy", forward)
    high = lax.ppermute(block[:SHIFT_MAX], "energy", backward)
    return low, high


def all_couplings(coupling):
    layers, groups = lax.axis_size("layer"), lax.axis_size("energy")
    rows = coupling.shape[1] // groups
    piece = lax.dynamic_slice_in_dim(coupling, lax.axis_index("energy") * rows, rows, axis=1)
    pieces = exchange(jnp.broadcast_to(piece, (layers,) + piece.shape[1:]), "layer")
    return exchange(jnp.broadcast_to(pieces[None], (groups,) + pieces.shape), "energy")


def body(correlations, retarded, coupling, phonon_shifts, phonon_coupling, layer_orbitals):
    weights = tap_weights(phonon_shifts, phonon_coupling)
    mine = correlations[0]
    green = retarded[0]
    couplings = all_couplings(coupling)
    arrived = [exchange(mine[:, 2 * p : 2 * p + 2], "layer") for p in range(2)]
    outs = []
    for p in range(2):
        low, high = halo_of(arrived[p])
        sigma = self_energy(p, weights, layer_orbitals, low, arrived[p], high)
        returned = exchange(sigma, "layer")
        finished = sweep(p, mine, returned, green, couplings)
        outs.append(exchange(finished, "layer"))
    return jnp.concatenate(outs, axis=1)[:, None]


def solution(mesh):
    return jax.shard_map(
        body,
        mesh=mesh,
        in_specs=(
            P(("energy", "layer"), None, None, None, None),
            P(("energy", "layer"), None, None, None, None),
            P("layer", None, None),
            P(),
            P(),
            P("layer"),
        ),
        out_specs=P("energy", "layer", None, None, None),
        check_vma=False,
    )
```

time: 561 us -> 397 us (0.71)
  blocking collectives: 217 us -> 125 us
  matrix products: 61.4 us -> 0 us
  Pallas kernels: 0 us -> 58.1 us
  local copies, waits for them, and re-layouts: 57.3 us -> 13.1 us
  between operations: 27 us -> 0.79 us
  starting transfers between devices: 9.1 us -> 35 us
  other arithmetic: 27.6 us -> 8.47 us
  waiting for transfers between devices: 159 us -> 153 us
    all_gather x1 -> x0, waiting for transfers between devices: 142 us -> none  [body(): couplings = lax.all_gather(coupling, 'layer', axis=0, tiled=True)]
    all_to_all x1 -> x5, waiting for transfers between devices: 5.97 us -> 127 us  [exchange(): return lax.all_to_all(block, axis, split_axis=0, concat_axis=0, tiled=True)]
    all_to_all x2 -> x3, blocking collectives: 217 us -> 125 us  [exchange(): return lax.all_to_all(block, axis, split_axis=0, concat_axis=0, tiled=True)]
    dot_general x144 -> x0, matrix products: 61.4 us -> none  [the longest x16 27.3 us: advance(): jnp.einsum('ab,...kbc->...kac', coupling_block, halfway, preferred_elemen...]
    pallas_call x0 -> x4, Pallas kernels: none -> 58.1 us  [the longest x2 39 us: sweep(): pl.pallas_call(sweep_kernel, grid=(layers,), in_specs=[pl.BlockSpec((1, 2...]
    all_to_all x1 -> x5, starting transfers between devices: 4.74 us -> 26.3 us  [exchange(): return lax.all_to_all(block, axis, split_axis=0, concat_axis=0, tiled=True)]
    convert_element_type x17 -> x0, other arithmetic: 20.9 us -> none  [the longest x1 20 us: body(): sigma_blocks = jnp.where(live_mask, accumulated, 0.0).astype(jnp.bfloat16)]
    unnamed x10 -> x16, local copies, waits for them, and re-layouts: 22.5 us -> 1.9 us
  transfers between devices with their start and end apart: 4 -> 9, of which waited for: 4 -> 9; matrix products, arithmetic and copies ran while one was open for 1% -> 3% of each run, Pallas kernels for 0% -> 15%
where the time goes in v1:
time: 397 us; the launch traced here: 393 us
  waiting for transfers between devices  153 us (39%)
  blocking collectives  125 us (31%)
  Pallas kernels  58.1 us (15%)
  starting transfers between devices  35 us (9%)
  local copies, waits for them, and re-layouts  13.1 us (3%)
  other arithmetic  8.47 us (2%)
    all_to_all x5, waiting for transfers between devices, exchange(): return lax.all_to_all(block, axis, split_axis=0, concat_axis=0, tiled=True)  127 us
    all_to_all x3, blocking collectives, exchange(): return lax.all_to_all(block, axis, split_axis=0, concat_axis=0, tiled=True)  125 us
    pallas_call x2, Pallas kernels, sweep(): pl.pallas_call(sweep_kernel, grid=(layers,), in_specs=[pl.BlockSpec((1, 2...  39 us
    all_to_all x5, starting transfers between devices, exchange(): return lax.all_to_all(block, axis, split_axis=0, concat_axis=0, tiled=True)  26.3 us
    pallas_call x2, Pallas kernels, self_energy(): pl.pallas_call(functools.partial(sigma_kernel, pair), grid=(parts, orbita...  19.1 us
    ppermute x2, waiting for transfers between devices, halo_of(): high = lax.ppermute(block[:SHIFT_MAX], 'energy', backward)  18 us
  transfers between devices with their start and end apart: 9, of which 9 were waited for; matrix products, arithmetic and copies ran while one was open for 3% of the time, Pallas kernels for 15%

profile of v1, /device:TPU:8, one launch (start us, length us, event | category | flops | bytes accessed | tf_op | source)
XLA Modules:
  0.0 393.4 jit_solution(8457816083879715361)
XLA Ops:
  0.9 16.2 %all_to_all.40 = bf16[16,32,256]{2,1,0:T(8,128)(2,1)S(1)} all-to-all(bf16[16,32,256]{2,1,0:T(8,128)(2,1)S(1)} %broadcast_in_dim.9), channel_id=1, replica_groups=mesh['energy'=8,'layer'=16] {'layer'}, dimensions={0} | all-to-all | bytes 524288 | tf_op jit(solution)/shard_map/all_to_all | solution.py:135
  18.7 4.9 %all-to-all-start.3 = ((bf16[8,16,32,256]{3,2,1,0:T(8,128)(2,1)}), bf16[8,16,32,256]{3,2,1,0:T(8,128)(2,1)S(1)}, u32[]{:S(2)}, u32[]{:S(2)}) async-start(bf16[8,16,32,256]{3,2,1,0:T(8,128)(2,1)} %broadcast_in_dim.10), calls=%async_computation.3 | async-start | bytes 4194304 | tf_op jit(solution)/shard_map/all_to_all | solution.py:135
  23.7 6.0 %fusion.3 = (bf16[16,2,256,256]{3,2,1,0:T(8,128)(2,1)}, bf16[16,2,256,256]{3,2,1,0:T(8,128)(2,1)}) fusion(bf16[16,4,256,256]{3,2,1,0:T(8,128)(2,1)} %bitcast.12), kind=kLoop, calls=%fused_computation.13 | loop fusion | bytes 16777216 | tf_op jit(solution)/shard_map/slice | solution.py:160
  29.6 19.7 %all-to-all-done.3.coupling = bf16[8,16,32,256]{3,2,1,0:T(8,128)(2,1)S(1)} async-done(((bf16[8,16,32,256]{3,2,1,0:T(8,128)(2,1)}), bf16[8,16,32,256]{3,2,1,0:T(8,128)(2,1)S(1)}, u32[]{:S(2)}, u32[]{:S(2)}) %all-to-all-start.3) | async-done | bytes 2097184 | tf_op jit(solution)/shard_map/all_to_all | solution.py:135
  49.4 55.3 %all_to_all.41.here = bf16[16,2,256,256]{3,2,1,0:T(8,128)(2,1)} all-to-all(bf16[16,2,256,256]{3,2,1,0:T(8,128)(2,1)} %get-tuple-element.10), channel_id=1, replica_groups=mesh['energy'=8,'layer'=16] {'layer'}, dimensions={0} | all-to-all | bytes 8388608 | tf_op jit(solution)/shard_map/all_to_all | solution.py:135
  104.6 4.5 %all-to-all-start = ((bf16[16,2,256,256]{3,2,1,0:T(8,128)(2,1)}), bf16[16,2,256,256]{3,2,1,0:T(8,128)(2,1)}, u32[]{:S(2)}, u32[]{:S(2)}) async-start(bf16[16,2,256,256]{3,2,1,0:T(8,128)(2,1)} %get-tuple-element.9), calls=%async_computation | async-start | bytes 8388608 | tf_op jit(solution)/shard_map/all_to_all | solution.py:135
  112.8 2.4 collective-permute-start.2
  117.0 8.1 %collective-permute-done.3.high = bf16[4,2,256,256]{3,2,1,0:T(8,128)(2,1)S(1)} collective-permute-done((bf16[4,2,256,256]{3,2,1,0:T(8,128)(2,1)S(1)}, bf16[4,2,256,256]{3,2,1,0:T(8,128)(2,1)S(1)}, u32[]{:S(2)}, u32[]{:S(2)}) %collective-permute-start.3) | collective-permute-done | bytes 1048608 | tf_op jit(solution)/shard_map/ppermute | solution.py:143
  125.1 3.9 collective-permute-done.2.low
  129.1 9.5 %self_energy_1.1 = bf16[16,2,256,256]{3,2,1,0:T(8,128)(2,1)} custom-call(f32[2,8]{1,0:T(2,128)} %pad_maximum_fusion.weights, s32[1]{0:T(128)S(6)} %copy.9.live, bf16[4,2,256,256]{3,2,1,0:T(8,128)(2,1)} %collective-permute-done.2.low, bf16[16,2,256,256]{3,2,1,0:T(8,128)(2,1)} %all_to_all.41.here, bf16[4,2,256,256]{3,2,1,0:T(8,128)(2,1)} %copy-done.3), custom_call_target="tpu_custom_call" | custom-call | flops 33554432 | bytes 10485760 | tf_op jit(solution)/shard_map/self_energy_1/pallas_call | solution.py:64
  138.6 24.9 %all-to-all-done.here = bf16[16,2,256,256]{3,2,1,0:T(8,128)(2,1)} async-done(((bf16[16,2,256,256]{3,2,1,0:T(8,128)(2,1)}), bf16[16,2,256,256]{3,2,1,0:T(8,128)(2,1)}, u32[]{:S(2)}, u32[]{:S(2)}) %all-to-all-start) | async-done | bytes 4194336 | tf_op jit(solution)/shard_map/all_to_all | solution.py:135
  163.5 4.6 %all-to-all-start.6 = ((bf16[16,2,256,256]{3,2,1,0:T(8,128)(2,1)}), bf16[16,2,256,256]{3,2,1,0:T(8,128)(2,1)}, u32[]{:S(2)}, u32[]{:S(2)}) async-start(bf16[16,2,256,256]{3,2,1,0:T(8,128)(2,1)} %self_energy_1.1), calls=%async_computation.6 | async-start | bytes 8388608 | tf_op jit(solution)/shard_map/all_to_all | solution.py:135
  174.1 9.9 %collective-permute-done.1.high = bf16[4,2,256,256]{3,2,1,0:T(8,128)(2,1)S(1)} collective-permute-done((bf16[4,2,256,256]{3,2,1,0:T(8,128)(2,1)S(1)}, bf16[4,2,256,256]{3,2,1,0:T(8,128)(2,1)S(1)}, u32[]{:S(2)}, u32[]{:S(2)}) %collective-permute-start.1) | collective-permute-done | bytes 1048608 | tf_op jit(solution)/shard_map/ppermute | solution.py:143
  184.0 3.8 collective-permute-done.low
  188.8 9.6 %self_energy_0.1 = bf16[16,2,256,256]{3,2,1,0:T(8,128)(2,1)} custom-call(f32[2,8]{1,0:T(2,128)} %pad_maximum_fusion.weights, s32[1]{0:T(128)S(6)} %copy.9.live, bf16[4,2,256,256]{3,2,1,0:T(8,128)(2,1)} %copy-done.5, bf16[16,2,256,256]{3,2,1,0:T(8,128)(2,1)} %all-to-all-done.here, bf16[4,2,256,256]{3,2,1,0:T(8,128)(2,1)} %copy-done.4), custom_call_target="tpu_custom_call" | custom-call | flops 33554432 | bytes 10485760 | tf_op jit(solution)/shard_map/self_energy_0/pallas_call | solution.py:64
  198.4 19.3 %all-to-all-done.6.sigma = bf16[16,2,256,256]{3,2,1,0:T(8,128)(2,1)} async-done(((bf16[16,2,256,256]{3,2,1,0:T(8,128)(2,1)}), bf16[16,2,256,256]{3,2,1,0:T(8,128)(2,1)}, u32[]{:S(2)}, u32[]{:S(2)}) %all-to-all-start.6) | async-done | bytes 4194336 | tf_op jit(solution)/shard_map/all_to_all | solution.py:135
  217.7 7.1 %all-to-all-start.1 = ((bf16[16,2,256,256]{3,2,1,0:T(8,128)(2,1)}), bf16[16,2,256,256]{3,2,1,0:T(8,128)(2,1)}, u32[]{:S(2)}, u32[]{:S(2)}) async-start(bf16[16,2,256,256]{3,2,1,0:T(8,128)(2,1)} %self_energy_0.1), calls=%async_computation.1 | async-start | bytes 8388608 | tf_op jit(solution)/shard_map/all_to_all | solution.py:135
  224.8 19.5 %sweep_1.1 = bf16[16,2,256,256]{3,2,1,0:T(8,128)(2,1)} custom-call(bf16[16,4,256,256]{3,2,1,0:T(8,128)(2,1)} %bitcast.13, bf16[16,2,256,256]{3,2,1,0:T(8,128)(2,1)} %all-to-all-done.6.sigma, bf16[16,2,256,256]{3,2,1,0:T(8,128)(2,1)} %bitcast.15, bf16[8,16,32,256]{3,2,1,0:T(8,128)(2,1)} %copy-done.2), custom_call_target="tpu_custom_call" | custom-call | flops 6442450944 | bytes 14680064 | tf_op jit(solution)/shard_map/sweep_1/pallas_call | solution.py:113
  244.3 31.9 %all-to-all-done.1.sigma = bf16[16,2,256,256]{3,2,1,0:T(8,128)(2,1)} async-done(((bf16[16,2,256,256]{3,2,1,0:T(8,128)(2,1)}), bf16[16,2,256,256]{3,2,1,0:T(8,128)(2,1)}, u32[]{:S(2)}, u32[]{:S(2)}) %all-to-all-start.1) | async-done | bytes 4194336 | tf_op jit(solution)/shard_map/all_to_all | solution.py:135
  276.2 5.2 %all-to-all-start.7 = ((bf16[16,2,256,256]{3,2,1,0:T(8,128)(2,1)}), bf16[16,2,256,256]{3,2,1,0:T(8,128)(2,1)}, u32[]{:S(2)}, u32[]{:S(2)}) async-start(bf16[16,2,256,256]{3,2,1,0:T(8,128)(2,1)} %sweep_1.1), calls=%async_computation.7 | async-start | bytes 8388608 | tf_op jit(solution)/shard_map/all_to_all | solution.py:135
  281.4 19.5 %sweep_0.1 = bf16[16,2,256,256]{3,2,1,0:T(8,128)(2,1)} custom-call(bf16[16,4,256,256]{3,2,1,0:T(8,128)(2,1)} %bitcast.14, bf16[16,2,256,256]{3,2,1,0:T(8,128)(2,1)} %all-to-all-done.1.sigma, bf16[16,2,256,256]{3,2,1,0:T(8,128)(2,1)} %bitcast.16, bf16[8,16,32,256]{3,2,1,0:T(8,128)(2,1)} %copy-done.2), custom_call_target="tpu_custom_call" | custom-call | flops 6442450944 | bytes 14680064 | tf_op jit(solution)/shard_map/sweep_0/pallas_call | solution.py:113
  300.9 31.4 %all-to-all-done.7 = bf16[16,2,256,256]{3,2,1,0:T(8,128)(2,1)} async-done(((bf16[16,2,256,256]{3,2,1,0:T(8,128)(2,1)}), bf16[16,2,256,256]{3,2,1,0:T(8,128)(2,1)}, u32[]{:S(2)}, u32[]{:S(2)}) %all-to-all-start.7) | async-done | bytes 4194336 | tf_op jit(solution)/shard_map/all_to_all | solution.py:135
  332.3 53.5 %all_to_all.42 = bf16[16,2,256,256]{3,2,1,0:T(8,128)(2,1)} all-to-all(bf16[16,2,256,256]{3,2,1,0:T(8,128)(2,1)} %sweep_0.1), channel_id=1, replica_groups=mesh['energy'=8,'layer'=16] {'layer'}, dimensions={0} | all-to-all | bytes 8388608 | tf_op jit(solution)/shard_map/all_to_all | solution.py:135
  385.8 7.6 %maximum_bitcast_fusion = bf16[16,1,4,256,256]{4,3,2,1,0:T(8,128)(2,1)} fusion(bf16[16,2,256,256]{3,2,1,0:T(8,128)(2,1)} %all-to-all-done.7, bf16[16,2,256,256]{3,2,1,0:T(8,128)(2,1)} %all_to_all.42), kind=kLoop, calls=%fused_computation | loop fusion | flops 4194304 | bytes 16777216 | tf_op jit(solution)/shard_map/broadcast_in_dim | solution.py:168
  (32 shorter events, 14.2 us)
Async XLA Ops:
  0.0 0.9 copy-start
  18.7 30.6 %all-to-all-start.3 = ((bf16[8,16,32,256]{3,2,1,0:T(8,128)(2,1)}), bf16[8,16,32,256]{3,2,1,0:T(8,128)(2,1)S(1)}, u32[]{:S(2)}, u32[]{:S(2)}) async-start(bf16[8,16,32,256]{3,2,1,0:T(8,128)(2,1)} %broadcast_in_dim.10), calls=%async_computation.3 | async-start | bytes 4194304 | tf_op jit(solution)/shard_map/all_to_all | solution.py:135
  49.4 55.3 %copy-start.2 = (bf16[8,16,32,256]{3,2,1,0:T(8,128)(2,1)}, bf16[8,16,32,256]{3,2,1,0:T(8,128)(2,1)S(1)}, u32[]{:S(2)}) copy-start(bf16[8,16,32,256]{3,2,1,0:T(8,128)(2,1)S(1)} %all-to-all-done.3.coupling) | copy-start | bytes 6291460
  104.6 58.9 %all-to-all-start = ((bf16[16,2,256,256]{3,2,1,0:T(8,128)(2,1)}), bf16[16,2,256,256]{3,2,1,0:T(8,128)(2,1)}, u32[]{:S(2)}, u32[]{:S(2)}) async-start(bf16[16,2,256,256]{3,2,1,0:T(8,128)(2,1)} %get-tuple-element.9), calls=%async_computation | async-start | bytes 8388608 | tf_op jit(solution)/shard_map/all_to_all | solution.py:135
  109.2 6.7 %copy-start.6 = (s32[4]{0:T(128)S(1)}, s32[4]{0:T(128)}, u32[]{:S(2)}) copy-start(s32[4]{0:T(128)} %param.9) | copy-start | bytes 52
  109.2 6.7 %copy-start.7 = (f32[4]{0:T(128)S(1)}, f32[4]{0:T(128)}, u32[]{:S(2)}) copy-start(f32[4]{0:T(128)} %param.10) | copy-start | bytes 52
  110.9 14.2 %collective-permute-start.3 = (bf16[4,2,256,256]{3,2,1,0:T(8,128)(2,1)S(1)}, bf16[4,2,256,256]{3,2,1,0:T(8,128)(2,1)S(1)}, u32[]{:S(2)}, u32[]{:S(2)}) collective-permute-start(bf16[4,2,256,256]{3,2,1,0:T(8,128)(2,1)S(1)} %get-tuple-element.13), channel_id=1, source_target_pairs={{16,0},{32,16},{48,32},{64,48},{80,64},{96,80},{112,96},{17,1},{33... | collective-permute-start | bytes 3145736 | tf_op jit(solution)/shard_map/ppermute | solution.py:143
  112.8 16.2 %collective-permute-start.2 = (bf16[4,2,256,256]{3,2,1,0:T(8,128)(2,1)S(1)}, bf16[4,2,256,256]{3,2,1,0:T(8,128)(2,1)}, u32[]{:S(2)}, u32[]{:S(2)}) collective-permute-start(bf16[4,2,256,256]{3,2,1,0:T(8,128)(2,1)S(1)} %get-tuple-element.14), channel_id=1, source_target_pairs={{0,16},{16,32},{32,48},{48,64},{64,80},{80,96},{96,112},{1,17},{17... | collective-permute-start | bytes 3145736 | tf_op jit(solution)/shard_map/ppermute | solution.py:142
  125.1 3.9 copy-start.3
  163.5 54.2 %all-to-all-start.6 = ((bf16[16,2,256,256]{3,2,1,0:T(8,128)(2,1)}), bf16[16,2,256,256]{3,2,1,0:T(8,128)(2,1)}, u32[]{:S(2)}, u32[]{:S(2)}) async-start(bf16[16,2,256,256]{3,2,1,0:T(8,128)(2,1)} %self_energy_1.1), calls=%async_computation.6 | async-start | bytes 8388608 | tf_op jit(solution)/shard_map/all_to_all | solution.py:135
  169.8 14.2 %collective-permute-start.1 = (bf16[4,2,256,256]{3,2,1,0:T(8,128)(2,1)S(1)}, bf16[4,2,256,256]{3,2,1,0:T(8,128)(2,1)S(1)}, u32[]{:S(2)}, u32[]{:S(2)}) collective-permute-start(bf16[4,2,256,256]{3,2,1,0:T(8,128)(2,1)S(1)} %get-tuple-element.11), channel_id=1, source_target_pairs={{16,0},{32,16},{48,32},{64,48},{80,64},{96,80},{112,96},{17,1},{33... | collective-permute-start | bytes 3145736 | tf_op jit(solution)/shard_map/ppermute | solution.py:143
  171.7 16.1 %collective-permute-start = (bf16[4,2,256,256]{3,2,1,0:T(8,128)(2,1)S(1)}, bf16[4,2,256,256]{3,2,1,0:T(8,128)(2,1)S(1)}, u32[]{:S(2)}, u32[]{:S(2)}) collective-permute-start(bf16[4,2,256,256]{3,2,1,0:T(8,128)(2,1)S(1)} %get-tuple-element.12), channel_id=1, source_target_pairs={{0,16},{16,32},{32,48},{48,64},{64,80},{80,96},{96,112},{1,17},{17... | collective-permute-start | bytes 3145736 | tf_op jit(solution)/shard_map/ppermute | solution.py:142
  184.0 3.8 copy-start.4
  187.8 1.0 copy-start.5
  217.7 58.5 %all-to-all-start.1 = ((bf16[16,2,256,256]{3,2,1,0:T(8,128)(2,1)}), bf16[16,2,256,256]{3,2,1,0:T(8,128)(2,1)}, u32[]{:S(2)}, u32[]{:S(2)}) async-start(bf16[16,2,256,256]{3,2,1,0:T(8,128)(2,1)} %self_energy_0.1), calls=%async_computation.1 | async-start | bytes 8388608 | tf_op jit(solution)/shard_map/all_to_all | solution.py:135
  276.2 56.1 %all-to-all-start.7 = ((bf16[16,2,256,256]{3,2,1,0:T(8,128)(2,1)}), bf16[16,2,256,256]{3,2,1,0:T(8,128)(2,1)}, u32[]{:S(2)}, u32[]{:S(2)}) async-start(bf16[16,2,256,256]{3,2,1,0:T(8,128)(2,1)} %sweep_1.1), calls=%async_computation.7 | async-start | bytes 8388608 | tf_op jit(solution)/shard_map/all_to_all | solution.py:135
  385.8 7.6 %copy-start.1 = (bf16[1,256,256]{2,1,0:T(8,128)(2,1)S(1)}, bf16[1,256,256]{2,1,0:T(8,128)(2,1)}, u32[]{:S(2)}) copy-start(bf16[1,256,256]{2,1,0:T(8,128)(2,1)} %param.8) | copy-start | bytes 393220

commit v2 on v1

--- a/solution.py
+++ b/solution.py
@@ -10,6 +10,10 @@
 SHIFT_MAX = 4
 BOSE_RATIO = 0.5
 ROWS = 64
+ENERGY_BITS = (2, 4, 1)
+ENERGY_OFFSETS = tuple(
+    sum(bit for place, bit in enumerate(ENERGY_BITS) if k >> place & 1) for k in range(8)
+)
 
 
 def tap_weights(phonon_shifts, phonon_coupling):
@@ -84,14 +88,18 @@
     )
 
 
-def sweep_kernel(lead, sigma, green, coupling, out, held):
+def sweep_kernel(place, lead, sigma, green, coupling, out, held, matrix):
     orbitals = green.shape[-1]
+    rows = coupling.shape[2]
+    for k, offset in enumerate(ENERGY_OFFSETS):
+        group = place[0] ^ offset
+        matrix[pl.ds(pl.multiple_of(group * rows, rows), rows), :] = coupling[k, 0]
 
     @pl.when(pl.program_id(0) == 0)
     def _():
         held[...] = lead[0].reshape(2 * orbitals, orbitals)
 
-    v = coupling[...].reshape(orbitals, orbitals)
+    v = matrix[...]
     halfway = dot_transposed(held[...], v).astype(jnp.bfloat16)
     g_real, g_imag = green[0, 0], green[0, 1]
     source_real = (sigma[0, 0].astype(jnp.float32) + dot(v, halfway[:orbitals])).astype(jnp.bfloat16)
@@ -106,29 +114,75 @@
     out[0, 1] = outer_imag
 
 
-def sweep(pair, correlations, sigma, green, coupling):
+def sweep(pair, place, correlations, sigma, green, coupling):
     layers, _, orbitals, _ = sigma.shape
     parts = coupling.shape[0]
-    block = pl.BlockSpec((1, 2, orbitals, orbitals), lambda i: (i, 0, 0, 0))
+    block = pl.BlockSpec((1, 2, orbitals, orbitals), lambda i, place: (i, 0, 0, 0))
     return pl.pallas_call(
         sweep_kernel,
-        grid=(layers,),
-        in_specs=[
-            pl.BlockSpec((1, 2, orbitals, orbitals), lambda i: (0, pair, 0, 0)),
-            block,
-            block,
-            pl.BlockSpec((parts, 1, orbitals // parts, orbitals), lambda i: (0, i, 0, 0)),
-        ],
-        out_specs=block,
+        grid_spec=pltpu.PrefetchScalarGridSpec(
+            num_scalar_prefetch=1,
+            grid=(layers,),
+            in_specs=[
+                pl.BlockSpec((1, 2, orbitals, orbitals), lambda i, place: (0, pair, 0, 0)),
+                block,
+                block,
+                pl.BlockSpec(
+                    (parts, 1, orbitals // parts, orbitals), lambda i, place: (0, i ^ place[1], 0, 0)
+                ),
+            ],
+            out_specs=block,
+            scratch_shapes=[
+                pltpu.VMEM((2 * orbitals, orbitals), jnp.bfloat16),
+                pltpu.VMEM((orbitals, orbitals), jnp.bfloat16),
+            ],
+        ),
         out_shape=jax.ShapeDtypeStruct(sigma.shape, jnp.bfloat16),
-        scratch_shapes=[pltpu.VMEM((2 * orbitals, orbitals), jnp.bfloat16)],
         cost_estimate=pl.CostEstimate(
             flops=24 * layers * orbitals**3,
             bytes_accessed=14 * layers * orbitals**2,
             transcendentals=0,
         ),
         name=f"sweep_{pair}",
-    )(correlations, sigma, green, coupling)
+    )(place, correlations, sigma, green, coupling)
+
+
+def copy_kernel(source, *rest):
+    rest[-1][...] = source[...]
+
+
+def pick_pair(pair, blocks):
+    layers, parts, orbitals, _ = blocks.shape
+    half = parts // 2
+    group = 2
+    return pl.pallas_call(
+        copy_kernel,
+        grid=(layers // group,),
+        in_specs=[pl.BlockSpec((group, half, orbitals, orbitals), lambda i: (i, pair, 0, 0))],
+        out_specs=pl.BlockSpec((group, half, orbitals, orbitals), lambda i: (i, 0, 0, 0)),
+        out_shape=jax.ShapeDtypeStruct((layers, half, orbitals, orbitals), blocks.dtype),
+        cost_estimate=pl.CostEstimate(flops=0, bytes_accessed=2 * blocks.size, transcendentals=0),
+        name=f"pick_{pair}",
+    )(blocks)
+
+
+def place_pair(pair, blocks, whole=None):
+    layers, half, orbitals, _ = blocks.shape
+    group = 2
+    shape = (layers, 1, 2 * half, orbitals, orbitals)
+    in_specs = [pl.BlockSpec((group, half, orbitals, orbitals), lambda i: (i, 0, 0, 0))]
+    if whole is not None:
+        in_specs.append(pl.BlockSpec(memory_space=pl.ANY))
+    return pl.pallas_call(
+        lambda source, *rest: rest[-1].__setitem__((slice(None), 0), source[...]),
+        grid=(layers // group,),
+        in_specs=in_specs,
+        out_specs=pl.BlockSpec((group, 1, half, orbitals, orbitals), lambda i: (i, 0, pair, 0, 0)),
+        out_shape=jax.ShapeDtypeStruct(shape, blocks.dtype),
+        input_output_aliases={} if whole is None else {1: 0},
+        cost_estimate=pl.CostEstimate(flops=0, bytes_accessed=4 * blocks.size, transcendentals=0),
+        name=f"place_{pair}",
+    )(*((blocks,) if whole is None else (blocks, whole)))
 
 
 def exchange(block, axis):
@@ -144,28 +198,48 @@
     return low, high
 
 
-def all_couplings(coupling):
+def swapped(block, axis, bit):
+    count = lax.axis_size(axis)
+    return lax.ppermute(block, axis, [(i, i ^ bit) for i in range(count)])
+
+
+def couplings_of_line(coupling):
     layers, groups = lax.axis_size("layer"), lax.axis_size("energy")
     rows = coupling.shape[1] // groups
-    piece = lax.dynamic_slice_in_dim(coupling, lax.axis_index("energy") * rows, rows, axis=1)
-    pieces = exchange(jnp.broadcast_to(piece, (layers,) + piece.shape[1:]), "layer")
-    return exchange(jnp.broadcast_to(pieces[None], (groups,) + pieces.shape), "energy")
+    held = lax.dynamic_slice_in_dim(coupling, lax.axis_index("energy") * rows, rows, axis=1)
+    bit = 1
+    while bit < layers:
+        held = jnp.concatenate([held, swapped(held, "layer", bit)], axis=0)
+        bit *= 2
+    return held[None]
+
+
+def doubled(held, bits):
+    for bit in bits:
+        held = jnp.concatenate([held, swapped(held, "energy", bit)], axis=0)
+    return held
 
 
 def body(correlations, retarded, coupling, phonon_shifts, phonon_coupling, layer_orbitals):
     weights = tap_weights(phonon_shifts, phonon_coupling)
+    place = jnp.stack([lax.axis_index("energy"), lax.axis_index("layer")]).astype(jnp.int32)
     mine = correlations[0]
     green = retarded[0]
-    couplings = all_couplings(coupling)
-    arrived = [exchange(mine[:, 2 * p : 2 * p + 2], "layer") for p in range(2)]
-    outs = []
+    picked, coupling = lax.optimization_barrier((pick_pair(1, mine), coupling))
+    held = doubled(couplings_of_line(coupling), ENERGY_BITS[:1])
+    picked, held = lax.optimization_barrier((picked, held))
+    arrived = [exchange(block, "layer") for block in (pick_pair(0, mine), picked)]
+    couplings = doubled(held, ENERGY_BITS[1:])
+    whole = None
     for p in range(2):
         low, high = halo_of(arrived[p])
         sigma = self_energy(p, weights, layer_orbitals, low, arrived[p], high)
+        if p == 0:
+            sigma, couplings = lax.optimization_barrier((sigma, couplings))
         returned = exchange(sigma, "layer")
-        finished = sweep(p, mine, returned, green, couplings)
-        outs.append(exchange(finished, "layer"))
-    return jnp.concatenate(outs, axis=1)[:, None]
+        finished = sweep(p, place, mine, returned, green, couplings)
+        whole = place_pair(p, exchange(finished, "layer"), whole)
+    return whole
 
 
 def solution(mesh):

time: 397 us -> 388 us (0.977)
  blocking collectives: 125 us -> 0 us
  waiting for transfers between devices: 153 us -> 226 us
  Pallas kernels: 58.1 us -> 85.9 us
  starting transfers between devices: 35 us -> 62.3 us
  local copies, waits for them, and re-layouts: 13.1 us -> 6.34 us
  other arithmetic: 8.47 us -> 4.4 us
    all_to_all x3 -> x0, blocking collectives: 125 us -> none  [exchange(): return lax.all_to_all(block, axis, split_axis=0, concat_axis=0, tiled=True)]
    ppermute x0 -> x7, waiting for transfers between devices: none -> 66.5 us  [swapped(): return lax.ppermute(block, axis, [(i, i ^ bit) for i in range(count)])]
    pallas_call x2 -> x6, Pallas kernels: 39 us -> 66.9 us  [the longest x2 40.6 us: sweep(): pl.pallas_call(sweep_kernel, grid_spec=pltpu.PrefetchScalarGridSpec(num_s...]
    ppermute x0 -> x7, starting transfers between devices: none -> 17.2 us  [swapped(): return lax.ppermute(block, axis, [(i, i ^ bit) for i in range(count)])]
    all_to_all x5 -> x6, starting transfers between devices: 26.3 us -> 36.3 us  [exchange(): return lax.all_to_all(block, axis, split_axis=0, concat_axis=0, tiled=True)]
    all_to_all x5 -> x6, waiting for transfers between devices: 127 us -> 135 us  [exchange(): return lax.all_to_all(block, axis, split_axis=0, concat_axis=0, tiled=True)]
    broadcast_in_dim x1 -> x0, other arithmetic: 7.61 us -> none  [body(): return jnp.concatenate(outs, axis=1)[:, None]]
    slice x1 -> x0, local copies, waits for them, and re-layouts: 5.98 us -> none  [body(): arrived = [exchange(mine[:, 2 * p:2 * p + 2], 'layer') for p in range(2)]]
  transfers between devices with their start and end apart: 9 -> 17, of which waited for: 9 -> 15; matrix products, arithmetic and copies ran while one was open for 3% -> 3% of each run, Pallas kernels for 15% -> 19%
where the time goes in v2:
time: 388 us; the launch traced here: 385 us
  waiting for transfers between devices  226 us (58%)
  Pallas kernels  85.9 us (22%)
  starting transfers between devices  62.3 us (16%)
  local copies, waits for them, and re-layouts  6.34 us (2%)
  other arithmetic  4.4 us (1%)
    all_to_all x6, waiting for transfers between devices, exchange(): return lax.all_to_all(block, axis, split_axis=0, concat_axis=0, tiled=True)  135 us
    ppermute x7, waiting for transfers between devices, swapped(): return lax.ppermute(block, axis, [(i, i ^ bit) for i in range(count)])  66.5 us
    pallas_call x2, Pallas kernels, sweep(): pl.pallas_call(sweep_kernel, grid_spec=pltpu.PrefetchScalarGridSpec(num_s...  40.6 us
    all_to_all x6, starting transfers between devices, exchange(): return lax.all_to_all(block, axis, split_axis=0, concat_axis=0, tiled=True)  36.3 us
    pallas_call x2, Pallas kernels, self_energy(): pl.pallas_call(functools.partial(sigma_kernel, pair), grid=(parts, orbita...  19 us
    ppermute x7, starting transfers between devices, swapped(): return lax.ppermute(block, axis, [(i, i ^ bit) for i in range(count)])  17.2 us
    ppermute x2, waiting for transfers between devices, halo_of(): high = lax.ppermute(block[:SHIFT_MAX], 'energy', backward)  16.7 us
    pallas_call x2, Pallas kernels, pick_pair(): pl.pallas_call(copy_kernel, grid=(layers // group,), in_specs=[pl.BlockSp...  13.2 us
  transfers between devices with their start and end apart: 17, of which 15 were waited for; matrix products, arithmetic and copies ran while one was open for 3% of the time, Pallas kernels for 19%

profile of v2, /device:TPU:8, one launch (start us, length us, event | category | flops | bytes accessed | tf_op | source)
XLA Modules:
  0.0 385.3 jit_solution(7174079244330540659)
XLA Ops:
  0.0 6.6 %pick_0.1 = bf16[16,2,256,256]{3,2,1,0:T(8,128)(2,1)} custom-call(bf16[16,4,256,256]{3,2,1,0:T(8,128)(2,1)} %bitcast.9), custom_call_target="tpu_custom_call" | custom-call | bytes 8388608 | tf_op jit(solution)/shard_map/pick_0/pallas_call | solution.py:158
  6.6 7.9 %all-to-all-start.2 = ((bf16[16,2,256,256]{3,2,1,0:T(8,128)(2,1)}), bf16[16,2,256,256]{3,2,1,0:T(8,128)(2,1)}, u32[]{:S(2)}, u32[]{:S(2)}) async-start(bf16[16,2,256,256]{3,2,1,0:T(8,128)(2,1)} %pick_0.1), calls=%async_computation.2 | async-start | bytes 8388608 | tf_op jit(solution)/shard_map/all_to_all | solution.py:189
  14.5 6.6 %pick_1.1 = bf16[16,2,256,256]{3,2,1,0:T(8,128)(2,1)} custom-call(bf16[16,4,256,256]{3,2,1,0:T(8,128)(2,1)} %bitcast.10), custom_call_target="tpu_custom_call" | custom-call | bytes 8388608 | tf_op jit(solution)/shard_map/pick_1/pallas_call | solution.py:158
  23.7 28.1 %collective-permute-done = bf16[1,32,256]{2,1,0:T(8,128)(2,1)S(1)} collective-permute-done((bf16[1,32,256]{2,1,0:T(8,128)(2,1)S(1)}, bf16[1,32,256]{2,1,0:T(8,128)(2,1)S(1)}, u32[]{:S(2)}, u32[]{:S(2)}) %collective-permute-start) | collective-permute-done | bytes 16416 | tf_op jit(solution)/shard_map/ppermute | solution.py:203
  51.9 19.5 %collective-permute-done.1 = bf16[2,32,256]{2,1,0:T(8,128)(2,1)S(1)} collective-permute-done((bf16[2,32,256]{2,1,0:T(8,128)(2,1)S(1)}, bf16[2,32,256]{2,1,0:T(8,128)(2,1)S(1)}, u32[]{:S(2)}, u32[]{:S(2)}) %collective-permute-start.1) | collective-permute-done | bytes 32800 | tf_op jit(solution)/shard_map/ppermute | solution.py:203
  71.4 6.1 %collective-permute-start.2 = (bf16[4,32,256]{2,1,0:T(8,128)(2,1)S(1)}, bf16[4,32,256]{2,1,0:T(8,128)(2,1)S(1)}, u32[]{:S(2)}, u32[]{:S(2)}) collective-permute-start(bf16[4,32,256]{2,1,0:T(8,128)(2,1)S(1)} %pad_maximum_fusion.4), channel_id=1, source_target_pairs={{0,4},{1,5},{2,6},{3,7},{4,0},{5,1},{6,2},{7,3},{8,12},{9,13},{10,... | collective-permute-start | bytes 196616 | tf_op jit(solution)/shard_map/ppermute | solution.py:203
  79.8 6.2 %collective-permute-start.3 = (bf16[8,32,256]{2,1,0:T(8,128)(2,1)S(1)}, bf16[8,32,256]{2,1,0:T(8,128)(2,1)S(1)}, u32[]{:S(2)}, u32[]{:S(2)}) collective-permute-start(bf16[8,32,256]{2,1,0:T(8,128)(2,1)S(1)} %pad_maximum_fusion.3), channel_id=1, source_target_pairs={{0,8},{1,9},{2,10},{3,11},{4,12},{5,13},{6,14},{7,15},{8,0},{9,1},... | collective-permute-start | bytes 393224 | tf_op jit(solution)/shard_map/ppermute | solution.py:203
  89.5 5.9 %collective-permute-done.4 = bf16[1,16,32,256]{3,2,1,0:T(8,128)(2,1)S(1)} collective-permute-done((bf16[1,16,32,256]{3,2,1,0:T(8,128)(2,1)S(1)}, bf16[1,16,32,256]{3,2,1,0:T(8,128)(2,1)S(1)}, u32[]{:S(2)}, u32[]{:S(2)}) %collective-permute-start.4) | collective-permute-done | bytes 262176 | tf_op jit(solution)/shard_map/ppermute | solution.py:203
  103.5 7.7 %collective-permute-done.9 = bf16[2,16,32,256]{3,2,1,0:T(8,128)(2,1)S(1)} collective-permute-done((bf16[2,16,32,256]{3,2,1,0:T(8,128)(2,1)S(1)}, bf16[2,16,32,256]{3,2,1,0:T(8,128)(2,1)S(1)}, u32[]{:S(2)}, u32[]{:S(2)}) %collective-permute-start.9) | collective-permute-done | bytes 524320 | tf_op jit(solution)/shard_map/ppermute | solution.py:203
  122.4 6.8 %collective-permute-done.8.high = bf16[4,2,256,256]{3,2,1,0:T(8,128)(2,1)} collective-permute-done((bf16[4,2,256,256]{3,2,1,0:T(8,128)(2,1)}, bf16[4,2,256,256]{3,2,1,0:T(8,128)(2,1)}, u32[]{:S(2)}, u32[]{:S(2)}) %collective-permute-start.8) | collective-permute-done | bytes 1048608 | tf_op jit(solution)/shard_map/ppermute | solution.py:197
  132.8 9.5 %self_energy_0.1 = bf16[16,2,256,256]{3,2,1,0:T(8,128)(2,1)} custom-call(f32[2,8]{1,0:T(2,128)} %pad_maximum_fusion.6.weights, s32[1]{0:T(128)S(6)} %copy.13.live, bf16[4,2,256,256]{3,2,1,0:T(8,128)(2,1)} %collective-permute-done.7.low, bf16[16,2,256,256]{3,2,1,0:T(8,128)(2,1)} %all-to-all-done.2.here, bf16[4,2,256,256]{3,2,1,0:T(8,128)(2,1)} %collective-permute-done.8.high), custom_call_target="tpu_custom_call" | custom-call | flops 33554432 | bytes 10485760 | tf_op jit(solution)/shard_map/self_energy_0/pallas_call | solution.py:68
  142.3 6.6 %all-to-all-done.here = bf16[16,2,256,256]{3,2,1,0:T(8,128)(2,1)} async-done(((bf16[16,2,256,256]{3,2,1,0:T(8,128)(2,1)}), bf16[16,2,256,256]{3,2,1,0:T(8,128)(2,1)}, u32[]{:S(2)}, u32[]{:S(2)}) %all-to-all-start) | async-done | bytes 4194336 | tf_op jit(solution)/shard_map/all_to_all | solution.py:189
  148.9 7.3 %all-to-all-start.4 = ((bf16[16,2,256,256]{3,2,1,0:T(8,128)(2,1)}), bf16[16,2,256,256]{3,2,1,0:T(8,128)(2,1)}, u32[]{:S(2)}, u32[]{:S(2)}) async-start(bf16[16,2,256,256]{3,2,1,0:T(8,128)(2,1)} %self_energy_0.1), calls=%async_computation.4 | async-start | bytes 8388608 | tf_op jit(solution)/shard_map/all_to_all | solution.py:189
  162.2 9.9 %collective-permute-done.6.high = bf16[4,2,256,256]{3,2,1,0:T(8,128)(2,1)S(1)} collective-permute-done((bf16[4,2,256,256]{3,2,1,0:T(8,128)(2,1)S(1)}, bf16[4,2,256,256]{3,2,1,0:T(8,128)(2,1)S(1)}, u32[]{:S(2)}, u32[]{:S(2)}) %collective-permute-start.6) | collective-permute-done | bytes 1048608 | tf_op jit(solution)/shard_map/ppermute | solution.py:197
  177.0 9.5 %self_energy_1.1 = bf16[16,2,256,256]{3,2,1,0:T(8,128)(2,1)} custom-call(f32[2,8]{1,0:T(2,128)} %pad_maximum_fusion.6.weights, s32[1]{0:T(128)S(6)} %copy.13.live, bf16[4,2,256,256]{3,2,1,0:T(8,128)(2,1)} %copy-done.1, bf16[16,2,256,256]{3,2,1,0:T(8,128)(2,1)} %all-to-all-done.here, bf16[4,2,256,256]{3,2,1,0:T(8,128)(2,1)} %copy-done), custom_call_target="tpu_custom_call" | custom-call | flops 33554432 | bytes 10485760 | tf_op jit(solution)/shard_map/self_energy_1/pallas_call | solution.py:68
  186.5 24.2 %all-to-all-done.4.sigma = bf16[16,2,256,256]{3,2,1,0:T(8,128)(2,1)} async-done(((bf16[16,2,256,256]{3,2,1,0:T(8,128)(2,1)}), bf16[16,2,256,256]{3,2,1,0:T(8,128)(2,1)}, u32[]{:S(2)}, u32[]{:S(2)}) %all-to-all-start.4) | async-done | bytes 4194336 | tf_op jit(solution)/shard_map/all_to_all | solution.py:189
  215.8 20.3 %sweep_0.1 = bf16[16,2,256,256]{3,2,1,0:T(8,128)(2,1)} custom-call(s32[2]{0:T(128)} %pad_add_fusion.place, bf16[16,4,256,256]{3,2,1,0:T(8,128)(2,1)} %bitcast.11, bf16[16,2,256,256]{3,2,1,0:T(8,128)(2,1)} %all-to-all-done.4.sigma, bf16[16,2,256,256]{3,2,1,0:T(8,128)(2,1)} %bitcast.15, bf16[8,16,32,256]{3,2,1,0:T(8,128)(2,1)} %pad_maximum_fusion.coupling), custom_call_target="tpu_custom_call" | custom-call | flops 6442450944 | bytes 14680064 | tf_op jit(solution)/shard_map/sweep_0/pallas_call | solution.py:121
  236.1 29.0 %all-to-all-done.1.sigma = bf16[16,2,256,256]{3,2,1,0:T(8,128)(2,1)} async-done(((bf16[16,2,256,256]{3,2,1,0:T(8,128)(2,1)}), bf16[16,2,256,256]{3,2,1,0:T(8,128)(2,1)}, u32[]{:S(2)}, u32[]{:S(2)}) %all-to-all-start.1) | async-done | bytes 4194336 | tf_op jit(solution)/shard_map/all_to_all | solution.py:189
  265.1 6.5 %all-to-all-start.5 = ((bf16[16,2,256,256]{3,2,1,0:T(8,128)(2,1)}), bf16[16,2,256,256]{3,2,1,0:T(8,128)(2,1)}, u32[]{:S(2)}, u32[]{:S(2)}) async-start(bf16[16,2,256,256]{3,2,1,0:T(8,128)(2,1)} %sweep_0.1), calls=%async_computation.5 | async-start | bytes 8388608 | tf_op jit(solution)/shard_map/all_to_all | solution.py:189
  271.6 20.3 %sweep_1.1 = bf16[16,2,256,256]{3,2,1,0:T(8,128)(2,1)} custom-call(s32[2]{0:T(128)} %pad_add_fusion.place, bf16[16,4,256,256]{3,2,1,0:T(8,128)(2,1)} %bitcast.12, bf16[16,2,256,256]{3,2,1,0:T(8,128)(2,1)} %all-to-all-done.1.sigma, bf16[16,2,256,256]{3,2,1,0:T(8,128)(2,1)} %bitcast.16, bf16[8,16,32,256]{3,2,1,0:T(8,128)(2,1)} %pad_maximum_fusion.coupling), custom_call_target="tpu_custom_call" | custom-call | flops 6442450944 | bytes 14680064 | tf_op jit(solution)/shard_map/sweep_1/pallas_call | solution.py:121
  291.9 31.8 %all-to-all-done.5.source = bf16[16,2,256,256]{3,2,1,0:T(8,128)(2,1)} async-done(((bf16[16,2,256,256]{3,2,1,0:T(8,128)(2,1)}), bf16[16,2,256,256]{3,2,1,0:T(8,128)(2,1)}, u32[]{:S(2)}, u32[]{:S(2)}) %all-to-all-start.5) | async-done | bytes 4194336 | tf_op jit(solution)/shard_map/all_to_all | solution.py:189
  328.8 6.6 %place_0.1.rest_0_ = bf16[16,1,4,256,256]{4,3,2,1,0:T(8,128)(2,1)} custom-call(bf16[16,2,256,256]{3,2,1,0:T(8,128)(2,1)} %all-to-all-done.5.source), custom_call_target="tpu_custom_call" | custom-call | bytes 8388608 | tf_op jit(solution)/shard_map/place_0/pallas_call | solution.py:176
  335.4 43.3 %all-to-all-done.3.source = bf16[16,2,256,256]{3,2,1,0:T(8,128)(2,1)} async-done(((bf16[16,2,256,256]{3,2,1,0:T(8,128)(2,1)}), bf16[16,2,256,256]{3,2,1,0:T(8,128)(2,1)}, u32[]{:S(2)}, u32[]{:S(2)}) %all-to-all-start.3) | async-done | bytes 4194336 | tf_op jit(solution)/shard_map/all_to_all | solution.py:189
  378.7 6.6 %place_1.1 = bf16[16,1,4,256,256]{4,3,2,1,0:T(8,128)(2,1)} custom-call(bf16[16,2,256,256]{3,2,1,0:T(8,128)(2,1)} %all-to-all-done.3.source, bf16[16,1,4,256,256]{4,3,2,1,0:T(8,128)(2,1)} %place_0.1.rest_0_), custom_call_target="tpu_custom_call", output_to_operand_aliasing={{}: (1, {})} | custom-call | bytes 8388608 | tf_op jit(solution)/shard_map/place_1/pallas_call | solution.py:176
  (48 shorter events, 51.5 us)
Async XLA Ops:
  6.6 88.9 %all-to-all-start.2 = ((bf16[16,2,256,256]{3,2,1,0:T(8,128)(2,1)}), bf16[16,2,256,256]{3,2,1,0:T(8,128)(2,1)}, u32[]{:S(2)}, u32[]{:S(2)}) async-start(bf16[16,2,256,256]{3,2,1,0:T(8,128)(2,1)} %pick_0.1), calls=%async_computation.2 | async-start | bytes 8388608 | tf_op jit(solution)/shard_map/all_to_all | solution.py:189
  21.9 30.0 %collective-permute-start = (bf16[1,32,256]{2,1,0:T(8,128)(2,1)S(1)}, bf16[1,32,256]{2,1,0:T(8,128)(2,1)S(1)}, u32[]{:S(2)}, u32[]{:S(2)}) collective-permute-start(bf16[1,32,256]{2,1,0:T(8,128)(2,1)S(1)} %get-tuple-element.20), channel_id=1, source_target_pairs={{0,1},{1,0},{2,3},{3,2},{4,5},{5,4},{6,7},{7,6},{8,9},{9,8},{10,11... | collective-permute-start | bytes 49160 | tf_op jit(solution)/shard_map/ppermute | solution.py:203
  51.9 19.5 %collective-permute-start.1 = (bf16[2,32,256]{2,1,0:T(8,128)(2,1)S(1)}, bf16[2,32,256]{2,1,0:T(8,128)(2,1)S(1)}, u32[]{:S(2)}, u32[]{:S(2)}) collective-permute-start(bf16[2,32,256]{2,1,0:T(8,128)(2,1)S(1)} %pad_maximum_fusion.5), channel_id=1, source_target_pairs={{0,2},{1,3},{2,0},{3,1},{4,6},{5,7},{6,4},{7,5},{8,10},{9,11},{10,... | collective-permute-start | bytes 98312 | tf_op jit(solution)/shard_map/ppermute | solution.py:203
  71.4 8.4 %collective-permute-start.2 = (bf16[4,32,256]{2,1,0:T(8,128)(2,1)S(1)}, bf16[4,32,256]{2,1,0:T(8,128)(2,1)S(1)}, u32[]{:S(2)}, u32[]{:S(2)}) collective-permute-start(bf16[4,32,256]{2,1,0:T(8,128)(2,1)S(1)} %pad_maximum_fusion.4), channel_id=1, source_target_pairs={{0,4},{1,5},{2,6},{3,7},{4,0},{5,1},{6,2},{7,3},{8,12},{9,13},{10,... | collective-permute-start | bytes 196616 | tf_op jit(solution)/shard_map/ppermute | solution.py:203
  79.8 9.2 %collective-permute-start.3 = (bf16[8,32,256]{2,1,0:T(8,128)(2,1)S(1)}, bf16[8,32,256]{2,1,0:T(8,128)(2,1)S(1)}, u32[]{:S(2)}, u32[]{:S(2)}) collective-permute-start(bf16[8,32,256]{2,1,0:T(8,128)(2,1)S(1)} %pad_maximum_fusion.3), channel_id=1, source_target_pairs={{0,8},{1,9},{2,10},{3,11},{4,12},{5,13},{6,14},{7,15},{8,0},{9,1},... | collective-permute-start | bytes 393224 | tf_op jit(solution)/shard_map/ppermute | solution.py:203
  89.0 6.5 %collective-permute-start.4 = (bf16[1,16,32,256]{3,2,1,0:T(8,128)(2,1)S(1)}, bf16[1,16,32,256]{3,2,1,0:T(8,128)(2,1)S(1)}, u32[]{:S(2)}, u32[]{:S(2)}) collective-permute-start(bf16[1,16,32,256]{3,2,1,0:T(8,128)(2,1)S(1)} %bitcast.13), channel_id=1, source_target_pairs={{0,32},{16,48},{32,0},{48,16},{64,96},{80,112},{96,64},{112,80},{1... | collective-permute-start | bytes 786440 | tf_op jit(solution)/shard_map/ppermute | solution.py:203
  95.5 53.4 %all-to-all-start = ((bf16[16,2,256,256]{3,2,1,0:T(8,128)(2,1)}), bf16[16,2,256,256]{3,2,1,0:T(8,128)(2,1)}, u32[]{:S(2)}, u32[]{:S(2)}) async-start(bf16[16,2,256,256]{3,2,1,0:T(8,128)(2,1)} %pick_1.1), calls=%async_computation | async-start | bytes 8388608 | tf_op jit(solution)/shard_map/all_to_all | solution.py:189
  100.5 18.1 %copy-start.2 = (s32[4]{0:T(128)S(1)}, s32[4]{0:T(128)}, u32[]{:S(2)}) copy-start(s32[4]{0:T(128)} %param.9) | copy-start | bytes 52
  100.5 18.1 %copy-start.3 = (f32[4]{0:T(128)S(1)}, f32[4]{0:T(128)}, u32[]{:S(2)}) copy-start(f32[4]{0:T(128)} %param.10) | copy-start | bytes 52
  100.5 10.8 %collective-permute-start.9 = (bf16[2,16,32,256]{3,2,1,0:T(8,128)(2,1)S(1)}, bf16[2,16,32,256]{3,2,1,0:T(8,128)(2,1)S(1)}, u32[]{:S(2)}, u32[]{:S(2)}) collective-permute-start(bf16[2,16,32,256]{3,2,1,0:T(8,128)(2,1)S(1)} %pad_maximum_fusion.2), channel_id=1, source_target_pairs={{0,64},{16,80},{32,96},{48,112},{64,0},{80,16},{96,32},{112,48},{1... | collective-permute-start | bytes 1572872 | tf_op jit(solution)/shard_map/ppermute | solution.py:203
  111.3 8.3 %collective-permute-start.10 = (bf16[4,16,32,256]{3,2,1,0:T(8,128)(2,1)S(1)}, bf16[4,16,32,256]{3,2,1,0:T(8,128)(2,1)}, u32[]{:S(2)}, u32[]{:S(2)}) collective-permute-start(bf16[4,16,32,256]{3,2,1,0:T(8,128)(2,1)S(1)} %pad_maximum_fusion.1), channel_id=1, source_target_pairs={{0,16},{16,0},{32,48},{48,32},{64,80},{80,64},{96,112},{112,96},{1... | collective-permute-start | bytes 3145736 | tf_op jit(solution)/shard_map/ppermute | solution.py:203
  114.1 15.1 %collective-permute-start.8 = (bf16[4,2,256,256]{3,2,1,0:T(8,128)(2,1)}, bf16[4,2,256,256]{3,2,1,0:T(8,128)(2,1)}, u32[]{:S(2)}, u32[]{:S(2)}) collective-permute-start(bf16[4,2,256,256]{3,2,1,0:T(8,128)(2,1)} %get-tuple-element.23), channel_id=1, source_target_pairs={{16,0},{32,16},{48,32},{64,48},{80,64},{96,80},{112,96},{17,1},{33... | collective-permute-start | bytes 3145736 | tf_op jit(solution)/shard_map/ppermute | solution.py:197
  116.6 16.2 %collective-permute-start.7 = (bf16[4,2,256,256]{3,2,1,0:T(8,128)(2,1)S(1)}, bf16[4,2,256,256]{3,2,1,0:T(8,128)(2,1)}, u32[]{:S(2)}, u32[]{:S(2)}) collective-permute-start(bf16[4,2,256,256]{3,2,1,0:T(8,128)(2,1)S(1)} %get-tuple-element.24), channel_id=1, source_target_pairs={{0,16},{16,32},{32,48},{48,64},{64,80},{80,96},{96,112},{1,17},{17... | collective-permute-start | bytes 3145736 | tf_op jit(solution)/shard_map/ppermute | solution.py:196
  148.9 61.8 %all-to-all-start.4 = ((bf16[16,2,256,256]{3,2,1,0:T(8,128)(2,1)}), bf16[16,2,256,256]{3,2,1,0:T(8,128)(2,1)}, u32[]{:S(2)}, u32[]{:S(2)}) async-start(bf16[16,2,256,256]{3,2,1,0:T(8,128)(2,1)} %self_energy_0.1), calls=%async_computation.4 | async-start | bytes 8388608 | tf_op jit(solution)/shard_map/all_to_all | solution.py:189
  157.9 14.2 %collective-permute-start.6 = (bf16[4,2,256,256]{3,2,1,0:T(8,128)(2,1)S(1)}, bf16[4,2,256,256]{3,2,1,0:T(8,128)(2,1)S(1)}, u32[]{:S(2)}, u32[]{:S(2)}) collective-permute-start(bf16[4,2,256,256]{3,2,1,0:T(8,128)(2,1)S(1)} %get-tuple-element.25), channel_id=1, source_target_pairs={{16,0},{32,16},{48,32},{64,48},{80,64},{96,80},{112,96},{17,1},{33... | collective-permute-start | bytes 3145736 | tf_op jit(solution)/shard_map/ppermute | solution.py:197
  159.8 16.1 %collective-permute-start.5 = (bf16[4,2,256,256]{3,2,1,0:T(8,128)(2,1)S(1)}, bf16[4,2,256,256]{3,2,1,0:T(8,128)(2,1)S(1)}, u32[]{:S(2)}, u32[]{:S(2)}) collective-permute-start(bf16[4,2,256,256]{3,2,1,0:T(8,128)(2,1)S(1)} %get-tuple-element.26), channel_id=1, source_target_pairs={{0,16},{16,32},{32,48},{48,64},{64,80},{80,96},{96,112},{1,17},{17... | collective-permute-start | bytes 3145736 | tf_op jit(solution)/shard_map/ppermute | solution.py:196
  172.1 3.8 copy-start
  176.0 1.0 copy-start.1
  210.7 54.4 %all-to-all-start.1 = ((bf16[16,2,256,256]{3,2,1,0:T(8,128)(2,1)}), bf16[16,2,256,256]{3,2,1,0:T(8,128)(2,1)}, u32[]{:S(2)}, u32[]{:S(2)}) async-start(bf16[16,2,256,256]{3,2,1,0:T(8,128)(2,1)} %self_energy_1.1), calls=%async_computation.1 | async-start | bytes 8388608 | tf_op jit(solution)/shard_map/all_to_all | solution.py:189
  265.1 58.6 %all-to-all-start.5 = ((bf16[16,2,256,256]{3,2,1,0:T(8,128)(2,1)}), bf16[16,2,256,256]{3,2,1,0:T(8,128)(2,1)}, u32[]{:S(2)}, u32[]{:S(2)}) async-start(bf16[16,2,256,256]{3,2,1,0:T(8,128)(2,1)} %sweep_0.1), calls=%async_computation.5 | async-start | bytes 8388608 | tf_op jit(solution)/shard_map/all_to_all | solution.py:189
  323.7 55.0 %all-to-all-start.3 = ((bf16[16,2,256,256]{3,2,1,0:T(8,128)(2,1)}), bf16[16,2,256,256]{3,2,1,0:T(8,128)(2,1)}, u32[]{:S(2)}, u32[]{:S(2)}) async-start(bf16[16,2,256,256]{3,2,1,0:T(8,128)(2,1)} %sweep_1.1), calls=%async_computation.3 | async-start | bytes 8388608 | tf_op jit(solution)/shard_map/all_to_all | solution.py:189

commit v3 on v2

v3 whole, which is shorter than its diff:
```python
import functools
import math

import jax
import jax.numpy as jnp
from jax import lax
from jax.experimental import pallas as pl
from jax.experimental.pallas import tpu as pltpu
from jax.sharding import PartitionSpec as P

SHIFT_MAX = 4
BOSE_RATIO = 0.5
ROWS = 64
ENERGY_BITS = (2, 4, 1)
ENERGY_OFFSETS = tuple(
    sum(bit for place, bit in enumerate(ENERGY_BITS) if k >> place & 1) for k in range(8)
)


def tap_weights(phonon_shifts, phonon_coupling):
    occupation = 1.0 / (jnp.exp(BOSE_RATIO * phonon_shifts.astype(jnp.float32)) - 1.0)
    distance = jnp.arange(1, SHIFT_MAX + 1, dtype=jnp.int32)
    hit = (phonon_shifts[None, :] == distance[:, None]).astype(jnp.float32)
    absorbed = jnp.sum(hit * (phonon_coupling * occupation)[None, :], axis=1)
    emitted = jnp.sum(hit * (phonon_coupling * (occupation + 1.0))[None, :], axis=1)
    lesser = jnp.concatenate([absorbed[::-1], emitted])
    greater = jnp.concatenate([emitted[::-1], absorbed])
    return jnp.stack([lesser, greater])


def sigma_kernel(pair, per_part, weights, live, low, here, high, out):
    energies, rows, columns = here.shape
    taps = [weights[pair, k] for k in range(2 * SHIFT_MAX)]
    offsets = [k - SHIFT_MAX if k < SHIFT_MAX else k - SHIFT_MAX + 1 for k in range(2 * SHIFT_MAX)]
    first_row = lax.rem(pl.program_id(0), per_part) * rows
    step = 16

    def block(position, carry):
        start = pl.multiple_of(position * step, step)
        row = lax.broadcasted_iota(jnp.int32, (step, columns), 0) + (first_row + start)
        column = lax.broadcasted_iota(jnp.int32, (step, columns), 1)
        mask = (row < live[0]) & (column < live[0])

        def load(energy):
            if energy < 0:
                ref, index = low, energy + SHIFT_MAX
            elif energy >= energies:
                ref, index = high, energy - energies
            else:
                ref, index = here, energy
            return ref[index, pl.ds(start, step), :].astype(jnp.float32)

        for energy in range(energies):
            total = taps[0] * load(energy + offsets[0])
            for tap, offset in zip(taps[1:], offsets[1:]):
                total = total + tap * load(energy + offset)
            out[energy, pl.ds(start, step), :] = jnp.where(mask, total, 0.0).astype(jnp.bfloat16)
        return carry

    lax.fori_loop(0, rows // step, block, 0)


def self_energy(pair, weights, live, low, here, high):
    energies, _, orbitals = here.shape
    per_part = orbitals // ROWS
    halo = pl.BlockSpec((SHIFT_MAX, ROWS, orbitals), lambda r: (0, r, 0))
    full = pl.BlockSpec((energies, ROWS, orbitals), lambda r: (0, r, 0))
    scalar = pl.BlockSpec(memory_space=pltpu.SMEM)
    shape = (energies, 2 * orbitals, orbitals)
    size = math.prod(shape)
    return pl.pallas_call(
        functools.partial(sigma_kernel, pair, per_part),
        grid=(2 * per_part,),
        in_specs=[scalar, scalar, halo, full, halo],
        out_specs=full,
        out_shape=jax.ShapeDtypeStruct(shape, jnp.bfloat16),
        cost_estimate=pl.CostEstimate(flops=16 * size, bytes_accessed=5 * size, transcendentals=0),
        name=f"self_energy_{pair}",
    )(weights, live, low, here, high)


def dot(left, right):
    return jnp.dot(left, right, preferred_element_type=jnp.float32)


def dot_transposed(left, right):
    return lax.dot_general(
        left, right, (((1,), (1,)), ((), ())), preferred_element_type=jnp.float32
    )


def sweep_kernel(place, lead, sigma, green, coupling, out, held, matrix):
    orbitals = green.shape[-1]
    rows = coupling.shape[2]
    for k, offset in enumerate(ENERGY_OFFSETS):
        group = place[0] ^ offset
        matrix[pl.ds(pl.multiple_of(group * rows, rows), rows), :] = coupling[k, 0]

    @pl.when(pl.program_id(0) == 0)
    def _():
        held[...] = lead[0]

    v = matrix[...]
    halfway = dot_transposed(held[...], v).astype(jnp.bfloat16)
    g_real, g_imag = green[0, 0], green[0, 1]
    wide = jnp.float32
    source_real = (sigma[0, :orbitals].astype(wide) + dot(v, halfway[:orbitals])).astype(jnp.bfloat16)
    source_imag = (sigma[0, orbitals:].astype(wide) + dot(v, halfway[orbitals:])).astype(jnp.bfloat16)
    inner_real = (dot(g_real, source_real) - dot(g_imag, source_imag)).astype(jnp.bfloat16)
    inner_imag = (dot(g_real, source_imag) + dot(g_imag, source_real)).astype(jnp.bfloat16)
    outer_real = (dot_transposed(inner_real, g_real) + dot_transposed(inner_imag, g_imag)).astype(jnp.bfloat16)
    outer_imag = (dot_transposed(inner_imag, g_real) - dot_transposed(inner_real, g_imag)).astype(jnp.bfloat16)
    held[:orbitals] = outer_real
    held[orbitals:] = outer_imag
    out[0, :orbitals] = outer_real
    out[0, orbitals:] = outer_imag


def sweep(pair, place, flat, sigma, green, coupling):
    layers, both, orbitals = sigma.shape
    parts = coupling.shape[0]
    block = pl.BlockSpec((1, both, orbitals), lambda i, place: (i, 0, 0))
    return pl.pallas_call(
        sweep_kernel,
        grid_spec=pltpu.PrefetchScalarGridSpec(
            num_scalar_prefetch=1,
            grid=(layers,),
            in_specs=[
                pl.BlockSpec((1, both, orbitals), lambda i, place: (0, pair, 0)),
                block,
                pl.BlockSpec((1, 2, orbitals, orbitals), lambda i, place: (i, 0, 0, 0)),
                pl.BlockSpec((parts, 1, orbitals // parts, orbitals), lambda i, place: (0, i, 0, 0)),
            ],
            out_specs=block,
            scratch_shapes=[
                pltpu.VMEM((both, orbitals), jnp.bfloat16),
                pltpu.VMEM((orbitals, orbitals), jnp.bfloat16),
            ],
        ),
        out_shape=jax.ShapeDtypeStruct(sigma.shape, jnp.bfloat16),
        cost_estimate=pl.CostEstimate(
            flops=24 * layers * orbitals**3,
            bytes_accessed=14 * layers * orbitals**2,
            transcendentals=0,
        ),
        name=f"sweep_{pair}",
    )(place, flat, sigma, green, coupling)


def relay(sources, slots, targets, arrived, gone):
    fetches = [
        pltpu.make_async_copy(source, slot, arrived.at[k])
        for k, (source, slot) in enumerate(zip(sources, slots))
    ]
    puts = [
        pltpu.make_async_copy(slot, target, gone.at[k])
        for k, (slot, target) in enumerate(zip(slots, targets))
    ]
    for fetch in fetches:
        fetch.start()
    for fetch, put in zip(fetches, puts):
        fetch.wait()
        put.start()
    for put in puts:
        put.wait()


def relay_scratch(layers, rows, orbitals):
    return [
        pltpu.VMEM((layers, rows, orbitals), jnp.bfloat16),
        pltpu.SemaphoreType.DMA((layers,)),
        pltpu.SemaphoreType.DMA((layers,)),
    ]


def pick_kernel(pair, blocks, out, held, arrived, gone):
    layers, rows = held.shape[:2]
    relay(
        [blocks.at[i, pl.ds(pair * rows, rows)] for i in range(layers)],
        [held.at[i] for i in range(layers)],
        [out.at[i, pl.ds(0, rows)] for i in range(layers)],
        arrived,
        gone,
    )


def pick_with_coupling_kernel(pair, blocks, coupling, out, held, arrived, gone, piece, here, sent):
    layers, rows = held.shape[:2]
    extra = piece.shape[0]
    group = lax.axis_index("energy")
    own = pl.ds(pl.multiple_of(group * extra, extra), extra)
    fetch = pltpu.make_async_copy(coupling.at[0, own], piece, here)
    fetch.start()
    pick_kernel(pair, blocks, out, held, arrived, gone)
    fetch.wait()
    puts = [
        pltpu.make_async_copy(piece, out.at[i, pl.ds(rows, extra)], sent.at[i]) for i in range(layers)
    ]
    for put in puts:
        put.start()
    for put in puts:
        put.wait()


def pick_pair(pair, flat, coupling=None):
    layers, rows, orbitals = flat.shape
    rows //= 2
    extra = 0
    kernel = functools.partial(pick_kernel, pair)
    operands, scratch = [flat], relay_scratch(layers, rows, orbitals)
    if coupling is not None:
        extra = orbitals // lax.axis_size("energy")
        kernel = functools.partial(pick_with_coupling_kernel, pair)
        operands.append(coupling)
        scratch += [
            pltpu.VMEM((extra, orbitals), jnp.bfloat16),
            pltpu.SemaphoreType.DMA(()),
            pltpu.SemaphoreType.DMA((layers,)),
        ]
    return pl.pallas_call(
        kernel,
        in_specs=[pl.BlockSpec(memory_space=pl.ANY)] * len(operands),
        out_specs=pl.BlockSpec(memory_space=pl.ANY),
        out_shape=jax.ShapeDtypeStruct((layers, rows + extra, orbitals), flat.dtype),
        scratch_shapes=scratch,
        cost_estimate=pl.CostEstimate(flops=0, bytes_accessed=2 * flat.size, transcendentals=0),
        name=f"pick_{pair}",
    )(*operands)


def place_kernel(pair, blocks, *rest):
    out, held, arrived, gone = rest[-4:]
    layers, rows = held.shape[:2]
    relay(
        [blocks.at[i] for i in range(layers)],
        [held.at[i] for i in range(layers)],
        [out.at[i, pl.ds(pair * rows, rows)] for i in range(layers)],
        arrived,
        gone,
    )


def place_pair(pair, blocks, whole=None):
    layers, rows, orbitals = blocks.shape
    operands = (blocks,) if whole is None else (blocks, whole)
    return pl.pallas_call(
        functools.partial(place_kernel, pair),
        in_specs=[pl.BlockSpec(memory_space=pl.ANY)] * len(operands),
        out_specs=pl.BlockSpec(memory_space=pl.ANY),
        out_shape=jax.ShapeDtypeStruct((layers, 2 * rows, orbitals), blocks.dtype),
        scratch_shapes=relay_scratch(layers, rows, orbitals),
        input_output_aliases={} if whole is None else {1: 0},
        cost_estimate=pl.CostEstimate(flops=0, bytes_accessed=4 * blocks.size, transcendentals=0),
        name=f"place_{pair}",
    )(*operands)


def exchange(block):
    return lax.all_to_all(block, "layer", split_axis=0, concat_axis=0, tiled=True)


def halo_of(block):
    count = lax.axis_size("energy")
    forward = [(i, i + 1) for i in range(count - 1)]
    backward = [(i + 1, i) for i in range(count - 1)]
    low = lax.ppermute(block[-SHIFT_MAX:], "energy", forward)
    high = lax.ppermute(block[:SHIFT_MAX], "energy", backward)
    return low, high


def all_couplings(held):
    count = lax.axis_size("energy")
    held = held[None]
    for bit in ENERGY_BITS:
        other = lax.ppermute(held, "energy", [(i, i ^ bit) for i in range(count)])
        held = jnp.concatenate([held, other], axis=0)
    return held


def body(correlations, retarded, coupling, phonon_shifts, phonon_coupling, layer_orbitals):
    weights = tap_weights(phonon_shifts, phonon_coupling)
    place = jnp.stack([lax.axis_index("energy"), lax.axis_index("layer")]).astype(jnp.int32)
    layers, parts, orbitals = correlations.shape[1:4]
    flat = correlations.reshape(layers, parts * orbitals, orbitals)
    rows = parts * orbitals // 2
    picked = lax.optimization_barrier([pick_pair(0, flat, coupling), pick_pair(1, flat)])
    arrived = [exchange(block) for block in picked]
    couplings = all_couplings(arrived[0][:, rows:])
    whole = None
    for p in range(2):
        low, high = halo_of(arrived[p][:, :rows])
        sigma = self_energy(p, weights, layer_orbitals, low, arrived[p], high)
        if p == 0:
            sigma, couplings = lax.optimization_barrier((sigma, couplings))
        finished = sweep(p, place, flat, exchange(sigma), retarded[0], couplings)
        whole = place_pair(p, exchange(finished), whole)
    return whole.reshape(layers, 1, parts, orbitals, orbitals)


def solution(mesh):
    return jax.shard_map(
        body,
        mesh=mesh,
        in_specs=(
            P(("energy", "layer"), None, None, None, None),
            P(("energy", "layer"), None, None, None, None),
            P("layer", None, None),
            P(),
            P(),
            P("layer"),
        ),
        out_specs=P("energy", "layer", None, None, None),
        check_vma=False,
    )
```

time: 388 us -> 362 us (0.933)
  blocking collectives: 0 us -> 61.9 us
  waiting for transfers between devices: 226 us -> 169 us
  starting transfers between devices: 62.3 us -> 41.2 us
  Pallas kernels: 85.9 us -> 75.7 us
    all_to_all x0 -> x1, blocking collectives: none -> 61.9 us  [exchange(): lax.all_to_all(block, 'layer', split_axis=0, concat_axis=0, tiled=True)]
    ppermute x7 -> x3, waiting for transfers between devices: 66.5 us -> 8.51 us  [all_couplings(): other = lax.ppermute(held, 'energy', [(i, i ^ bit) for i in range(count)])]
    ppermute x7 -> x3, starting transfers between devices: 17.2 us -> 3.88 us  [all_couplings(): other = lax.ppermute(held, 'energy', [(i, i ^ bit) for i in range(count)])]
    pallas_call x6, Pallas kernels: 45.3 us -> 35.2 us  [the longest x2 19 us: self_energy(): pl.pallas_call(functools.partial(sigma_kernel, pair, per_part), grid=(2 *...]
    all_to_all x6 -> x5, starting transfers between devices: 36.3 us -> 28.6 us  [exchange(): lax.all_to_all(block, 'layer', split_axis=0, concat_axis=0, tiled=True)]
    all_to_all x6 -> x5, waiting for transfers between devices: 135 us -> 137 us  [exchange(): lax.all_to_all(block, 'layer', split_axis=0, concat_axis=0, tiled=True)]
  transfers between devices with their start and end apart: 17 -> 12, of which waited for: 15 -> 11; matrix products, arithmetic and copies ran while one was open for 3% -> 3% of each run, Pallas kernels for 19% -> 18%
where the time goes in v3:
time: 362 us; the launch traced here: 359 us
  waiting for transfers between devices  169 us (47%)
  Pallas kernels  75.7 us (21%)
  blocking collectives  61.9 us (17%)
  starting transfers between devices  41.2 us (11%)
  local copies, waits for them, and re-layouts  6.51 us (2%)
  other arithmetic  4.46 us (1%)
    all_to_all x5, waiting for transfers between devices, exchange(): lax.all_to_all(block, 'layer', split_axis=0, concat_axis=0, tiled=True)  137 us
    all_to_all x1, blocking collectives, exchange(): lax.all_to_all(block, 'layer', split_axis=0, concat_axis=0, tiled=True)  61.9 us
    pallas_call x2, Pallas kernels, sweep(): pl.pallas_call(sweep_kernel, grid_spec=pltpu.PrefetchScalarGridSpec(num_s...  40.5 us
    all_to_all x5, starting transfers between devices, exchange(): lax.all_to_all(block, 'layer', split_axis=0, concat_axis=0, tiled=True)  28.6 us
    pallas_call x2, Pallas kernels, self_energy(): pl.pallas_call(functools.partial(sigma_kernel, pair, per_part), grid=(2 *...  19 us
    ppermute x2, waiting for transfers between devices, halo_of(): high = lax.ppermute(block[:SHIFT_MAX], 'energy', backward)  17.5 us
    pallas_call x2, Pallas kernels, pick_pair(): pl.pallas_call(kernel, in_specs=[pl.BlockSpec(memory_space=pl.ANY)] * len...  8.54 us
    ppermute x3, waiting for transfers between devices, all_couplings(): other = lax.ppermute(held, 'energy', [(i, i ^ bit) for i in range(count)])  8.51 us
  transfers between devices with their start and end apart: 12, of which 11 were waited for; matrix products, arithmetic and copies ran while one was open for 3% of the time, Pallas kernels for 18%

profile of v3, /device:TPU:8, one launch (start us, length us, event | category | flops | bytes accessed | tf_op | source)
XLA Modules:
  0.0 359.5 jit_solution(4818621542262655969)
XLA Ops:
  0.0 3.8 %pick_1.1 = bf16[16,512,256]{2,1,0:T(8,128)(2,1)} custom-call(bf16[16,1024,256]{2,1,0:T(8,128)(2,1)} %bitcast.13), custom_call_target="tpu_custom_call" | custom-call | bytes 8388608 | tf_op jit(solution)/shard_map/pick_1/pallas_call | solution.py:220
  3.9 4.7 %pick_0.1 = bf16[16,544,256]{2,1,0:T(8,128)(2,1)} custom-call(bf16[16,1024,256]{2,1,0:T(8,128)(2,1)} %bitcast.14, bf16[1,256,256]{2,1,0:T(8,128)(2,1)} %coupling.1), custom_call_target="tpu_custom_call" | custom-call | bytes 8388608 | tf_op jit(solution)/shard_map/pick_0/pallas_call | solution.py:220
  8.6 61.9 %all_to_all.30.here = bf16[16,544,256]{2,1,0:T(8,128)(2,1)} all-to-all(bf16[16,544,256]{2,1,0:T(8,128)(2,1)} %pick_0.1), channel_id=1, replica_groups=mesh['energy'=8,'layer'=16] {'layer'}, dimensions={0} | all-to-all | bytes 8912896 | tf_op jit(solution)/shard_map/all_to_all | solution.py:259
  70.4 4.6 %all-to-all-start = ((bf16[16,512,256]{2,1,0:T(8,128)(2,1)}), bf16[16,512,256]{2,1,0:T(8,128)(2,1)}, u32[]{:S(2)}, u32[]{:S(2)}) async-start(bf16[16,512,256]{2,1,0:T(8,128)(2,1)} %pick_1.1), calls=%async_computation | async-start | bytes 8388608 | tf_op jit(solution)/shard_map/all_to_all | solution.py:259
  76.5 5.9 %collective-permute-done.4 = bf16[1,16,32,256]{3,2,1,0:T(8,128)(2,1)S(1)} collective-permute-done((bf16[1,16,32,256]{3,2,1,0:T(8,128)(2,1)S(1)}, bf16[1,16,32,256]{3,2,1,0:T(8,128)(2,1)S(1)}, u32[]{:S(2)}, u32[]{:S(2)}) %collective-permute-start.4) | collective-permute-done | bytes 262176 | tf_op jit(solution)/shard_map/ppermute | solution.py:275
  82.5 3.3 collective-permute-start.5
  97.3 7.6 %collective-permute-done.3.high = bf16[4,512,256]{2,1,0:T(8,128)(2,1)} collective-permute-done((bf16[4,512,256]{2,1,0:T(8,128)(2,1)}, bf16[4,512,256]{2,1,0:T(8,128)(2,1)}, u32[]{:S(2)}, u32[]{:S(2)}) %collective-permute-start.3) | collective-permute-done | bytes 1048608 | tf_op jit(solution)/shard_map/ppermute | solution.py:267
  106.7 9.5 %self_energy_0.1 = bf16[16,512,256]{2,1,0:T(8,128)(2,1)} custom-call(f32[2,8]{1,0:T(2,128)} %pad_maximum_fusion.3.weights, s32[1]{0:T(128)S(6)} %copy.11.live, bf16[4,512,256]{2,1,0:T(8,128)(2,1)} %collective-permute-done.2.low, bf16[16,544,256]{2,1,0:T(8,128)(2,1)} %all_to_all.30.here, bf16[4,512,256]{2,1,0:T(8,128)(2,1)} %collective-permute-done.3.high), custom_call_target="tpu_custom_call" | custom-call | flops 33554432 | bytes 10485760 | tf_op jit(solution)/shard_map/self_energy_0/pallas_call | solution.py:71
  119.0 10.2 %all-to-all-done.here = bf16[16,512,256]{2,1,0:T(8,128)(2,1)} async-done(((bf16[16,512,256]{2,1,0:T(8,128)(2,1)}), bf16[16,512,256]{2,1,0:T(8,128)(2,1)}, u32[]{:S(2)}, u32[]{:S(2)}) %all-to-all-start) | async-done | bytes 4194336 | tf_op jit(solution)/shard_map/all_to_all | solution.py:259
  129.2 4.5 %all-to-all-start.4 = ((bf16[16,512,256]{2,1,0:T(8,128)(2,1)}), bf16[16,512,256]{2,1,0:T(8,128)(2,1)}, u32[]{:S(2)}, u32[]{:S(2)}) async-start(bf16[16,512,256]{2,1,0:T(8,128)(2,1)} %self_energy_0.1), calls=%async_computation.4 | async-start | bytes 8388608 | tf_op jit(solution)/shard_map/all_to_all | solution.py:259
  139.8 9.9 %collective-permute-done.1.high = bf16[4,512,256]{2,1,0:T(8,128)(2,1)S(1)} collective-permute-done((bf16[4,512,256]{2,1,0:T(8,128)(2,1)S(1)}, bf16[4,512,256]{2,1,0:T(8,128)(2,1)S(1)}, u32[]{:S(2)}, u32[]{:S(2)}) %collective-permute-start.1) | collective-permute-done | bytes 1048608 | tf_op jit(solution)/shard_map/ppermute | solution.py:267
  149.7 3.8 %collective-permute-done.low = bf16[4,512,256]{2,1,0:T(8,128)(2,1)S(1)} collective-permute-done((bf16[4,512,256]{2,1,0:T(8,128)(2,1)S(1)}, bf16[4,512,256]{2,1,0:T(8,128)(2,1)S(1)}, u32[]{:S(2)}, u32[]{:S(2)}) %collective-permute-start) | collective-permute-done | bytes 1048608 | tf_op jit(solution)/shard_map/ppermute | solution.py:266
  154.5 9.5 %self_energy_1.1 = bf16[16,512,256]{2,1,0:T(8,128)(2,1)} custom-call(f32[2,8]{1,0:T(2,128)} %pad_maximum_fusion.3.weights, s32[1]{0:T(128)S(6)} %copy.11.live, bf16[4,512,256]{2,1,0:T(8,128)(2,1)} %copy-done.1, bf16[16,512,256]{2,1,0:T(8,128)(2,1)} %all-to-all-done.here, bf16[4,512,256]{2,1,0:T(8,128)(2,1)} %copy-done), custom_call_target="tpu_custom_call" | custom-call | flops 33554432 | bytes 10485760 | tf_op jit(solution)/shard_map/self_energy_1/pallas_call | solution.py:71
  164.0 18.8 %all-to-all-done.4.sigma = bf16[16,512,256]{2,1,0:T(8,128)(2,1)} async-done(((bf16[16,512,256]{2,1,0:T(8,128)(2,1)}), bf16[16,512,256]{2,1,0:T(8,128)(2,1)}, u32[]{:S(2)}, u32[]{:S(2)}) %all-to-all-start.4) | async-done | bytes 4194336 | tf_op jit(solution)/shard_map/all_to_all | solution.py:259
  182.7 7.5 %all-to-all-start.1 = ((bf16[16,512,256]{2,1,0:T(8,128)(2,1)}), bf16[16,512,256]{2,1,0:T(8,128)(2,1)}, u32[]{:S(2)}, u32[]{:S(2)}) async-start(bf16[16,512,256]{2,1,0:T(8,128)(2,1)} %self_energy_1.1), calls=%async_computation.1 | async-start | bytes 8388608 | tf_op jit(solution)/shard_map/all_to_all | solution.py:259
  190.9 20.2 %sweep_0.1 = bf16[16,512,256]{2,1,0:T(8,128)(2,1)} custom-call(s32[2]{0:T(128)} %pad_add_fusion.place, bf16[16,1024,256]{2,1,0:T(8,128)(2,1)} %bitcast.15, bf16[16,512,256]{2,1,0:T(8,128)(2,1)} %all-to-all-done.4.sigma, bf16[16,2,256,256]{3,2,1,0:T(8,128)(2,1)} %bitcast.17, bf16[8,16,32,256]{3,2,1,0:T(8,128)(2,1)} %pad_maximum_fusion.coupling), custom_call_target="tpu_custom_call" | custom-call | flops 6442450944 | bytes 14680064 | tf_op jit(solution)/shard_map/sweep_0/pallas_call | solution.py:123
  211.1 31.0 %all-to-all-done.1.sigma = bf16[16,512,256]{2,1,0:T(8,128)(2,1)} async-done(((bf16[16,512,256]{2,1,0:T(8,128)(2,1)}), bf16[16,512,256]{2,1,0:T(8,128)(2,1)}, u32[]{:S(2)}, u32[]{:S(2)}) %all-to-all-start.1) | async-done | bytes 4194336 | tf_op jit(solution)/shard_map/all_to_all | solution.py:259
  242.1 5.2 %all-to-all-start.5 = ((bf16[16,512,256]{2,1,0:T(8,128)(2,1)}), bf16[16,512,256]{2,1,0:T(8,128)(2,1)}, u32[]{:S(2)}, u32[]{:S(2)}) async-start(bf16[16,512,256]{2,1,0:T(8,128)(2,1)} %sweep_0.1), calls=%async_computation.5 | async-start | bytes 8388608 | tf_op jit(solution)/shard_map/all_to_all | solution.py:259
  247.3 20.3 %sweep_1.1 = bf16[16,512,256]{2,1,0:T(8,128)(2,1)} custom-call(s32[2]{0:T(128)} %pad_add_fusion.place, bf16[16,1024,256]{2,1,0:T(8,128)(2,1)} %bitcast.16, bf16[16,512,256]{2,1,0:T(8,128)(2,1)} %all-to-all-done.1.sigma, bf16[16,2,256,256]{3,2,1,0:T(8,128)(2,1)} %bitcast.18, bf16[8,16,32,256]{3,2,1,0:T(8,128)(2,1)} %pad_maximum_fusion.coupling), custom_call_target="tpu_custom_call" | custom-call | flops 6442450944 | bytes 14680064 | tf_op jit(solution)/shard_map/sweep_1/pallas_call | solution.py:123
  267.6 29.6 %all-to-all-done.5.blocks = bf16[16,512,256]{2,1,0:T(8,128)(2,1)} async-done(((bf16[16,512,256]{2,1,0:T(8,128)(2,1)}), bf16[16,512,256]{2,1,0:T(8,128)(2,1)}, u32[]{:S(2)}, u32[]{:S(2)}) %all-to-all-start.5) | async-done | bytes 4194336 | tf_op jit(solution)/shard_map/all_to_all | solution.py:259
  297.1 6.9 %all-to-all-start.3 = ((bf16[16,512,256]{2,1,0:T(8,128)(2,1)}), bf16[16,512,256]{2,1,0:T(8,128)(2,1)}, u32[]{:S(2)}, u32[]{:S(2)}) async-start(bf16[16,512,256]{2,1,0:T(8,128)(2,1)} %sweep_1.1), calls=%async_computation.3 | async-start | bytes 8388608 | tf_op jit(solution)/shard_map/all_to_all | solution.py:259
  304.0 3.9 %place_0.1.rest_0_ = bf16[16,1024,256]{2,1,0:T(8,128)(2,1)} custom-call(bf16[16,512,256]{2,1,0:T(8,128)(2,1)} %all-to-all-done.5.blocks), custom_call_target="tpu_custom_call" | custom-call | bytes 8388608 | tf_op jit(solution)/shard_map/place_0/pallas_call | solution.py:246
  307.9 47.8 %all-to-all-done.3.blocks = bf16[16,512,256]{2,1,0:T(8,128)(2,1)} async-done(((bf16[16,512,256]{2,1,0:T(8,128)(2,1)}), bf16[16,512,256]{2,1,0:T(8,128)(2,1)}, u32[]{:S(2)}, u32[]{:S(2)}) %all-to-all-start.3) | async-done | bytes 4194336 | tf_op jit(solution)/shard_map/all_to_all | solution.py:259
  355.6 3.8 %place_1.1 = bf16[16,1024,256]{2,1,0:T(8,128)(2,1)} custom-call(bf16[16,512,256]{2,1,0:T(8,128)(2,1)} %all-to-all-done.3.blocks, bf16[16,1024,256]{2,1,0:T(8,128)(2,1)} %place_0.1.rest_0_), custom_call_target="tpu_custom_call", output_to_operand_aliasing={{}: (1, {})} | custom-call | bytes 8388608 | tf_op jit(solution)/shard_map/place_1/pallas_call | solution.py:246
  (32 shorter events, 24.6 us)
Async XLA Ops:
  70.4 58.8 %all-to-all-start = ((bf16[16,512,256]{2,1,0:T(8,128)(2,1)}), bf16[16,512,256]{2,1,0:T(8,128)(2,1)}, u32[]{:S(2)}, u32[]{:S(2)}) async-start(bf16[16,512,256]{2,1,0:T(8,128)(2,1)} %pick_1.1), calls=%async_computation | async-start | bytes 8388608 | tf_op jit(solution)/shard_map/all_to_all | solution.py:259
  75.0 21.2 %copy-start.2 = (s32[4]{0:T(128)S(1)}, s32[4]{0:T(128)}, u32[]{:S(2)}) copy-start(s32[4]{0:T(128)} %param.9) | copy-start | bytes 52
  75.0 21.2 %copy-start.3 = (f32[4]{0:T(128)S(1)}, f32[4]{0:T(128)}, u32[]{:S(2)}) copy-start(f32[4]{0:T(128)} %param.10) | copy-start | bytes 52
  76.0 6.5 %collective-permute-start.4 = (bf16[1,16,32,256]{3,2,1,0:T(8,128)(2,1)S(1)}, bf16[1,16,32,256]{3,2,1,0:T(8,128)(2,1)S(1)}, u32[]{:S(2)}, u32[]{:S(2)}) collective-permute-start(bf16[1,16,32,256]{3,2,1,0:T(8,128)(2,1)S(1)} %slice_bitcast_fusion), channel_id=1, source_target_pairs={{0,32},{16,48},{32,0},{48,16},{64,96},{80,112},{96,64},{112,80},{1... | collective-permute-start | bytes 786440 | tf_op jit(solution)/shard_map/ppermute | solution.py:275
  82.5 12.8 %collective-permute-start.5 = (bf16[2,16,32,256]{3,2,1,0:T(8,128)(2,1)S(1)}, bf16[2,16,32,256]{3,2,1,0:T(8,128)(2,1)S(1)}, u32[]{:S(2)}, u32[]{:S(2)}) collective-permute-start(bf16[2,16,32,256]{3,2,1,0:T(8,128)(2,1)S(1)} %pad_maximum_fusion.2), channel_id=1, source_target_pairs={{0,64},{16,80},{32,96},{48,112},{64,0},{80,16},{96,32},{112,48},{1... | collective-permute-start | bytes 1572872 | tf_op jit(solution)/shard_map/ppermute | solution.py:275
  88.4 16.5 %collective-permute-start.3 = (bf16[4,512,256]{2,1,0:T(8,128)(2,1)}, bf16[4,512,256]{2,1,0:T(8,128)(2,1)}, u32[]{:S(2)}, u32[]{:S(2)}) collective-permute-start(bf16[4,512,256]{2,1,0:T(8,128)(2,1)} %get-tuple-element.17), channel_id=1, source_target_pairs={{16,0},{32,16},{48,32},{64,48},{80,64},{96,80},{112,96},{17,1},{33... | collective-permute-start | bytes 3145736 | tf_op jit(solution)/shard_map/ppermute | solution.py:267
  90.4 16.4 %collective-permute-start.2 = (bf16[4,512,256]{2,1,0:T(8,128)(2,1)S(1)}, bf16[4,512,256]{2,1,0:T(8,128)(2,1)}, u32[]{:S(2)}, u32[]{:S(2)}) collective-permute-start(bf16[4,512,256]{2,1,0:T(8,128)(2,1)S(1)} %get-tuple-element.18), channel_id=1, source_target_pairs={{0,16},{16,32},{32,48},{48,64},{64,80},{80,96},{96,112},{1,17},{17... | collective-permute-start | bytes 3145736 | tf_op jit(solution)/shard_map/ppermute | solution.py:266
  95.5 20.8 %collective-permute-start.6 = (bf16[4,16,32,256]{3,2,1,0:T(8,128)(2,1)S(1)}, bf16[4,16,32,256]{3,2,1,0:T(8,128)(2,1)}, u32[]{:S(2)}, u32[]{:S(2)}) collective-permute-start(bf16[4,16,32,256]{3,2,1,0:T(8,128)(2,1)S(1)} %pad_maximum_fusion.1), channel_id=1, source_target_pairs={{0,16},{16,0},{32,48},{48,32},{64,80},{80,64},{96,112},{112,96},{1... | collective-permute-start | bytes 3145736 | tf_op jit(solution)/shard_map/ppermute | solution.py:275
  129.2 53.5 %all-to-all-start.4 = ((bf16[16,512,256]{2,1,0:T(8,128)(2,1)}), bf16[16,512,256]{2,1,0:T(8,128)(2,1)}, u32[]{:S(2)}, u32[]{:S(2)}) async-start(bf16[16,512,256]{2,1,0:T(8,128)(2,1)} %self_energy_0.1), calls=%async_computation.4 | async-start | bytes 8388608 | tf_op jit(solution)/shard_map/all_to_all | solution.py:259
  135.4 14.2 %collective-permute-start.1 = (bf16[4,512,256]{2,1,0:T(8,128)(2,1)S(1)}, bf16[4,512,256]{2,1,0:T(8,128)(2,1)S(1)}, u32[]{:S(2)}, u32[]{:S(2)}) collective-permute-start(bf16[4,512,256]{2,1,0:T(8,128)(2,1)S(1)} %get-tuple-element.19), channel_id=1, source_target_pairs={{16,0},{32,16},{48,32},{64,48},{80,64},{96,80},{112,96},{17,1},{33... | collective-permute-start | bytes 3145736 | tf_op jit(solution)/shard_map/ppermute | solution.py:267
  137.4 16.1 %collective-permute-start = (bf16[4,512,256]{2,1,0:T(8,128)(2,1)S(1)}, bf16[4,512,256]{2,1,0:T(8,128)(2,1)S(1)}, u32[]{:S(2)}, u32[]{:S(2)}) collective-permute-start(bf16[4,512,256]{2,1,0:T(8,128)(2,1)S(1)} %get-tuple-element.20), channel_id=1, source_target_pairs={{0,16},{16,32},{32,48},{48,64},{64,80},{80,96},{96,112},{1,17},{17... | collective-permute-start | bytes 3145736 | tf_op jit(solution)/shard_map/ppermute | solution.py:266
  149.7 3.8 %copy-start = (bf16[4,512,256]{2,1,0:T(8,128)(2,1)}, bf16[4,512,256]{2,1,0:T(8,128)(2,1)S(1)}, u32[]{:S(2)}) copy-start(bf16[4,512,256]{2,1,0:T(8,128)(2,1)S(1)} %collective-permute-done.1.high) | copy-start | bytes 3145732
  153.5 1.0 copy-start.1
  182.7 59.4 %all-to-all-start.1 = ((bf16[16,512,256]{2,1,0:T(8,128)(2,1)}), bf16[16,512,256]{2,1,0:T(8,128)(2,1)}, u32[]{:S(2)}, u32[]{:S(2)}) async-start(bf16[16,512,256]{2,1,0:T(8,128)(2,1)} %self_energy_1.1), calls=%async_computation.1 | async-start | bytes 8388608 | tf_op jit(solution)/shard_map/all_to_all | solution.py:259
  242.1 55.0 %all-to-all-start.5 = ((bf16[16,512,256]{2,1,0:T(8,128)(2,1)}), bf16[16,512,256]{2,1,0:T(8,128)(2,1)}, u32[]{:S(2)}, u32[]{:S(2)}) async-start(bf16[16,512,256]{2,1,0:T(8,128)(2,1)} %sweep_0.1), calls=%async_computation.5 | async-start | bytes 8388608 | tf_op jit(solution)/shard_map/all_to_all | solution.py:259
  297.1 58.5 %all-to-all-start.3 = ((bf16[16,512,256]{2,1,0:T(8,128)(2,1)}), bf16[16,512,256]{2,1,0:T(8,128)(2,1)}, u32[]{:S(2)}, u32[]{:S(2)}) async-start(bf16[16,512,256]{2,1,0:T(8,128)(2,1)} %sweep_1.1), calls=%async_computation.3 | async-start | bytes 8388608 | tf_op jit(solution)/shard_map/all_to_all | solution.py:259

commit v4 on v1

v4 whole, which is shorter than its diff:
```python
import functools
import math

import jax
import jax.numpy as jnp
from jax import lax
from jax.experimental import pallas as pl
from jax.experimental.pallas import tpu as pltpu
from jax.sharding import PartitionSpec as P

SHIFT_MAX = 4
BOSE_RATIO = 0.5
FIRST_LAYERS = 10
LIVE_ROWS = 16
ENERGY_BITS = (2, 4, 1)
ENERGY_OFFSETS = tuple(
    sum(bit for place, bit in enumerate(ENERGY_BITS) if k >> place & 1) for k in range(8)
)


def tap_weights(phonon_shifts, phonon_coupling):
    occupation = 1.0 / (jnp.exp(BOSE_RATIO * phonon_shifts.astype(jnp.float32)) - 1.0)
    distance = jnp.arange(1, SHIFT_MAX + 1, dtype=jnp.int32)
    hit = (phonon_shifts[None, :] == distance[:, None]).astype(jnp.float32)
    absorbed = jnp.sum(hit * (phonon_coupling * occupation)[None, :], axis=1)
    emitted = jnp.sum(hit * (phonon_coupling * (occupation + 1.0))[None, :], axis=1)
    lesser = jnp.concatenate([absorbed[::-1], emitted])
    greater = jnp.concatenate([emitted[::-1], absorbed])
    return jnp.stack([lesser, greater])


def sigma_kernel(weights, low, here, high, out):
    energies, rows, columns = here.shape
    taps = [weights[k] for k in range(2 * SHIFT_MAX)]
    offsets = [k - SHIFT_MAX if k < SHIFT_MAX else k - SHIFT_MAX + 1 for k in range(2 * SHIFT_MAX)]
    step, width = 16, 128
    refs = [(low, e) for e in range(SHIFT_MAX)]
    refs += [(here, e) for e in range(energies)]
    refs += [(high, e) for e in range(SHIFT_MAX)]

    def block(position, carry):
        tile = pl.ds(pl.multiple_of(position * step, step), step)
        for left in range(0, columns, width):
            lanes = pl.ds(left, width)
            loaded = [ref[e, tile, lanes].astype(jnp.float32) for ref, e in refs]
            for energy in range(energies):
                terms = [
                    tap * loaded[energy + SHIFT_MAX + offset] for tap, offset in zip(taps, offsets)
                ]
                while len(terms) > 1:
                    terms = [x + y for x, y in zip(terms[0::2], terms[1::2])]
                out[energy, tile, lanes] = terms[0].astype(jnp.bfloat16)
        return carry

    lax.fori_loop(0, rows // step, block, 0)


def self_energy(name, weights, low, here, high, rows, share):
    energies, _, orbitals = here.shape
    halo = pl.BlockSpec((SHIFT_MAX, share, orbitals), lambda r: (0, r, 0))
    full = pl.BlockSpec((energies, share, orbitals), lambda r: (0, r, 0))
    size = energies * rows * orbitals
    return pl.pallas_call(
        sigma_kernel,
        grid=(rows // share,),
        in_specs=[pl.BlockSpec(memory_space=pltpu.SMEM), halo, full, halo],
        out_specs=full,
        out_shape=jax.ShapeDtypeStruct((energies, rows, orbitals), jnp.bfloat16),
        cost_estimate=pl.CostEstimate(flops=16 * size, bytes_accessed=5 * size, transcendentals=0),
        name=f"self_energy_{name}",
    )(weights, low, here, high)


def dot(left, right):
    return jnp.dot(left, right, preferred_element_type=jnp.float32)


def dot_transposed(left, right):
    return lax.dot_general(
        left, right, (((1,), (1,)), ((), ())), preferred_element_type=jnp.float32
    )


def sweep_kernel(first, group, live, lead, sigma, green, coupling, *rest):
    out, last, held, matrix = rest[-4:]
    narrow = jnp.bfloat16
    orbitals = green.shape[-1]
    rows = coupling.shape[2]
    layer = pl.program_id(0)
    for k, offset in enumerate(ENERGY_OFFSETS):
        start = pl.multiple_of((group[0] ^ offset) * rows, rows)
        matrix[pl.ds(start, rows), :] = coupling[k, 0]

    @pl.when(layer == 0)
    def _():
        held[...] = lead[0]

    row = lax.broadcasted_iota(jnp.int32, (orbitals, orbitals), 0)
    column = lax.broadcasted_iota(jnp.int32, (orbitals, orbitals), 1)
    mask = jnp.maximum(row, column) < live[first + layer]

    v = matrix[...]
    halfway = dot_transposed(held[...], v).astype(narrow)
    own = sigma[...].reshape(4 * orbitals, orbitals)
    source = []
    for k in range(4):
        part = slice(k * orbitals, (k + 1) * orbitals)
        spread = dot(v, halfway[part])
        source.append((jnp.where(mask, own[part].astype(jnp.float32), 0.0) + spread).astype(narrow))
    g_real, g_imag = green[0, 0], green[0, 1]
    g_minus = jnp.concatenate([g_real, -g_imag], axis=1)
    g_plus = jnp.concatenate([g_real, g_imag], axis=1)
    stacked = []
    for k in (0, 2):
        inner_real = dot(g_minus, jnp.concatenate([source[k], source[k + 1]], axis=0)).astype(narrow)
        inner_imag = dot(g_plus, jnp.concatenate([source[k + 1], source[k]], axis=0)).astype(narrow)
        stacked.append(jnp.concatenate([inner_real, inner_imag], axis=1))
        stacked.append(jnp.concatenate([inner_imag, -inner_real], axis=1))
    outer = dot_transposed(jnp.concatenate(stacked, axis=0), g_plus).astype(narrow)
    held[...] = outer
    out[0] = outer
    last[0] = outer


def sweep(first, group, live, lead, sigma, retarded, couplings, whole=None):
    layers, _, orbitals, _ = retarded.shape
    sources, rows, _ = sigma.shape
    share = 4 * orbitals // sources
    count = rows // share
    parts = couplings.shape[0]
    state = pl.BlockSpec((1, 4 * orbitals, orbitals), lambda i, group, live: (0, 0, 0))
    in_specs = [
        state,
        pl.BlockSpec((sources, share, orbitals), lambda i, group, live: (0, i, 0)),
        pl.BlockSpec((1, 2, orbitals, orbitals), lambda i, group, live: (first + i, 0, 0, 0)),
        pl.BlockSpec((parts, 1, orbitals // parts, orbitals), lambda i, group, live: (0, first + i, 0, 0)),
    ]
    operands = [group, live, lead, sigma, retarded, couplings]
    if whole is not None:
        in_specs.append(pl.BlockSpec(memory_space=pl.ANY))
        operands.append(whole)
    return pl.pallas_call(
        functools.partial(sweep_kernel, first),
        grid_spec=pltpu.PrefetchScalarGridSpec(
            num_scalar_prefetch=2,
            grid=(count,),
            in_specs=in_specs,
            out_specs=[
                pl.BlockSpec((1, 4 * orbitals, orbitals), lambda i, group, live: (first + i, 0, 0)),
                state,
            ],
            scratch_shapes=[
                pltpu.VMEM((4 * orbitals, orbitals), jnp.bfloat16),
                pltpu.VMEM((orbitals, orbitals), jnp.bfloat16),
            ],
        ),
        out_shape=[
            jax.ShapeDtypeStruct((layers, 4 * orbitals, orbitals), jnp.bfloat16),
            jax.ShapeDtypeStruct((1, 4 * orbitals, orbitals), jnp.bfloat16),
        ],
        input_output_aliases={} if whole is None else {6: 0},
        cost_estimate=pl.CostEstimate(
            flops=48 * count * orbitals**3,
            bytes_accessed=28 * count * orbitals**2,
            transcendentals=0,
        ),
        name=f"sweep_{first}",
    )(*operands)


def pick_kernel(blocks, coupling, live, first, second, arrived, here, sent):
    layers, devices, share, _ = blocks.shape
    split = first.shape[1] // share
    rows = coupling.shape[1] // lax.axis_size("energy")
    start = pl.multiple_of(lax.axis_index("energy") * rows, rows)
    tail = (layers - split) * share
    copies = []
    for i in range(layers):
        target = first if i < split else second
        where = pl.ds((i if i < split else i - split) * share, share)
        copies.append(pltpu.make_async_copy(blocks.at[i], target.at[:, where], arrived.at[i]))
    for d in range(devices):
        mine = coupling.at[0, pl.ds(start, rows)]
        copies.append(pltpu.make_async_copy(mine, second.at[d, pl.ds(tail, rows)], here.at[d]))
        target = second.at[d, pl.ds(tail + rows, LIVE_ROWS)]
        copies.append(pltpu.make_async_copy(live, target, sent.at[d]))
    for copy in copies:
        copy.start()
    for copy in copies:
        copy.wait()


def pick(blocks, coupling, live_rows):
    layers, devices, share, orbitals = blocks.shape
    rows = orbitals // lax.axis_size("energy")
    extra = rows + LIVE_ROWS
    shapes = (FIRST_LAYERS * share, (layers - FIRST_LAYERS) * share + extra)
    return pl.pallas_call(
        pick_kernel,
        in_specs=[pl.BlockSpec(memory_space=pltpu.HBM)] * 3,
        out_specs=[pl.BlockSpec(memory_space=pltpu.VMEM)] * 2,
        out_shape=[pltpu.VMEM((devices, n, orbitals), blocks.dtype) for n in shapes],
        scratch_shapes=[pltpu.SemaphoreType.DMA((n,)) for n in (layers, devices, devices)],
        cost_estimate=pl.CostEstimate(flops=0, bytes_accessed=2 * blocks.size, transcendentals=0),
        compiler_params=pltpu.CompilerParams(vmem_limit_bytes=16 << 20),
        name="pick",
    )(blocks, coupling, live_rows)


def settle_kernel(source, out, gone):
    copies = [
        pltpu.make_async_copy(source.at[i], out.at[i], gone.at[i]) for i in range(source.shape[0])
    ]
    for copy in copies:
        copy.start()
    for copy in copies:
        copy.wait()


def settle(blocks):
    return pl.pallas_call(
        settle_kernel,
        in_specs=[pl.BlockSpec(memory_space=pltpu.VMEM)],
        out_specs=pl.BlockSpec(memory_space=pl.ANY),
        out_shape=jax.ShapeDtypeStruct(blocks.shape, blocks.dtype),
        scratch_shapes=[pltpu.SemaphoreType.DMA((blocks.shape[0],))],
        cost_estimate=pl.CostEstimate(flops=0, bytes_accessed=2 * blocks.size, transcendentals=0),
        compiler_params=pltpu.CompilerParams(vmem_limit_bytes=16 << 20),
        name="settle",
    )(blocks)


def exchange(block):
    return lax.all_to_all(block, "layer", split_axis=0, concat_axis=0, tiled=True)


def exchange_into(block, space):
    return pltpu.with_memory_space_constraint(exchange(block), space)


def halo_of(block):
    count = lax.axis_size("energy")
    forward = [(i, i + 1) for i in range(count - 1)]
    backward = [(i + 1, i) for i in range(count - 1)]
    low = lax.ppermute(block[-SHIFT_MAX:], "energy", forward)
    high = lax.ppermute(block[:SHIFT_MAX], "energy", backward)
    return low, high


def all_couplings(held):
    count = lax.axis_size("energy")
    held = held[None]
    for bit in ENERGY_BITS:
        other = lax.ppermute(held, "energy", [(i, i ^ bit) for i in range(count)])
        held = jnp.concatenate([held, other], axis=0)
    return held


def body(correlations, retarded, coupling, phonon_shifts, phonon_coupling, layer_orbitals):
    layers, parts, orbitals = correlations.shape[1:4]
    devices = lax.axis_size("layer")
    share = parts * orbitals // devices
    pair = lax.axis_index("layer") * 2 // devices
    weights = lax.dynamic_index_in_dim(tap_weights(phonon_shifts, phonon_coupling), pair, 0, keepdims=False)
    group = lax.axis_index("energy").astype(jnp.int32)[None]
    live_rows = jnp.broadcast_to(layer_orbitals.astype(jnp.bfloat16)[:, None], (LIVE_ROWS, orbitals))
    picked = pick(correlations.reshape(layers, devices, share, orbitals), coupling, live_rows)
    arrived = [exchange(block) for block in picked]
    rows = (FIRST_LAYERS * share, (layers - FIRST_LAYERS) * share)
    extra = arrived[1][:, rows[1] :]
    group_rows = extra.shape[1] - LIVE_ROWS
    couplings = all_couplings(extra[:, :group_rows])
    live = extra[:, group_rows, 0].astype(jnp.int32)
    sigmas = []
    for c in range(2):
        low, high = halo_of(arrived[c][:, : rows[c]])
        sigmas.append(self_energy(c, weights, low, arrived[c], high, rows[c], share))
    sigmas[1], couplings, live = lax.optimization_barrier((sigmas[1], couplings, live))
    lead = correlations.reshape(layers, parts * orbitals, orbitals)
    returned = [exchange_into(sigma, pltpu.HBM) for sigma in sigmas]
    whole, lead = sweep(0, group, live, lead, returned[0], retarded[0], couplings)
    whole, _ = sweep(FIRST_LAYERS, group, live, lead, returned[1], retarded[0], couplings, whole)
    return settle(exchange_into(whole, pltpu.VMEM)).reshape(layers, 1, parts, orbitals, orbitals)


def solution(mesh):
    return jax.shard_map(
        body,
        mesh=mesh,
        in_specs=(
            P(("energy", "layer"), None, None, None, None),
            P(("energy", "layer"), None, None, None, None),
            P("layer", None, None),
            P(),
            P(),
            P("layer"),
        ),
        out_specs=P("energy", "layer", None, None, None),
        check_vma=False,
    )
```

time: 397 us -> 359 us (0.904)
  waiting for transfers between devices: 153 us -> 88 us
  blocking collectives: 125 us -> 171 us
  starting transfers between devices: 35 us -> 28.6 us
  Pallas kernels: 58.1 us -> 51.8 us
    all_to_all x5 -> x3, waiting for transfers between devices: 127 us -> 48.4 us  [exchange(): lax.all_to_all(block, 'layer', split_axis=0, concat_axis=0, tiled=True)]
    all_to_all x3 -> x2, blocking collectives: 125 us -> 171 us  [exchange(): lax.all_to_all(block, 'layer', split_axis=0, concat_axis=0, tiled=True)]
    ppermute x0 -> x3, waiting for transfers between devices: none -> 14.2 us  [all_couplings(): other = lax.ppermute(held, 'energy', [(i, i ^ bit) for i in range(count)])]
    all_to_all x5 -> x3, starting transfers between devices: 26.3 us -> 14.8 us  [exchange(): lax.all_to_all(block, 'layer', split_axis=0, concat_axis=0, tiled=True)]
    broadcast_in_dim x1 -> x0, other arithmetic: 7.61 us -> none  [body(): return jnp.concatenate(outs, axis=1)[:, None]]
    pallas_call x4 -> x6, Pallas kernels: 58.1 us -> 51.8 us  [the longest x2 26.5 us: sweep(): pl.pallas_call(functools.partial(sweep_kernel, first), grid_spec=pltpu.Pr...]
    slice x1 -> x0, local copies, waits for them, and re-layouts: 5.98 us -> none  [body(): arrived = [exchange(mine[:, 2 * p:2 * p + 2], 'layer') for p in range(2)]]
    unnamed x16 -> x26, local copies, waits for them, and re-layouts: 1.9 us -> 6.86 us
  transfers between devices with their start and end apart: 9 -> 10, of which waited for: 9 -> 9; matrix products, arithmetic and copies ran while one was open for 3% -> 3% of each run, Pallas kernels for 15% -> 10%
where the time goes in v4:
time: 359 us; the launch traced here: 357 us
  blocking collectives  171 us (48%)
  waiting for transfers between devices  88 us (25%)
  Pallas kernels  51.8 us (14%)
  starting transfers between devices  28.6 us (8%)
  local copies, waits for them, and re-layouts  11.1 us (3%)
  other arithmetic  5.22 us (1%)
    all_to_all x2, blocking collectives, exchange(): lax.all_to_all(block, 'layer', split_axis=0, concat_axis=0, tiled=True)  171 us
    all_to_all x3, waiting for transfers between devices, exchange(): lax.all_to_all(block, 'layer', split_axis=0, concat_axis=0, tiled=True)  48.4 us
    pallas_call x2, Pallas kernels, sweep(): pl.pallas_call(functools.partial(sweep_kernel, first), grid_spec=pltpu.Pr...  26.5 us
    ppermute x2, waiting for transfers between devices, halo_of(): high = lax.ppermute(block[:SHIFT_MAX], 'energy', backward)  18.5 us
    pallas_call x2, Pallas kernels, self_energy(): pl.pallas_call(sigma_kernel, grid=(rows // share,), in_specs=[pl.BlockSpe...  18.5 us
    all_to_all x3, starting transfers between devices, exchange(): lax.all_to_all(block, 'layer', split_axis=0, concat_axis=0, tiled=True)  14.8 us
    ppermute x3, waiting for transfers between devices, all_couplings(): other = lax.ppermute(held, 'energy', [(i, i ^ bit) for i in range(count)])  14.2 us
  transfers between devices with their start and end apart: 10, of which 9 were waited for; matrix products, arithmetic and copies ran while one was open for 3% of the time, Pallas kernels for 10%

profile of v4, /device:TPU:8, one launch (start us, length us, event | category | flops | bytes accessed | tf_op | source)
XLA Modules:
  0.0 357.0 jit_solution(13247261867251580948)
XLA Ops:
  0.7 3.4 copy-done
  5.0 3.4 pick.1
  8.4 69.9 %all_to_all.25.here = bf16[16,640,256]{2,1,0:T(8,128)(2,1)} all-to-all(bf16[16,640,256]{2,1,0:T(8,128)(2,1)S(1)} %get-tuple-element.15), channel_id=1, replica_groups=mesh['energy'=8,'layer'=16] {'layer'}, dimensions={0} | all-to-all | bytes 10485760 | tf_op jit(solution)/shard_map/all_to_all | solution.py:234
  78.3 4.2 %all-to-all-start = ((bf16[16,432,256]{2,1,0:T(8,128)(2,1)}), bf16[16,432,256]{2,1,0:T(8,128)(2,1)S(1)}, u32[]{:S(2)}, u32[]{:S(2)}) async-start(bf16[16,432,256]{2,1,0:T(8,128)(2,1)} %get-tuple-element.13), calls=%async_computation | async-start | bytes 7077888 | tf_op jit(solution)/shard_map/all_to_all | solution.py:234
  82.5 3.4 fusion.4
  91.3 12.0 %collective-permute-done.6.high = bf16[4,640,256]{2,1,0:T(8,128)(2,1)} collective-permute-done((bf16[4,640,256]{2,1,0:T(8,128)(2,1)}, bf16[4,640,256]{2,1,0:T(8,128)(2,1)}, u32[]{:S(2)}, u32[]{:S(2)}) %collective-permute-start.6) | collective-permute-done | bytes 1310752 | tf_op jit(solution)/shard_map/ppermute | solution.py:246
  103.3 3.8 %collective-permute-done.5.low = bf16[4,640,256]{2,1,0:T(8,128)(2,1)} collective-permute-done((bf16[4,640,256]{2,1,0:T(8,128)(2,1)}, bf16[4,640,256]{2,1,0:T(8,128)(2,1)}, u32[]{:S(2)}, u32[]{:S(2)}) %collective-permute-start.5) | collective-permute-done | bytes 1310752 | tf_op jit(solution)/shard_map/ppermute | solution.py:245
  107.1 11.2 %self_energy_0.1 = bf16[16,640,256]{2,1,0:T(8,128)(2,1)} custom-call(f32[8]{0:T(128)} %dynamic-slice_bitcast_fusion.weights, bf16[4,640,256]{2,1,0:T(8,128)(2,1)} %collective-permute-done.5.low, bf16[16,640,256]{2,1,0:T(8,128)(2,1)} %all_to_all.25.here, bf16[4,640,256]{2,1,0:T(8,128)(2,1)} %collective-permute-done.6.high), custom_call_target="tpu_custom_call" | custom-call | flops 41943040 | bytes 13107200 | tf_op jit(solution)/shard_map/self_energy_0/pallas_call | solution.py:63
  118.3 10.7 %all-to-all-done.here = bf16[16,432,256]{2,1,0:T(8,128)(2,1)S(1)} async-done(((bf16[16,432,256]{2,1,0:T(8,128)(2,1)}), bf16[16,432,256]{2,1,0:T(8,128)(2,1)S(1)}, u32[]{:S(2)}, u32[]{:S(2)}) %all-to-all-start) | async-done | bytes 3538976 | tf_op jit(solution)/shard_map/all_to_all | solution.py:234
  129.1 4.6 %all-to-all-start.2 = ((bf16[16,640,256]{2,1,0:T(8,128)(2,1)}), bf16[16,640,256]{2,1,0:T(8,128)(2,1)}, u32[]{:S(2)}, u32[]{:S(2)}) async-start(bf16[16,640,256]{2,1,0:T(8,128)(2,1)} %self_energy_0.1), calls=%async_computation.2 | async-start | bytes 10485760 | tf_op jit(solution)/shard_map/all_to_all | solution.py:234
  134.2 7.0 %collective-permute-done.2 = bf16[1,16,32,256]{3,2,1,0:T(8,128)(2,1)S(1)} collective-permute-done((bf16[1,16,32,256]{3,2,1,0:T(8,128)(2,1)S(1)}, bf16[1,16,32,256]{3,2,1,0:T(8,128)(2,1)S(1)}, u32[]{:S(2)}, u32[]{:S(2)}) %collective-permute-start.2) | collective-permute-done | bytes 262176 | tf_op jit(solution)/shard_map/ppermute | solution.py:254
  141.3 4.1 %collective-permute-start.3 = (bf16[2,16,32,256]{3,2,1,0:T(8,128)(2,1)S(1)}, bf16[2,16,32,256]{3,2,1,0:T(8,128)(2,1)S(1)}, u32[]{:S(2)}, u32[]{:S(2)}) collective-permute-start(bf16[2,16,32,256]{3,2,1,0:T(8,128)(2,1)S(1)} %pad_maximum_fusion.2), channel_id=1, source_target_pairs={{0,64},{16,80},{32,96},{48,112},{64,0},{80,16},{96,32},{112,48},{1... | collective-permute-start | bytes 1572872 | tf_op jit(solution)/shard_map/ppermute | solution.py:254
  145.4 7.2 %collective-permute-done.3 = bf16[2,16,32,256]{3,2,1,0:T(8,128)(2,1)S(1)} collective-permute-done((bf16[2,16,32,256]{3,2,1,0:T(8,128)(2,1)S(1)}, bf16[2,16,32,256]{3,2,1,0:T(8,128)(2,1)S(1)}, u32[]{:S(2)}, u32[]{:S(2)}) %collective-permute-start.3) | collective-permute-done | bytes 524320 | tf_op jit(solution)/shard_map/ppermute | solution.py:254
  153.8 2.9 collective-permute-start.1
  159.6 6.6 %collective-permute-done.1.high = bf16[4,384,256]{2,1,0:T(8,128)(2,1)S(1)} collective-permute-done((bf16[4,384,256]{2,1,0:T(8,128)(2,1)S(1)}, bf16[4,384,256]{2,1,0:T(8,128)(2,1)S(1)}, u32[]{:S(2)}, u32[]{:S(2)}) %collective-permute-start.1) | collective-permute-done | bytes 786464 | tf_op jit(solution)/shard_map/ppermute | solution.py:246
  167.1 3.0 collective-permute-done.low
  170.1 7.3 %self_energy_1.1 = bf16[16,384,256]{2,1,0:T(8,128)(2,1)} custom-call(f32[8]{0:T(128)} %dynamic-slice_bitcast_fusion.weights, bf16[4,384,256]{2,1,0:T(8,128)(2,1)} %collective-permute-done.low, bf16[16,432,256]{2,1,0:T(8,128)(2,1)} %copy-done.2, bf16[4,384,256]{2,1,0:T(8,128)(2,1)} %copy-done.10), custom_call_target="tpu_custom_call" | custom-call | flops 25165824 | bytes 7864320 | tf_op jit(solution)/shard_map/self_energy_1/pallas_call | solution.py:63
  180.3 16.3 %all-to-all-done.2.sigma = bf16[16,640,256]{2,1,0:T(8,128)(2,1)} async-done(((bf16[16,640,256]{2,1,0:T(8,128)(2,1)}), bf16[16,640,256]{2,1,0:T(8,128)(2,1)}, u32[]{:S(2)}, u32[]{:S(2)}) %all-to-all-start.2) | async-done | bytes 5242912 | tf_op jit(solution)/shard_map/all_to_all | solution.py:234
  196.5 6.0 %all-to-all-start.3 = ((bf16[16,384,256]{2,1,0:T(8,128)(2,1)}), bf16[16,384,256]{2,1,0:T(8,128)(2,1)S(1)}, u32[]{:S(2)}, u32[]{:S(2)}) async-start(bf16[16,384,256]{2,1,0:T(8,128)(2,1)} %self_energy_1.1), calls=%async_computation.3 | async-start | bytes 6291456 | tf_op jit(solution)/shard_map/all_to_all | solution.py:234
  202.5 15.8 %sweep_0.1 = (bf16[16,1024,256]{2,1,0:T(8,128)(2,1)}, bf16[1,1024,256]{2,1,0:T(8,128)(2,1)}) custom-call(s32[1]{0:T(128)} %bitcast.group, s32[16]{0:T(128)} %fusion.live, bf16[16,1024,256]{2,1,0:T(8,128)(2,1)} %bitcast.16, bf16[16,640,256]{2,1,0:T(8,128)(2,1)} %all-to-all-done.2.sigma, bf16[16,2,256,256]{3,2,1,0:T(8,128)(2,1)} %bitcast.18, ...), custom_call_target="tpu_custom_call" | custom-call | flops 8053063680 | bytes 18350080 | tf_op jit(solution)/shard_map/sweep_0/pallas_call | solution.py:142
  218.3 21.4 %all-to-all-done.3.sigma = bf16[16,384,256]{2,1,0:T(8,128)(2,1)S(1)} async-done(((bf16[16,384,256]{2,1,0:T(8,128)(2,1)}), bf16[16,384,256]{2,1,0:T(8,128)(2,1)S(1)}, u32[]{:S(2)}, u32[]{:S(2)}) %all-to-all-start.3) | async-done | bytes 3145760 | tf_op jit(solution)/shard_map/all_to_all | solution.py:234
  241.4 10.7 %sweep_10.1 = (bf16[16,1024,256]{2,1,0:T(8,128)(2,1)}, bf16[1,1024,256]{2,1,0:T(8,128)(2,1)}) custom-call(s32[1]{0:T(128)} %bitcast.group, s32[16]{0:T(128)} %fusion.live, bf16[1,1024,256]{2,1,0:T(8,128)(2,1)} %get-tuple-element.17.lead, bf16[16,384,256]{2,1,0:T(8,128)(2,1)} %copy-done.3, ...), custom_call_target="tpu_custom_call", output_to_operand_aliasing={{0}: (6, {})} | custom-call | flops 4831838208 | bytes 11010048 | tf_op jit(solution)/shard_map/sweep_10/pallas_call | solution.py:142
  252.1 101.5 %all_to_all.26.source = bf16[16,1024,256]{2,1,0:T(8,128)(2,1)S(1)} all-to-all(bf16[16,1024,256]{2,1,0:T(8,128)(2,1)} %get-tuple-element.20), channel_id=1, replica_groups=mesh['energy'=8,'layer'=16] {'layer'}, dimensions={0} | all-to-all | bytes 16777216 | tf_op jit(solution)/shard_map/all_to_all | solution.py:234
  353.6 3.4 settle.1
  (47 shorter events, 16.3 us)
Async XLA Ops:
  0.7 3.4 copy-start
  4.1 0.9 copy-start.1
  78.3 50.8 %all-to-all-start = ((bf16[16,432,256]{2,1,0:T(8,128)(2,1)}), bf16[16,432,256]{2,1,0:T(8,128)(2,1)S(1)}, u32[]{:S(2)}, u32[]{:S(2)}) async-start(bf16[16,432,256]{2,1,0:T(8,128)(2,1)} %get-tuple-element.13), calls=%async_computation | async-start | bytes 7077888 | tf_op jit(solution)/shard_map/all_to_all | solution.py:234
  82.5 7.8 %copy-start.11 = (s32[4]{0:T(128)S(1)}, s32[4]{0:T(128)}, u32[]{:S(2)}) copy-start(s32[4]{0:T(128)} %param.9) | copy-start | bytes 52
  82.5 7.8 %copy-start.12 = (f32[4]{0:T(128)S(1)}, f32[4]{0:T(128)}, u32[]{:S(2)}) copy-start(f32[4]{0:T(128)} %param.10) | copy-start | bytes 52
  86.0 17.3 %collective-permute-start.6 = (bf16[4,640,256]{2,1,0:T(8,128)(2,1)}, bf16[4,640,256]{2,1,0:T(8,128)(2,1)}, u32[]{:S(2)}, u32[]{:S(2)}) collective-permute-start(bf16[4,640,256]{2,1,0:T(8,128)(2,1)} %get-tuple-element.25), channel_id=1, source_target_pairs={{16,0},{32,16},{48,32},{64,48},{80,64},{96,80},{112,96},{17,1},{33... | collective-permute-start | bytes 3932168 | tf_op jit(solution)/shard_map/ppermute | solution.py:246
  87.9 19.2 %collective-permute-start.5 = (bf16[4,640,256]{2,1,0:T(8,128)(2,1)}, bf16[4,640,256]{2,1,0:T(8,128)(2,1)}, u32[]{:S(2)}, u32[]{:S(2)}) collective-permute-start(bf16[4,640,256]{2,1,0:T(8,128)(2,1)} %get-tuple-element.26), channel_id=1, source_target_pairs={{0,16},{16,32},{32,48},{48,64},{64,80},{80,96},{96,112},{1,17},{17... | collective-permute-start | bytes 3932168 | tf_op jit(solution)/shard_map/ppermute | solution.py:245
  129.0 29.6 %copy-start.2 = (bf16[16,432,256]{2,1,0:T(8,128)(2,1)}, bf16[16,432,256]{2,1,0:T(8,128)(2,1)S(1)}, u32[]{:S(2)}) copy-start(bf16[16,432,256]{2,1,0:T(8,128)(2,1)S(1)} %all-to-all-done.here) | copy-start | bytes 10616836
  129.1 67.5 %all-to-all-start.2 = ((bf16[16,640,256]{2,1,0:T(8,128)(2,1)}), bf16[16,640,256]{2,1,0:T(8,128)(2,1)}, u32[]{:S(2)}, u32[]{:S(2)}) async-start(bf16[16,640,256]{2,1,0:T(8,128)(2,1)} %self_energy_0.1), calls=%async_computation.2 | async-start | bytes 10485760 | tf_op jit(solution)/shard_map/all_to_all | solution.py:234
  133.7 26.0 %copy-start.4 = (bf16[1,16,32,256]{3,2,1,0:T(8,128)(2,1)}, bf16[1,16,32,256]{3,2,1,0:T(8,128)(2,1)S(1)}, u32[]{:S(2)}) copy-start(bf16[1,16,32,256]{3,2,1,0:T(8,128)(2,1)S(1)} %slice_bitcast_fusion) | copy-start | bytes 786436
  133.7 7.5 %collective-permute-start.2 = (bf16[1,16,32,256]{3,2,1,0:T(8,128)(2,1)S(1)}, bf16[1,16,32,256]{3,2,1,0:T(8,128)(2,1)S(1)}, u32[]{:S(2)}, u32[]{:S(2)}) collective-permute-start(bf16[1,16,32,256]{3,2,1,0:T(8,128)(2,1)S(1)} %slice_bitcast_fusion), channel_id=1, source_target_pairs={{0,32},{16,48},{32,0},{48,16},{64,96},{80,112},{96,64},{112,80},{1... | collective-permute-start | bytes 786440 | tf_op jit(solution)/shard_map/ppermute | solution.py:254
  141.2 25.0 %copy-start.6 = (bf16[1,16,32,256]{3,2,1,0:T(8,128)(2,1)}, bf16[1,16,32,256]{3,2,1,0:T(8,128)(2,1)S(1)}, u32[]{:S(2)}) copy-start(bf16[1,16,32,256]{3,2,1,0:T(8,128)(2,1)S(1)} %collective-permute-done.2) | copy-start | bytes 786436
  141.3 11.3 %collective-permute-start.3 = (bf16[2,16,32,256]{3,2,1,0:T(8,128)(2,1)S(1)}, bf16[2,16,32,256]{3,2,1,0:T(8,128)(2,1)S(1)}, u32[]{:S(2)}, u32[]{:S(2)}) collective-permute-start(bf16[2,16,32,256]{3,2,1,0:T(8,128)(2,1)S(1)} %pad_maximum_fusion.2), channel_id=1, source_target_pairs={{0,64},{16,80},{32,96},{48,112},{64,0},{80,16},{96,32},{112,48},{1... | collective-permute-start | bytes 1572872 | tf_op jit(solution)/shard_map/ppermute | solution.py:254
  152.5 13.7 %copy-start.8 = (bf16[2,16,32,256]{3,2,1,0:T(8,128)(2,1)}, bf16[2,16,32,256]{3,2,1,0:T(8,128)(2,1)S(1)}, u32[]{:S(2)}) copy-start(bf16[2,16,32,256]{3,2,1,0:T(8,128)(2,1)S(1)} %collective-permute-done.3) | copy-start | bytes 1572868
  153.7 23.8 %collective-permute-start.4 = (bf16[4,16,32,256]{3,2,1,0:T(8,128)(2,1)}, bf16[4,16,32,256]{3,2,1,0:T(8,128)(2,1)}, u32[]{:S(2)}, u32[]{:S(2)}) collective-permute-start(bf16[4,16,32,256]{3,2,1,0:T(8,128)(2,1)} %pad_maximum_fusion.1), channel_id=1, source_target_pairs={{0,16},{16,0},{32,48},{48,32},{64,80},{80,64},{96,112},{112,96},{1... | collective-permute-start | bytes 3145736 | tf_op jit(solution)/shard_map/ppermute | solution.py:254
  153.8 12.4 %collective-permute-start.1 = (bf16[4,384,256]{2,1,0:T(8,128)(2,1)S(1)}, bf16[4,384,256]{2,1,0:T(8,128)(2,1)S(1)}, u32[]{:S(2)}, u32[]{:S(2)}) collective-permute-start(bf16[4,384,256]{2,1,0:T(8,128)(2,1)S(1)} %get-tuple-element.27), channel_id=1, source_target_pairs={{16,0},{32,16},{48,32},{64,48},{80,64},{96,80},{112,96},{17,1},{33... | collective-permute-start | bytes 2359304 | tf_op jit(solution)/shard_map/ppermute | solution.py:246
  156.7 13.4 %collective-permute-start = (bf16[4,384,256]{2,1,0:T(8,128)(2,1)S(1)}, bf16[4,384,256]{2,1,0:T(8,128)(2,1)}, u32[]{:S(2)}, u32[]{:S(2)}) collective-permute-start(bf16[4,384,256]{2,1,0:T(8,128)(2,1)S(1)} %get-tuple-element.28), channel_id=1, source_target_pairs={{0,16},{16,32},{32,48},{48,64},{64,80},{80,96},{96,112},{1,17},{17... | collective-permute-start | bytes 2359304 | tf_op jit(solution)/shard_map/ppermute | solution.py:245
  166.2 0.9 copy-start.10
  167.1 10.4 %copy-start.5 = (bf16[1,16,32,256]{3,2,1,0:T(8,128)(2,1)S(1)}, bf16[1,16,32,256]{3,2,1,0:T(8,128)(2,1)}, u32[]{:S(2)}) copy-start(bf16[1,16,32,256]{3,2,1,0:T(8,128)(2,1)} %copy-done.4) | copy-start | bytes 786436
  170.1 7.3 %copy-start.7 = (bf16[1,16,32,256]{3,2,1,0:T(8,128)(2,1)S(1)}, bf16[1,16,32,256]{3,2,1,0:T(8,128)(2,1)}, u32[]{:S(2)}) copy-start(bf16[1,16,32,256]{3,2,1,0:T(8,128)(2,1)} %copy-done.6) | copy-start | bytes 786436
  170.1 7.4 %copy-start.9 = (bf16[2,16,32,256]{3,2,1,0:T(8,128)(2,1)S(1)}, bf16[2,16,32,256]{3,2,1,0:T(8,128)(2,1)}, u32[]{:S(2)}) copy-start(bf16[2,16,32,256]{3,2,1,0:T(8,128)(2,1)} %copy-done.8) | copy-start | bytes 1572868
  196.5 43.2 %all-to-all-start.3 = ((bf16[16,384,256]{2,1,0:T(8,128)(2,1)}), bf16[16,384,256]{2,1,0:T(8,128)(2,1)S(1)}, u32[]{:S(2)}, u32[]{:S(2)}) async-start(bf16[16,384,256]{2,1,0:T(8,128)(2,1)} %self_energy_1.1), calls=%async_computation.3 | async-start | bytes 6291456 | tf_op jit(solution)/shard_map/all_to_all | solution.py:234
  239.8 1.6 copy-start.3

commit v5 on v4

--- a/solution.py
+++ b/solution.py
@@ -11,7 +11,7 @@
 SHIFT_MAX = 4
 BOSE_RATIO = 0.5
 FIRST_LAYERS = 10
-LIVE_ROWS = 16
+LIVE_ROWS = 8
 ENERGY_BITS = (2, 4, 1)
 ENERGY_OFFSETS = tuple(
     sum(bit for place, bit in enumerate(ENERGY_BITS) if k >> place & 1) for k in range(8)
@@ -101,7 +101,12 @@
 
     v = matrix[...]
     halfway = dot_transposed(held[...], v).astype(narrow)
-    own = sigma[...].reshape(4 * orbitals, orbitals)
+    share = 4 * orbitals // sigma.shape[0]
+    if sigma.shape[1] == share:
+        own = sigma[...]
+    else:
+        own = sigma[:, pl.ds(pl.multiple_of(layer * share, share), share), :]
+    own = own.reshape(4 * orbitals, orbitals)
     source = []
     for k in range(4):
         part = slice(k * orbitals, (k + 1) * orbitals)
@@ -131,7 +136,9 @@
     state = pl.BlockSpec((1, 4 * orbitals, orbitals), lambda i, group, live: (0, 0, 0))
     in_specs = [
         state,
-        pl.BlockSpec((sources, share, orbitals), lambda i, group, live: (0, i, 0)),
+        pl.BlockSpec((sources, share, orbitals), lambda i, group, live: (0, i, 0))
+        if whole is None
+        else pl.BlockSpec(memory_space=pltpu.VMEM),
         pl.BlockSpec((1, 2, orbitals, orbitals), lambda i, group, live: (first + i, 0, 0, 0)),
         pl.BlockSpec((parts, 1, orbitals // parts, orbitals), lambda i, group, live: (0, first + i, 0, 0)),
     ]
@@ -155,8 +162,8 @@
             ],
         ),
         out_shape=[
-            jax.ShapeDtypeStruct((layers, 4 * orbitals, orbitals), jnp.bfloat16),
-            jax.ShapeDtypeStruct((1, 4 * orbitals, orbitals), jnp.bfloat16),
+            pltpu.HBM((layers, 4 * orbitals, orbitals), jnp.bfloat16),
+            pltpu.HBM((1, 4 * orbitals, orbitals), jnp.bfloat16),
         ],
         input_output_aliases={} if whole is None else {6: 0},
         cost_estimate=pl.CostEstimate(
@@ -164,44 +171,70 @@
             bytes_accessed=28 * count * orbitals**2,
             transcendentals=0,
         ),
+        compiler_params=pltpu.CompilerParams(vmem_limit_bytes=24 << 20),
         name=f"sweep_{first}",
     )(*operands)
 
 
-def pick_kernel(blocks, coupling, live, first, second, arrived, here, sent):
+def pick_kernel(blocks, coupling, live, first, second, held, extra, arrived, gone, here, sent):
     layers, devices, share, _ = blocks.shape
     split = first.shape[1] // share
-    rows = coupling.shape[1] // lax.axis_size("energy")
+    count = layers - split
+    rows = extra.shape[0] - LIVE_ROWS
     start = pl.multiple_of(lax.axis_index("energy") * rows, rows)
-    tail = (layers - split) * share
-    copies = []
-    for i in range(layers):
-        target = first if i < split else second
-        where = pl.ds((i if i < split else i - split) * share, share)
-        copies.append(pltpu.make_async_copy(blocks.at[i], target.at[:, where], arrived.at[i]))
-    for d in range(devices):
-        mine = coupling.at[0, pl.ds(start, rows)]
-        copies.append(pltpu.make_async_copy(mine, second.at[d, pl.ds(tail, rows)], here.at[d]))
-        target = second.at[d, pl.ds(tail + rows, LIVE_ROWS)]
-        copies.append(pltpu.make_async_copy(live, target, sent.at[d]))
-    for copy in copies:
+    extras = [
+        pltpu.make_async_copy(coupling.at[0, pl.ds(start, rows)], extra.at[pl.ds(0, rows)], here.at[0]),
+        pltpu.make_async_copy(live, extra.at[pl.ds(rows, LIVE_ROWS)], here.at[1]),
+    ]
+    tails = [
+        pltpu.make_async_copy(extra, second.at[d, pl.ds(count * share, rows + LIVE_ROWS)], sent.at[d])
+        for d in range(devices)
+    ]
+    fetches = [
+        pltpu.make_async_copy(blocks.at[split + i], held.at[i], arrived.at[i]) for i in range(count)
+    ]
+    puts = [
+        pltpu.make_async_copy(held.at[i], second.at[:, pl.ds(i * share, share)], gone.at[i])
+        for i in range(count)
+    ]
+    direct = [
+        pltpu.make_async_copy(blocks.at[i], first.at[:, pl.ds(i * share, share)], arrived.at[count + i])
+        for i in range(split)
+    ]
+    for copy in extras + fetches + direct:
         copy.start()
-    for copy in copies:
+    for copy in extras:
+        copy.wait()
+    for copy in tails:
+        copy.start()
+    for fetch, put in zip(fetches, puts):
+        fetch.wait()
+        put.start()
+    for copy in direct + tails + puts:
         copy.wait()
 
 
 def pick(blocks, coupling, live_rows):
     layers, devices, share, orbitals = blocks.shape
-    rows = orbitals // lax.axis_size("energy")
-    extra = rows + LIVE_ROWS
-    shapes = (FIRST_LAYERS * share, (layers - FIRST_LAYERS) * share + extra)
+    count = layers - FIRST_LAYERS
+    extra = orbitals // lax.axis_size("energy") + LIVE_ROWS
     return pl.pallas_call(
         pick_kernel,
         in_specs=[pl.BlockSpec(memory_space=pltpu.HBM)] * 3,
-        out_specs=[pl.BlockSpec(memory_space=pltpu.VMEM)] * 2,
-        out_shape=[pltpu.VMEM((devices, n, orbitals), blocks.dtype) for n in shapes],
-        scratch_shapes=[pltpu.SemaphoreType.DMA((n,)) for n in (layers, devices, devices)],
-        cost_estimate=pl.CostEstimate(flops=0, bytes_accessed=2 * blocks.size, transcendentals=0),
+        out_specs=[pl.BlockSpec(memory_space=pltpu.VMEM), pl.BlockSpec(memory_space=pltpu.HBM)],
+        out_shape=[
+            pltpu.VMEM((devices, FIRST_LAYERS * share, orbitals), blocks.dtype),
+            pltpu.HBM((devices, count * share + extra, orbitals), blocks.dtype),
+        ],
+        scratch_shapes=[
+            pltpu.VMEM((count, devices, share, orbitals), blocks.dtype),
+            pltpu.VMEM((extra, orbitals), blocks.dtype),
+            pltpu.SemaphoreType.DMA((layers,)),
+            pltpu.SemaphoreType.DMA((count,)),
+            pltpu.SemaphoreType.DMA((2,)),
+            pltpu.SemaphoreType.DMA((devices,)),
+        ],
+        cost_estimate=pl.CostEstimate(flops=0, bytes_accessed=4 * blocks.size, transcendentals=0),
         compiler_params=pltpu.CompilerParams(vmem_limit_bytes=16 << 20),
         name="pick",
     )(blocks, coupling, live_rows)
@@ -234,6 +267,10 @@
     return lax.all_to_all(block, "layer", split_axis=0, concat_axis=0, tiled=True)
 
 
+def in_hbm(array):
+    return pltpu.with_memory_space_constraint(array, pltpu.HBM)
+
+
 def exchange_into(block, space):
     return pltpu.with_memory_space_constraint(exchange(block), space)
 
@@ -264,7 +301,8 @@
     weights = lax.dynamic_index_in_dim(tap_weights(phonon_shifts, phonon_coupling), pair, 0, keepdims=False)
     group = lax.axis_index("energy").astype(jnp.int32)[None]
     live_rows = jnp.broadcast_to(layer_orbitals.astype(jnp.bfloat16)[:, None], (LIVE_ROWS, orbitals))
-    picked = pick(correlations.reshape(layers, devices, share, orbitals), coupling, live_rows)
+    blocks = correlations.reshape(layers, devices, share, orbitals)
+    picked = pick(in_hbm(blocks), in_hbm(coupling), live_rows)
     arrived = [exchange(block) for block in picked]
     rows = (FIRST_LAYERS * share, (layers - FIRST_LAYERS) * share)
     extra = arrived[1][:, rows[1] :]
@@ -276,10 +314,12 @@
         low, high = halo_of(arrived[c][:, : rows[c]])
         sigmas.append(self_energy(c, weights, low, arrived[c], high, rows[c], share))
     sigmas[1], couplings, live = lax.optimization_barrier((sigmas[1], couplings, live))
-    lead = correlations.reshape(layers, parts * orbitals, orbitals)
-    returned = [exchange_into(sigma, pltpu.HBM) for sigma in sigmas]
-    whole, lead = sweep(0, group, live, lead, returned[0], retarded[0], couplings)
-    whole, _ = sweep(FIRST_LAYERS, group, live, lead, returned[1], retarded[0], couplings, whole)
+    lead = in_hbm(correlations.reshape(layers, parts * orbitals, orbitals))
+    green, couplings = in_hbm(retarded[0]), in_hbm(couplings)
+    spaces = (pltpu.HBM, pltpu.VMEM)
+    returned = [exchange_into(sigma, space) for sigma, space in zip(sigmas, spaces)]
+    whole, lead = sweep(0, group, live, lead, returned[0], green, couplings)
+    whole, _ = sweep(FIRST_LAYERS, group, live, in_hbm(lead), returned[1], green, couplings, whole)
     return settle(exchange_into(whole, pltpu.VMEM)).reshape(layers, 1, parts, orbitals, orbitals)
 
 

time: 359 us -> 353 us (0.983)
  local copies, waits for them, and re-layouts: 11.1 us -> 5.24 us
    unnamed x26 -> x20, local copies, waits for them, and re-layouts: 6.86 us -> 0.93 us
where the time goes in v5:
time: 353 us; the launch traced here: 351 us
  blocking collectives  171 us (48%)
  waiting for transfers between devices  87.7 us (25%)
  Pallas kernels  53 us (15%)
  starting transfers between devices  28.6 us (8%)
  local copies, waits for them, and re-layouts  5.24 us (1%)
  other arithmetic  4.68 us (1%)
    all_to_all x2, blocking collectives, exchange(): lax.all_to_all(block, 'layer', split_axis=0, concat_axis=0, tiled=True)  171 us
    all_to_all x3, waiting for transfers between devices, exchange(): lax.all_to_all(block, 'layer', split_axis=0, concat_axis=0, tiled=True)  47.7 us
    pallas_call x2, Pallas kernels, sweep(): pl.pallas_call(functools.partial(sweep_kernel, first), grid_spec=pltpu.Pr...  26 us
    ppermute x2, waiting for transfers between devices, halo_of(): high = lax.ppermute(block[:SHIFT_MAX], 'energy', backward)  19 us
    pallas_call x2, Pallas kernels, self_energy(): pl.pallas_call(sigma_kernel, grid=(rows // share,), in_specs=[pl.BlockSpe...  18.6 us
    all_to_all x3, starting transfers between devices, exchange(): lax.all_to_all(block, 'layer', split_axis=0, concat_axis=0, tiled=True)  14.8 us
    ppermute x3, waiting for transfers between devices, all_couplings(): other = lax.ppermute(held, 'energy', [(i, i ^ bit) for i in range(count)])  14.1 us
  transfers between devices with their start and end apart: 10, of which 9 were waited for; matrix products, arithmetic and copies ran while one was open for 3% of the time, Pallas kernels for 10%

profile of v5, /device:TPU:8, one launch (start us, length us, event | category | flops | bytes accessed | tf_op | source)
XLA Modules:
  0.0 351.2 jit_solution(2460736828751742427)
XLA Ops:
  0.7 5.0 %pick.1 = (bf16[16,640,256]{2,1,0:T(8,128)(2,1)S(1)}, bf16[16,424,256]{2,1,0:T(8,128)(2,1)}) custom-call(bf16[16,16,64,256]{3,2,1,0:T(8,128)(2,1)} %bitcast.16, bf16[1,256,256]{2,1,0:T(8,128)(2,1)} %coupling.1, bf16[8,256]{1,0:T(8,128)(2,1)S(1)} %broadcast_in_dim.20.live), custom_call_target="tpu_custom_call" | custom-call | bytes 16777216 | tf_op jit(solution)/shard_map/pick/pallas_call | solution.py:221
  5.7 69.9 %all_to_all.25.here = bf16[16,640,256]{2,1,0:T(8,128)(2,1)} all-to-all(bf16[16,640,256]{2,1,0:T(8,128)(2,1)S(1)} %get-tuple-element.15), channel_id=1, replica_groups=mesh['energy'=8,'layer'=16] {'layer'}, dimensions={0} | all-to-all | bytes 10485760 | tf_op jit(solution)/shard_map/all_to_all | solution.py:267
  75.6 4.2 %all-to-all-start = ((bf16[16,424,256]{2,1,0:T(8,128)(2,1)}), bf16[16,424,256]{2,1,0:T(8,128)(2,1)S(1)}, u32[]{:S(2)}, u32[]{:S(2)}) async-start(bf16[16,424,256]{2,1,0:T(8,128)(2,1)} %get-tuple-element.13), calls=%async_computation | async-start | bytes 6946816 | tf_op jit(solution)/shard_map/all_to_all | solution.py:267
  79.9 3.4 fusion.4
  88.7 11.9 %collective-permute-done.6.high = bf16[4,640,256]{2,1,0:T(8,128)(2,1)} collective-permute-done((bf16[4,640,256]{2,1,0:T(8,128)(2,1)}, bf16[4,640,256]{2,1,0:T(8,128)(2,1)}, u32[]{:S(2)}, u32[]{:S(2)}) %collective-permute-start.6) | collective-permute-done | bytes 1310752 | tf_op jit(solution)/shard_map/ppermute | solution.py:283
  100.6 3.8 %collective-permute-done.5.low = bf16[4,640,256]{2,1,0:T(8,128)(2,1)} collective-permute-done((bf16[4,640,256]{2,1,0:T(8,128)(2,1)}, bf16[4,640,256]{2,1,0:T(8,128)(2,1)}, u32[]{:S(2)}, u32[]{:S(2)}) %collective-permute-start.5) | collective-permute-done | bytes 1310752 | tf_op jit(solution)/shard_map/ppermute | solution.py:282
  104.4 11.2 %self_energy_0.1 = bf16[16,640,256]{2,1,0:T(8,128)(2,1)} custom-call(f32[8]{0:T(128)} %dynamic-slice_bitcast_fusion.weights, bf16[4,640,256]{2,1,0:T(8,128)(2,1)} %collective-permute-done.5.low, bf16[16,640,256]{2,1,0:T(8,128)(2,1)} %all_to_all.25.here, bf16[4,640,256]{2,1,0:T(8,128)(2,1)} %collective-permute-done.6.high), custom_call_target="tpu_custom_call" | custom-call | flops 41943040 | bytes 13107200 | tf_op jit(solution)/shard_map/self_energy_0/pallas_call | solution.py:63
  115.6 9.9 %all-to-all-done.here = bf16[16,424,256]{2,1,0:T(8,128)(2,1)S(1)} async-done(((bf16[16,424,256]{2,1,0:T(8,128)(2,1)}), bf16[16,424,256]{2,1,0:T(8,128)(2,1)S(1)}, u32[]{:S(2)}, u32[]{:S(2)}) %all-to-all-start) | async-done | bytes 3473440 | tf_op jit(solution)/shard_map/all_to_all | solution.py:267
  125.6 4.6 %all-to-all-start.2 = ((bf16[16,640,256]{2,1,0:T(8,128)(2,1)}), bf16[16,640,256]{2,1,0:T(8,128)(2,1)}, u32[]{:S(2)}, u32[]{:S(2)}) async-start(bf16[16,640,256]{2,1,0:T(8,128)(2,1)} %self_energy_0.1), calls=%async_computation.2 | async-start | bytes 10485760 | tf_op jit(solution)/shard_map/all_to_all | solution.py:267
  130.7 7.0 %collective-permute-done.2 = bf16[1,16,32,256]{3,2,1,0:T(8,128)(2,1)S(1)} collective-permute-done((bf16[1,16,32,256]{3,2,1,0:T(8,128)(2,1)S(1)}, bf16[1,16,32,256]{3,2,1,0:T(8,128)(2,1)S(1)}, u32[]{:S(2)}, u32[]{:S(2)}) %collective-permute-start.2) | collective-permute-done | bytes 262176 | tf_op jit(solution)/shard_map/ppermute | solution.py:291
  137.8 4.1 %collective-permute-start.3 = (bf16[2,16,32,256]{3,2,1,0:T(8,128)(2,1)S(1)}, bf16[2,16,32,256]{3,2,1,0:T(8,128)(2,1)S(1)}, u32[]{:S(2)}, u32[]{:S(2)}) collective-permute-start(bf16[2,16,32,256]{3,2,1,0:T(8,128)(2,1)S(1)} %pad_maximum_fusion.2), channel_id=1, source_target_pairs={{0,64},{16,80},{32,96},{48,112},{64,0},{80,16},{96,32},{112,48},{1... | collective-permute-start | bytes 1572872 | tf_op jit(solution)/shard_map/ppermute | solution.py:291
  141.9 7.2 %collective-permute-done.3 = bf16[2,16,32,256]{3,2,1,0:T(8,128)(2,1)S(1)} collective-permute-done((bf16[2,16,32,256]{3,2,1,0:T(8,128)(2,1)S(1)}, bf16[2,16,32,256]{3,2,1,0:T(8,128)(2,1)S(1)}, u32[]{:S(2)}, u32[]{:S(2)}) %collective-permute-start.3) | collective-permute-done | bytes 524320 | tf_op jit(solution)/shard_map/ppermute | solution.py:291
  150.3 2.9 collective-permute-start.1
  155.6 7.2 %collective-permute-done.1.high = bf16[4,384,256]{2,1,0:T(8,128)(2,1)S(1)} collective-permute-done((bf16[4,384,256]{2,1,0:T(8,128)(2,1)S(1)}, bf16[4,384,256]{2,1,0:T(8,128)(2,1)S(1)}, u32[]{:S(2)}, u32[]{:S(2)}) %collective-permute-start.1) | collective-permute-done | bytes 786464 | tf_op jit(solution)/shard_map/ppermute | solution.py:283
  163.7 3.0 collective-permute-done.low
  166.7 7.4 %self_energy_1.1 = bf16[16,384,256]{2,1,0:T(8,128)(2,1)} custom-call(f32[8]{0:T(128)} %dynamic-slice_bitcast_fusion.weights, bf16[4,384,256]{2,1,0:T(8,128)(2,1)} %collective-permute-done.low, bf16[16,424,256]{2,1,0:T(8,128)(2,1)} %copy-done, bf16[4,384,256]{2,1,0:T(8,128)(2,1)} %copy-done.7), custom_call_target="tpu_custom_call" | custom-call | flops 25165824 | bytes 7864320 | tf_op jit(solution)/shard_map/self_energy_1/pallas_call | solution.py:63
  174.1 2.8 pad_maximum_fusion.coupling
  176.9 16.2 %all-to-all-done.2.sigma = bf16[16,640,256]{2,1,0:T(8,128)(2,1)} async-done(((bf16[16,640,256]{2,1,0:T(8,128)(2,1)}), bf16[16,640,256]{2,1,0:T(8,128)(2,1)}, u32[]{:S(2)}, u32[]{:S(2)}) %all-to-all-start.2) | async-done | bytes 5242912 | tf_op jit(solution)/shard_map/all_to_all | solution.py:267
  193.1 6.0 %all-to-all-start.3 = ((bf16[16,384,256]{2,1,0:T(8,128)(2,1)}), bf16[16,384,256]{2,1,0:T(8,128)(2,1)S(1)}, u32[]{:S(2)}, u32[]{:S(2)}) async-start(bf16[16,384,256]{2,1,0:T(8,128)(2,1)} %self_energy_1.1), calls=%async_computation.3 | async-start | bytes 6291456 | tf_op jit(solution)/shard_map/all_to_all | solution.py:267
  199.1 15.7 %sweep_0.1 = (bf16[16,1024,256]{2,1,0:T(8,128)(2,1)}, bf16[1,1024,256]{2,1,0:T(8,128)(2,1)}) custom-call(s32[1]{0:T(128)} %bitcast.group, s32[16]{0:T(128)S(1)} %fusion.live, bf16[16,1024,256]{2,1,0:T(8,128)(2,1)} %bitcast.17, bf16[16,640,256]{2,1,0:T(8,128)(2,1)} %all-to-all-done.2.sigma, bf16[16,2,256,256]{3,2,1,0:T(8,128)(2,1)} %bitcast.18, ...), custom_call_target="tpu_custom_call" | custom-call | flops 8053063680 | bytes 18350080 | tf_op jit(solution)/shard_map/sweep_0/pallas_call | solution.py:149
  214.8 21.5 %all-to-all-done.3.sigma = bf16[16,384,256]{2,1,0:T(8,128)(2,1)S(1)} async-done(((bf16[16,384,256]{2,1,0:T(8,128)(2,1)}), bf16[16,384,256]{2,1,0:T(8,128)(2,1)S(1)}, u32[]{:S(2)}, u32[]{:S(2)}) %all-to-all-start.3) | async-done | bytes 3145760 | tf_op jit(solution)/shard_map/all_to_all | solution.py:267
  236.3 10.2 %sweep_10.1 = (bf16[16,1024,256]{2,1,0:T(8,128)(2,1)}, bf16[1,1024,256]{2,1,0:T(8,128)(2,1)}) custom-call(s32[1]{0:T(128)} %bitcast.group, s32[16]{0:T(128)S(1)} %fusion.live, bf16[1,1024,256]{2,1,0:T(8,128)(2,1)} %get-tuple-element.17.lead, bf16[16,384,256]{2,1,0:T(8,128)(2,1)S(1)} %all-to-all-done.3.sigma, ...), custom_call_target="tpu_custom_call", output_to_operand_aliasing={{0}: (6, {})} | custom-call | flops 4831838208 | bytes 11010048 | tf_op jit(solution)/shard_map/sweep_10/pallas_call | solution.py:149
  246.6 101.3 %all_to_all.26.source = bf16[16,1024,256]{2,1,0:T(8,128)(2,1)S(1)} all-to-all(bf16[16,1024,256]{2,1,0:T(8,128)(2,1)} %get-tuple-element.20), channel_id=1, replica_groups=mesh['energy'=8,'layer'=16] {'layer'}, dimensions={0} | all-to-all | bytes 16777216 | tf_op jit(solution)/shard_map/all_to_all | solution.py:267
  347.8 3.4 settle.1
  (41 shorter events, 10.5 us)
Async XLA Ops:
  75.6 49.9 %all-to-all-start = ((bf16[16,424,256]{2,1,0:T(8,128)(2,1)}), bf16[16,424,256]{2,1,0:T(8,128)(2,1)S(1)}, u32[]{:S(2)}, u32[]{:S(2)}) async-start(bf16[16,424,256]{2,1,0:T(8,128)(2,1)} %get-tuple-element.13), calls=%async_computation | async-start | bytes 6946816 | tf_op jit(solution)/shard_map/all_to_all | solution.py:267
  79.8 7.8 %copy-start.8 = (s32[4]{0:T(128)S(1)}, s32[4]{0:T(128)}, u32[]{:S(2)}) copy-start(s32[4]{0:T(128)} %param.9) | copy-start | bytes 52
  79.9 7.8 %copy-start.9 = (f32[4]{0:T(128)S(1)}, f32[4]{0:T(128)}, u32[]{:S(2)}) copy-start(f32[4]{0:T(128)} %param.10) | copy-start | bytes 52
  83.3 17.3 %collective-permute-start.6 = (bf16[4,640,256]{2,1,0:T(8,128)(2,1)}, bf16[4,640,256]{2,1,0:T(8,128)(2,1)}, u32[]{:S(2)}, u32[]{:S(2)}) collective-permute-start(bf16[4,640,256]{2,1,0:T(8,128)(2,1)} %get-tuple-element.25), channel_id=1, source_target_pairs={{16,0},{32,16},{48,32},{64,48},{80,64},{96,80},{112,96},{17,1},{33... | collective-permute-start | bytes 3932168 | tf_op jit(solution)/shard_map/ppermute | solution.py:283
  85.2 19.2 %collective-permute-start.5 = (bf16[4,640,256]{2,1,0:T(8,128)(2,1)}, bf16[4,640,256]{2,1,0:T(8,128)(2,1)}, u32[]{:S(2)}, u32[]{:S(2)}) collective-permute-start(bf16[4,640,256]{2,1,0:T(8,128)(2,1)} %get-tuple-element.26), channel_id=1, source_target_pairs={{0,16},{16,32},{32,48},{48,64},{64,80},{80,96},{96,112},{1,17},{17... | collective-permute-start | bytes 3932168 | tf_op jit(solution)/shard_map/ppermute | solution.py:282
  125.6 29.7 %copy-start = (bf16[16,424,256]{2,1,0:T(8,128)(2,1)}, bf16[16,424,256]{2,1,0:T(8,128)(2,1)S(1)}, u32[]{:S(2)}) copy-start(bf16[16,424,256]{2,1,0:T(8,128)(2,1)S(1)} %all-to-all-done.here) | copy-start | bytes 10420228
  125.6 67.5 %all-to-all-start.2 = ((bf16[16,640,256]{2,1,0:T(8,128)(2,1)}), bf16[16,640,256]{2,1,0:T(8,128)(2,1)}, u32[]{:S(2)}, u32[]{:S(2)}) async-start(bf16[16,640,256]{2,1,0:T(8,128)(2,1)} %self_energy_0.1), calls=%async_computation.2 | async-start | bytes 10485760 | tf_op jit(solution)/shard_map/all_to_all | solution.py:267
  130.2 25.4 %copy-start.1 = (bf16[1,16,32,256]{3,2,1,0:T(8,128)(2,1)}, bf16[1,16,32,256]{3,2,1,0:T(8,128)(2,1)S(1)}, u32[]{:S(2)}) copy-start(bf16[1,16,32,256]{3,2,1,0:T(8,128)(2,1)S(1)} %slice_bitcast_fusion) | copy-start | bytes 786436
  130.2 7.5 %collective-permute-start.2 = (bf16[1,16,32,256]{3,2,1,0:T(8,128)(2,1)S(1)}, bf16[1,16,32,256]{3,2,1,0:T(8,128)(2,1)S(1)}, u32[]{:S(2)}, u32[]{:S(2)}) collective-permute-start(bf16[1,16,32,256]{3,2,1,0:T(8,128)(2,1)S(1)} %slice_bitcast_fusion), channel_id=1, source_target_pairs={{0,32},{16,48},{32,0},{48,16},{64,96},{80,112},{96,64},{112,80},{1... | collective-permute-start | bytes 786440 | tf_op jit(solution)/shard_map/ppermute | solution.py:291
  137.7 25.1 %copy-start.3 = (bf16[1,16,32,256]{3,2,1,0:T(8,128)(2,1)}, bf16[1,16,32,256]{3,2,1,0:T(8,128)(2,1)S(1)}, u32[]{:S(2)}) copy-start(bf16[1,16,32,256]{3,2,1,0:T(8,128)(2,1)S(1)} %collective-permute-done.2) | copy-start | bytes 786436
  137.8 11.3 %collective-permute-start.3 = (bf16[2,16,32,256]{3,2,1,0:T(8,128)(2,1)S(1)}, bf16[2,16,32,256]{3,2,1,0:T(8,128)(2,1)S(1)}, u32[]{:S(2)}, u32[]{:S(2)}) collective-permute-start(bf16[2,16,32,256]{3,2,1,0:T(8,128)(2,1)S(1)} %pad_maximum_fusion.2), channel_id=1, source_target_pairs={{0,64},{16,80},{32,96},{48,112},{64,0},{80,16},{96,32},{112,48},{1... | collective-permute-start | bytes 1572872 | tf_op jit(solution)/shard_map/ppermute | solution.py:291
  149.0 13.7 %copy-start.5 = (bf16[2,16,32,256]{3,2,1,0:T(8,128)(2,1)}, bf16[2,16,32,256]{3,2,1,0:T(8,128)(2,1)S(1)}, u32[]{:S(2)}) copy-start(bf16[2,16,32,256]{3,2,1,0:T(8,128)(2,1)S(1)} %collective-permute-done.3) | copy-start | bytes 1572868
  150.2 23.8 %collective-permute-start.4 = (bf16[4,16,32,256]{3,2,1,0:T(8,128)(2,1)}, bf16[4,16,32,256]{3,2,1,0:T(8,128)(2,1)}, u32[]{:S(2)}, u32[]{:S(2)}) collective-permute-start(bf16[4,16,32,256]{3,2,1,0:T(8,128)(2,1)} %pad_maximum_fusion.1), channel_id=1, source_target_pairs={{0,16},{16,0},{32,48},{48,32},{64,80},{80,64},{96,112},{112,96},{1... | collective-permute-start | bytes 3145736 | tf_op jit(solution)/shard_map/ppermute | solution.py:291
  150.3 12.4 %collective-permute-start.1 = (bf16[4,384,256]{2,1,0:T(8,128)(2,1)S(1)}, bf16[4,384,256]{2,1,0:T(8,128)(2,1)S(1)}, u32[]{:S(2)}, u32[]{:S(2)}) collective-permute-start(bf16[4,384,256]{2,1,0:T(8,128)(2,1)S(1)} %get-tuple-element.27), channel_id=1, source_target_pairs={{16,0},{32,16},{48,32},{64,48},{80,64},{96,80},{112,96},{17,1},{33... | collective-permute-start | bytes 2359304 | tf_op jit(solution)/shard_map/ppermute | solution.py:283
  153.3 13.4 %collective-permute-start = (bf16[4,384,256]{2,1,0:T(8,128)(2,1)S(1)}, bf16[4,384,256]{2,1,0:T(8,128)(2,1)}, u32[]{:S(2)}, u32[]{:S(2)}) collective-permute-start(bf16[4,384,256]{2,1,0:T(8,128)(2,1)S(1)} %get-tuple-element.28), channel_id=1, source_target_pairs={{0,16},{16,32},{32,48},{48,64},{64,80},{80,96},{96,112},{1,17},{17... | collective-permute-start | bytes 2359304 | tf_op jit(solution)/shard_map/ppermute | solution.py:282
  162.8 0.9 copy-start.7
  163.7 10.4 %copy-start.2 = (bf16[1,16,32,256]{3,2,1,0:T(8,128)(2,1)S(1)}, bf16[1,16,32,256]{3,2,1,0:T(8,128)(2,1)}, u32[]{:S(2)}) copy-start(bf16[1,16,32,256]{3,2,1,0:T(8,128)(2,1)} %copy-done.1) | copy-start | bytes 786436
  166.7 7.4 %copy-start.4 = (bf16[1,16,32,256]{3,2,1,0:T(8,128)(2,1)S(1)}, bf16[1,16,32,256]{3,2,1,0:T(8,128)(2,1)}, u32[]{:S(2)}) copy-start(bf16[1,16,32,256]{3,2,1,0:T(8,128)(2,1)} %copy-done.3) | copy-start | bytes 786436
  166.7 7.4 %copy-start.6 = (bf16[2,16,32,256]{3,2,1,0:T(8,128)(2,1)S(1)}, bf16[2,16,32,256]{3,2,1,0:T(8,128)(2,1)}, u32[]{:S(2)}) copy-start(bf16[2,16,32,256]{3,2,1,0:T(8,128)(2,1)} %copy-done.5) | copy-start | bytes 1572868
  193.1 43.2 %all-to-all-start.3 = ((bf16[16,384,256]{2,1,0:T(8,128)(2,1)}), bf16[16,384,256]{2,1,0:T(8,128)(2,1)S(1)}, u32[]{:S(2)}, u32[]{:S(2)}) async-start(bf16[16,384,256]{2,1,0:T(8,128)(2,1)} %self_energy_1.1), calls=%async_computation.3 | async-start | bytes 6291456 | tf_op jit(solution)/shard_map/all_to_all | solution.py:267

commit v6 on v5

--- a/solution.py
+++ b/solution.py
@@ -82,7 +82,8 @@
 
 
 def sweep_kernel(first, group, live, lead, sigma, green, coupling, *rest):
-    out, last, held, matrix = rest[-4:]
+    last = rest[1] if first == 0 else None
+    out, held, matrix = rest[0] if first == 0 else rest[1], rest[-2], rest[-1]
     narrow = jnp.bfloat16
     orbitals = green.shape[-1]
     rows = coupling.shape[2]
@@ -124,26 +125,31 @@
     outer = dot_transposed(jnp.concatenate(stacked, axis=0), g_plus).astype(narrow)
     held[...] = outer
     out[0] = outer
-    last[0] = outer
-
-
-def sweep(first, group, live, lead, sigma, retarded, couplings, whole=None):
-    layers, _, orbitals, _ = retarded.shape
+    if last is not None:
+        last[0] = outer
+
+
+def sweep(first, layers, group, live, lead, sigma, green, couplings, whole=None):
+    orbitals = green.shape[-1]
     sources, rows, _ = sigma.shape
     share = 4 * orbitals // sources
     count = rows // share
     parts = couplings.shape[0]
     state = pl.BlockSpec((1, 4 * orbitals, orbitals), lambda i, group, live: (0, 0, 0))
+    output = pl.BlockSpec((1, 4 * orbitals, orbitals), lambda i, group, live: (first + i, 0, 0))
+    operands = [group, live, lead, sigma, green, couplings]
+    out_specs, out_shape = [output], [pltpu.HBM((layers, 4 * orbitals, orbitals), jnp.bfloat16)]
     in_specs = [
         state,
-        pl.BlockSpec((sources, share, orbitals), lambda i, group, live: (0, i, 0))
-        if whole is None
-        else pl.BlockSpec(memory_space=pltpu.VMEM),
+        pl.BlockSpec((sources, share, orbitals), lambda i, group, live: (0, i, 0)),
         pl.BlockSpec((1, 2, orbitals, orbitals), lambda i, group, live: (first + i, 0, 0, 0)),
         pl.BlockSpec((parts, 1, orbitals // parts, orbitals), lambda i, group, live: (0, first + i, 0, 0)),
     ]
-    operands = [group, live, lead, sigma, retarded, couplings]
-    if whole is not None:
+    if whole is None:
+        out_specs.append(state)
+        out_shape.append(pltpu.HBM((1, 4 * orbitals, orbitals), jnp.bfloat16))
+    else:
+        in_specs[1] = pl.BlockSpec(memory_space=pltpu.VMEM)
         in_specs.append(pl.BlockSpec(memory_space=pl.ANY))
         operands.append(whole)
     return pl.pallas_call(
@@ -152,19 +158,13 @@
             num_scalar_prefetch=2,
             grid=(count,),
             in_specs=in_specs,
-            out_specs=[
-                pl.BlockSpec((1, 4 * orbitals, orbitals), lambda i, group, live: (first + i, 0, 0)),
-                state,
-            ],
+            out_specs=out_specs,
             scratch_shapes=[
                 pltpu.VMEM((4 * orbitals, orbitals), jnp.bfloat16),
                 pltpu.VMEM((orbitals, orbitals), jnp.bfloat16),
             ],
         ),
-        out_shape=[
-            pltpu.HBM((layers, 4 * orbitals, orbitals), jnp.bfloat16),
-            pltpu.HBM((1, 4 * orbitals, orbitals), jnp.bfloat16),
-        ],
+        out_shape=out_shape,
         input_output_aliases={} if whole is None else {6: 0},
         cost_estimate=pl.CostEstimate(
             flops=48 * count * orbitals**3,
@@ -312,14 +312,14 @@
     sigmas = []
     for c in range(2):
         low, high = halo_of(arrived[c][:, : rows[c]])
-        sigmas.append(self_energy(c, weights, low, arrived[c], high, rows[c], share))
+        sigmas.append(self_energy(c, weights, low, arrived[c], high, rows[c], 2 * share))
     sigmas[1], couplings, live = lax.optimization_barrier((sigmas[1], couplings, live))
     lead = in_hbm(correlations.reshape(layers, parts * orbitals, orbitals))
     green, couplings = in_hbm(retarded[0]), in_hbm(couplings)
     spaces = (pltpu.HBM, pltpu.VMEM)
     returned = [exchange_into(sigma, space) for sigma, space in zip(sigmas, spaces)]
-    whole, lead = sweep(0, group, live, lead, returned[0], green, couplings)
-    whole, _ = sweep(FIRST_LAYERS, group, live, in_hbm(lead), returned[1], green, couplings, whole)
+    whole, lead = sweep(0, layers, group, live, lead, returned[0], green, couplings)
+    (whole,) = sweep(FIRST_LAYERS, layers, group, live, in_hbm(lead), returned[1], green, couplings, whole)
     return settle(exchange_into(whole, pltpu.VMEM)).reshape(layers, 1, parts, orbitals, orbitals)
 
 

time: 353 us -> 352 us (level)
  transfers between devices with their start and end apart: 10 -> 10, of which waited for: 9 -> 9; matrix products, arithmetic and copies ran while one was open for 3% -> 3% of each run, Pallas kernels for 10% -> 9%
where the time goes in v6:
time: 352 us; the launch traced here: 351 us
  blocking collectives  171 us (49%)
  waiting for transfers between devices  90 us (26%)
  Pallas kernels  50.4 us (14%)
  starting transfers between devices  28.6 us (8%)
  local copies, waits for them, and re-layouts  5.2 us (1%)
  other arithmetic  4.65 us (1%)
    all_to_all x2, blocking collectives, exchange(): lax.all_to_all(block, 'layer', split_axis=0, concat_axis=0, tiled=True)  171 us
    all_to_all x3, waiting for transfers between devices, exchange(): lax.all_to_all(block, 'layer', split_axis=0, concat_axis=0, tiled=True)  50 us
    pallas_call x2, Pallas kernels, sweep(): pl.pallas_call(functools.partial(sweep_kernel, first), grid_spec=pltpu.Pr...  25.7 us
    ppermute x2, waiting for transfers between devices, halo_of(): high = lax.ppermute(block[:SHIFT_MAX], 'energy', backward)  19.1 us
    pallas_call x2, Pallas kernels, self_energy(): pl.pallas_call(sigma_kernel, grid=(rows // share,), in_specs=[pl.BlockSpe...  16.3 us
    all_to_all x3, starting transfers between devices, exchange(): lax.all_to_all(block, 'layer', split_axis=0, concat_axis=0, tiled=True)  14.8 us
    ppermute x3, waiting for transfers between devices, all_couplings(): other = lax.ppermute(held, 'energy', [(i, i ^ bit) for i in range(count)])  14.1 us
  transfers between devices with their start and end apart: 10, of which 9 were waited for; matrix products, arithmetic and copies ran while one was open for 3% of the time, Pallas kernels for 9%

profile of v6, /device:TPU:8, one launch (start us, length us, event | category | flops | bytes accessed | tf_op | source)
XLA Modules:
  0.0 351.0 jit_solution(9788496933815195857)
XLA Ops:
  0.7 5.0 %pick.1 = (bf16[16,640,256]{2,1,0:T(8,128)(2,1)S(1)}, bf16[16,424,256]{2,1,0:T(8,128)(2,1)}) custom-call(bf16[16,16,64,256]{3,2,1,0:T(8,128)(2,1)} %bitcast.16, bf16[1,256,256]{2,1,0:T(8,128)(2,1)} %coupling.1, bf16[8,256]{1,0:T(8,128)(2,1)S(1)} %broadcast_in_dim.20.live), custom_call_target="tpu_custom_call" | custom-call | bytes 16777216 | tf_op jit(solution)/shard_map/pick/pallas_call | solution.py:221
  5.7 69.9 %all_to_all.25.here = bf16[16,640,256]{2,1,0:T(8,128)(2,1)} all-to-all(bf16[16,640,256]{2,1,0:T(8,128)(2,1)S(1)} %get-tuple-element.14), channel_id=1, replica_groups=mesh['energy'=8,'layer'=16] {'layer'}, dimensions={0} | all-to-all | bytes 10485760 | tf_op jit(solution)/shard_map/all_to_all | solution.py:267
  75.6 4.2 %all-to-all-start = ((bf16[16,424,256]{2,1,0:T(8,128)(2,1)}), bf16[16,424,256]{2,1,0:T(8,128)(2,1)S(1)}, u32[]{:S(2)}, u32[]{:S(2)}) async-start(bf16[16,424,256]{2,1,0:T(8,128)(2,1)} %get-tuple-element.12), calls=%async_computation | async-start | bytes 6946816 | tf_op jit(solution)/shard_map/all_to_all | solution.py:267
  79.9 3.4 fusion.4
  88.7 11.9 %collective-permute-done.6.high = bf16[4,640,256]{2,1,0:T(8,128)(2,1)} collective-permute-done((bf16[4,640,256]{2,1,0:T(8,128)(2,1)}, bf16[4,640,256]{2,1,0:T(8,128)(2,1)}, u32[]{:S(2)}, u32[]{:S(2)}) %collective-permute-start.6) | collective-permute-done | bytes 1310752 | tf_op jit(solution)/shard_map/ppermute | solution.py:283
  100.6 3.8 %collective-permute-done.5.low = bf16[4,640,256]{2,1,0:T(8,128)(2,1)} collective-permute-done((bf16[4,640,256]{2,1,0:T(8,128)(2,1)}, bf16[4,640,256]{2,1,0:T(8,128)(2,1)}, u32[]{:S(2)}, u32[]{:S(2)}) %collective-permute-start.5) | collective-permute-done | bytes 1310752 | tf_op jit(solution)/shard_map/ppermute | solution.py:282
  104.4 9.6 %self_energy_0.1 = bf16[16,640,256]{2,1,0:T(8,128)(2,1)} custom-call(f32[8]{0:T(128)} %dynamic-slice_bitcast_fusion.weights, bf16[4,640,256]{2,1,0:T(8,128)(2,1)} %collective-permute-done.5.low, bf16[16,640,256]{2,1,0:T(8,128)(2,1)} %all_to_all.25.here, bf16[4,640,256]{2,1,0:T(8,128)(2,1)} %collective-permute-done.6.high), custom_call_target="tpu_custom_call" | custom-call | flops 41943040 | bytes 13107200 | tf_op jit(solution)/shard_map/self_energy_0/pallas_call | solution.py:63
  114.0 11.6 %all-to-all-done.here = bf16[16,424,256]{2,1,0:T(8,128)(2,1)S(1)} async-done(((bf16[16,424,256]{2,1,0:T(8,128)(2,1)}), bf16[16,424,256]{2,1,0:T(8,128)(2,1)S(1)}, u32[]{:S(2)}, u32[]{:S(2)}) %all-to-all-start) | async-done | bytes 3473440 | tf_op jit(solution)/shard_map/all_to_all | solution.py:267
  125.6 4.6 %all-to-all-start.2 = ((bf16[16,640,256]{2,1,0:T(8,128)(2,1)}), bf16[16,640,256]{2,1,0:T(8,128)(2,1)}, u32[]{:S(2)}, u32[]{:S(2)}) async-start(bf16[16,640,256]{2,1,0:T(8,128)(2,1)} %self_energy_0.1), calls=%async_computation.2 | async-start | bytes 10485760 | tf_op jit(solution)/shard_map/all_to_all | solution.py:267
  130.7 7.0 %collective-permute-done.2 = bf16[1,16,32,256]{3,2,1,0:T(8,128)(2,1)S(1)} collective-permute-done((bf16[1,16,32,256]{3,2,1,0:T(8,128)(2,1)S(1)}, bf16[1,16,32,256]{3,2,1,0:T(8,128)(2,1)S(1)}, u32[]{:S(2)}, u32[]{:S(2)}) %collective-permute-start.2) | collective-permute-done | bytes 262176 | tf_op jit(solution)/shard_map/ppermute | solution.py:291
  137.8 4.1 %collective-permute-start.3 = (bf16[2,16,32,256]{3,2,1,0:T(8,128)(2,1)S(1)}, bf16[2,16,32,256]{3,2,1,0:T(8,128)(2,1)S(1)}, u32[]{:S(2)}, u32[]{:S(2)}) collective-permute-start(bf16[2,16,32,256]{3,2,1,0:T(8,128)(2,1)S(1)} %pad_maximum_fusion.2), channel_id=1, source_target_pairs={{0,64},{16,80},{32,96},{48,112},{64,0},{80,16},{96,32},{112,48},{1... | collective-permute-start | bytes 1572872 | tf_op jit(solution)/shard_map/ppermute | solution.py:291
  141.9 7.2 %collective-permute-done.3 = bf16[2,16,32,256]{3,2,1,0:T(8,128)(2,1)S(1)} collective-permute-done((bf16[2,16,32,256]{3,2,1,0:T(8,128)(2,1)S(1)}, bf16[2,16,32,256]{3,2,1,0:T(8,128)(2,1)S(1)}, u32[]{:S(2)}, u32[]{:S(2)}) %collective-permute-start.3) | collective-permute-done | bytes 524320 | tf_op jit(solution)/shard_map/ppermute | solution.py:291
  150.3 2.9 collective-permute-start.1
  155.6 7.2 %collective-permute-done.1.high = bf16[4,384,256]{2,1,0:T(8,128)(2,1)S(1)} collective-permute-done((bf16[4,384,256]{2,1,0:T(8,128)(2,1)S(1)}, bf16[4,384,256]{2,1,0:T(8,128)(2,1)S(1)}, u32[]{:S(2)}, u32[]{:S(2)}) %collective-permute-start.1) | collective-permute-done | bytes 786464 | tf_op jit(solution)/shard_map/ppermute | solution.py:283
  163.6 3.0 collective-permute-done.low
  166.7 6.7 %self_energy_1.1 = bf16[16,384,256]{2,1,0:T(8,128)(2,1)} custom-call(f32[8]{0:T(128)} %dynamic-slice_bitcast_fusion.weights, bf16[4,384,256]{2,1,0:T(8,128)(2,1)} %collective-permute-done.low, bf16[16,424,256]{2,1,0:T(8,128)(2,1)} %copy-done, bf16[4,384,256]{2,1,0:T(8,128)(2,1)} %copy-done.7), custom_call_target="tpu_custom_call" | custom-call | flops 25165824 | bytes 7864320 | tf_op jit(solution)/shard_map/self_energy_1/pallas_call | solution.py:63
  173.4 2.8 pad_maximum_fusion.coupling
  176.2 16.9 %all-to-all-done.2.sigma = bf16[16,640,256]{2,1,0:T(8,128)(2,1)} async-done(((bf16[16,640,256]{2,1,0:T(8,128)(2,1)}), bf16[16,640,256]{2,1,0:T(8,128)(2,1)}, u32[]{:S(2)}, u32[]{:S(2)}) %all-to-all-start.2) | async-done | bytes 5242912 | tf_op jit(solution)/shard_map/all_to_all | solution.py:267
  193.1 6.0 %all-to-all-start.3 = ((bf16[16,384,256]{2,1,0:T(8,128)(2,1)}), bf16[16,384,256]{2,1,0:T(8,128)(2,1)S(1)}, u32[]{:S(2)}, u32[]{:S(2)}) async-start(bf16[16,384,256]{2,1,0:T(8,128)(2,1)} %self_energy_1.1), calls=%async_computation.3 | async-start | bytes 6291456 | tf_op jit(solution)/shard_map/all_to_all | solution.py:267
  199.1 15.7 %sweep_0.1 = (bf16[16,1024,256]{2,1,0:T(8,128)(2,1)}, bf16[1,1024,256]{2,1,0:T(8,128)(2,1)}) custom-call(s32[1]{0:T(128)} %bitcast.group, s32[16]{0:T(128)S(1)} %fusion.live, bf16[16,1024,256]{2,1,0:T(8,128)(2,1)} %bitcast.17, bf16[16,640,256]{2,1,0:T(8,128)(2,1)} %all-to-all-done.2.sigma, bf16[16,2,256,256]{3,2,1,0:T(8,128)(2,1)} %bitcast.18, ...), custom_call_target="tpu_custom_call" | custom-call | flops 8053063680 | bytes 18350080 | tf_op jit(solution)/shard_map/sweep_0/pallas_call | solution.py:155
  214.8 21.5 %all-to-all-done.3.sigma = bf16[16,384,256]{2,1,0:T(8,128)(2,1)S(1)} async-done(((bf16[16,384,256]{2,1,0:T(8,128)(2,1)}), bf16[16,384,256]{2,1,0:T(8,128)(2,1)S(1)}, u32[]{:S(2)}, u32[]{:S(2)}) %all-to-all-start.3) | async-done | bytes 3145760 | tf_op jit(solution)/shard_map/all_to_all | solution.py:267
  236.3 10.0 %sweep_10.1 = bf16[16,1024,256]{2,1,0:T(8,128)(2,1)} custom-call(s32[1]{0:T(128)} %bitcast.group, s32[16]{0:T(128)S(1)} %fusion.live, bf16[1,1024,256]{2,1,0:T(8,128)(2,1)} %get-tuple-element.16.lead, bf16[16,384,256]{2,1,0:T(8,128)(2,1)S(1)} %all-to-all-done.3.sigma, bf16[16,2,256,256]{3,2,1,0:T(8,128)(2,1)} %bitcast.19, ...), custom_call_target="tpu_custom_call", output_to_operand_aliasing={{}: (6, {})} | custom-call | flops 4831838208 | bytes 11010048 | tf_op jit(solution)/shard_map/sweep_10/pallas_call | solution.py:155
  246.3 101.3 %all_to_all.26.source = bf16[16,1024,256]{2,1,0:T(8,128)(2,1)S(1)} all-to-all(bf16[16,1024,256]{2,1,0:T(8,128)(2,1)} %sweep_10.1), channel_id=1, replica_groups=mesh['energy'=8,'layer'=16] {'layer'}, dimensions={0} | all-to-all | bytes 16777216 | tf_op jit(solution)/shard_map/all_to_all | solution.py:267
  347.6 3.4 settle.1
  (41 shorter events, 10.4 us)
Async XLA Ops:
  75.6 49.9 %all-to-all-start = ((bf16[16,424,256]{2,1,0:T(8,128)(2,1)}), bf16[16,424,256]{2,1,0:T(8,128)(2,1)S(1)}, u32[]{:S(2)}, u32[]{:S(2)}) async-start(bf16[16,424,256]{2,1,0:T(8,128)(2,1)} %get-tuple-element.12), calls=%async_computation | async-start | bytes 6946816 | tf_op jit(solution)/shard_map/all_to_all | solution.py:267
  79.8 7.8 %copy-start.8 = (s32[4]{0:T(128)S(1)}, s32[4]{0:T(128)}, u32[]{:S(2)}) copy-start(s32[4]{0:T(128)} %param.9) | copy-start | bytes 52
  79.9 7.8 %copy-start.9 = (f32[4]{0:T(128)S(1)}, f32[4]{0:T(128)}, u32[]{:S(2)}) copy-start(f32[4]{0:T(128)} %param.10) | copy-start | bytes 52
  83.3 17.3 %collective-permute-start.6 = (bf16[4,640,256]{2,1,0:T(8,128)(2,1)}, bf16[4,640,256]{2,1,0:T(8,128)(2,1)}, u32[]{:S(2)}, u32[]{:S(2)}) collective-permute-start(bf16[4,640,256]{2,1,0:T(8,128)(2,1)} %get-tuple-element.23), channel_id=1, source_target_pairs={{16,0},{32,16},{48,32},{64,48},{80,64},{96,80},{112,96},{17,1},{33... | collective-permute-start | bytes 3932168 | tf_op jit(solution)/shard_map/ppermute | solution.py:283
  85.2 19.2 %collective-permute-start.5 = (bf16[4,640,256]{2,1,0:T(8,128)(2,1)}, bf16[4,640,256]{2,1,0:T(8,128)(2,1)}, u32[]{:S(2)}, u32[]{:S(2)}) collective-permute-start(bf16[4,640,256]{2,1,0:T(8,128)(2,1)} %get-tuple-element.24), channel_id=1, source_target_pairs={{0,16},{16,32},{32,48},{48,64},{64,80},{80,96},{96,112},{1,17},{17... | collective-permute-start | bytes 3932168 | tf_op jit(solution)/shard_map/ppermute | solution.py:282
  125.6 29.6 %copy-start = (bf16[16,424,256]{2,1,0:T(8,128)(2,1)}, bf16[16,424,256]{2,1,0:T(8,128)(2,1)S(1)}, u32[]{:S(2)}) copy-start(bf16[16,424,256]{2,1,0:T(8,128)(2,1)S(1)} %all-to-all-done.here) | copy-start | bytes 10420228
  125.6 67.5 %all-to-all-start.2 = ((bf16[16,640,256]{2,1,0:T(8,128)(2,1)}), bf16[16,640,256]{2,1,0:T(8,128)(2,1)}, u32[]{:S(2)}, u32[]{:S(2)}) async-start(bf16[16,640,256]{2,1,0:T(8,128)(2,1)} %self_energy_0.1), calls=%async_computation.2 | async-start | bytes 10485760 | tf_op jit(solution)/shard_map/all_to_all | solution.py:267
  130.2 25.4 %copy-start.1 = (bf16[1,16,32,256]{3,2,1,0:T(8,128)(2,1)}, bf16[1,16,32,256]{3,2,1,0:T(8,128)(2,1)S(1)}, u32[]{:S(2)}) copy-start(bf16[1,16,32,256]{3,2,1,0:T(8,128)(2,1)S(1)} %slice_bitcast_fusion) | copy-start | bytes 786436
  130.2 7.5 %collective-permute-start.2 = (bf16[1,16,32,256]{3,2,1,0:T(8,128)(2,1)S(1)}, bf16[1,16,32,256]{3,2,1,0:T(8,128)(2,1)S(1)}, u32[]{:S(2)}, u32[]{:S(2)}) collective-permute-start(bf16[1,16,32,256]{3,2,1,0:T(8,128)(2,1)S(1)} %slice_bitcast_fusion), channel_id=1, source_target_pairs={{0,32},{16,48},{32,0},{48,16},{64,96},{80,112},{96,64},{112,80},{1... | collective-permute-start | bytes 786440 | tf_op jit(solution)/shard_map/ppermute | solution.py:291
  137.7 25.0 %copy-start.3 = (bf16[1,16,32,256]{3,2,1,0:T(8,128)(2,1)}, bf16[1,16,32,256]{3,2,1,0:T(8,128)(2,1)S(1)}, u32[]{:S(2)}) copy-start(bf16[1,16,32,256]{3,2,1,0:T(8,128)(2,1)S(1)} %collective-permute-done.2) | copy-start | bytes 786436
  137.8 11.3 %collective-permute-start.3 = (bf16[2,16,32,256]{3,2,1,0:T(8,128)(2,1)S(1)}, bf16[2,16,32,256]{3,2,1,0:T(8,128)(2,1)S(1)}, u32[]{:S(2)}, u32[]{:S(2)}) collective-permute-start(bf16[2,16,32,256]{3,2,1,0:T(8,128)(2,1)S(1)} %pad_maximum_fusion.2), channel_id=1, source_target_pairs={{0,64},{16,80},{32,96},{48,112},{64,0},{80,16},{96,32},{112,48},{1... | collective-permute-start | bytes 1572872 | tf_op jit(solution)/shard_map/ppermute | solution.py:291
  149.1 13.7 %copy-start.5 = (bf16[2,16,32,256]{3,2,1,0:T(8,128)(2,1)}, bf16[2,16,32,256]{3,2,1,0:T(8,128)(2,1)S(1)}, u32[]{:S(2)}) copy-start(bf16[2,16,32,256]{3,2,1,0:T(8,128)(2,1)S(1)} %collective-permute-done.3) | copy-start | bytes 1572868
  150.2 23.2 %collective-permute-start.4 = (bf16[4,16,32,256]{3,2,1,0:T(8,128)(2,1)}, bf16[4,16,32,256]{3,2,1,0:T(8,128)(2,1)}, u32[]{:S(2)}, u32[]{:S(2)}) collective-permute-start(bf16[4,16,32,256]{3,2,1,0:T(8,128)(2,1)} %pad_maximum_fusion.1), channel_id=1, source_target_pairs={{0,16},{16,0},{32,48},{48,32},{64,80},{80,64},{96,112},{112,96},{1... | collective-permute-start | bytes 3145736 | tf_op jit(solution)/shard_map/ppermute | solution.py:291
  150.3 12.4 %collective-permute-start.1 = (bf16[4,384,256]{2,1,0:T(8,128)(2,1)S(1)}, bf16[4,384,256]{2,1,0:T(8,128)(2,1)S(1)}, u32[]{:S(2)}, u32[]{:S(2)}) collective-permute-start(bf16[4,384,256]{2,1,0:T(8,128)(2,1)S(1)} %get-tuple-element.25), channel_id=1, source_target_pairs={{16,0},{32,16},{48,32},{64,48},{80,64},{96,80},{112,96},{17,1},{33... | collective-permute-start | bytes 2359304 | tf_op jit(solution)/shard_map/ppermute | solution.py:283
  153.3 13.4 %collective-permute-start = (bf16[4,384,256]{2,1,0:T(8,128)(2,1)S(1)}, bf16[4,384,256]{2,1,0:T(8,128)(2,1)}, u32[]{:S(2)}, u32[]{:S(2)}) collective-permute-start(bf16[4,384,256]{2,1,0:T(8,128)(2,1)S(1)} %get-tuple-element.26), channel_id=1, source_target_pairs={{0,16},{16,32},{32,48},{48,64},{64,80},{80,96},{96,112},{1,17},{17... | collective-permute-start | bytes 2359304 | tf_op jit(solution)/shard_map/ppermute | solution.py:282
  162.7 0.9 copy-start.7
  163.6 9.7 %copy-start.2 = (bf16[1,16,32,256]{3,2,1,0:T(8,128)(2,1)S(1)}, bf16[1,16,32,256]{3,2,1,0:T(8,128)(2,1)}, u32[]{:S(2)}) copy-start(bf16[1,16,32,256]{3,2,1,0:T(8,128)(2,1)} %copy-done.1) | copy-start | bytes 786436
  166.7 6.7 %copy-start.4 = (bf16[1,16,32,256]{3,2,1,0:T(8,128)(2,1)S(1)}, bf16[1,16,32,256]{3,2,1,0:T(8,128)(2,1)}, u32[]{:S(2)}) copy-start(bf16[1,16,32,256]{3,2,1,0:T(8,128)(2,1)} %copy-done.3) | copy-start | bytes 786436
  166.7 6.7 %copy-start.6 = (bf16[2,16,32,256]{3,2,1,0:T(8,128)(2,1)S(1)}, bf16[2,16,32,256]{3,2,1,0:T(8,128)(2,1)}, u32[]{:S(2)}) copy-start(bf16[2,16,32,256]{3,2,1,0:T(8,128)(2,1)} %copy-done.5) | copy-start | bytes 1572868
  193.1 43.2 %all-to-all-start.3 = ((bf16[16,384,256]{2,1,0:T(8,128)(2,1)}), bf16[16,384,256]{2,1,0:T(8,128)(2,1)S(1)}, u32[]{:S(2)}, u32[]{:S(2)}) async-start(bf16[16,384,256]{2,1,0:T(8,128)(2,1)} %self_energy_1.1), calls=%async_computation.3 | async-start | bytes 6291456 | tf_op jit(solution)/shard_map/all_to_all | solution.py:267

commit v7 on v6

--- a/solution.py
+++ b/solution.py
@@ -116,17 +116,17 @@
     g_real, g_imag = green[0, 0], green[0, 1]
     g_minus = jnp.concatenate([g_real, -g_imag], axis=1)
     g_plus = jnp.concatenate([g_real, g_imag], axis=1)
-    stacked = []
     for k in (0, 2):
         inner_real = dot(g_minus, jnp.concatenate([source[k], source[k + 1]], axis=0)).astype(narrow)
         inner_imag = dot(g_plus, jnp.concatenate([source[k + 1], source[k]], axis=0)).astype(narrow)
-        stacked.append(jnp.concatenate([inner_real, inner_imag], axis=1))
-        stacked.append(jnp.concatenate([inner_imag, -inner_real], axis=1))
-    outer = dot_transposed(jnp.concatenate(stacked, axis=0), g_plus).astype(narrow)
-    held[...] = outer
-    out[0] = outer
-    if last is not None:
-        last[0] = outer
+        upper = jnp.concatenate([inner_real, inner_imag], axis=1)
+        lower = jnp.concatenate([inner_imag, -inner_real], axis=1)
+        outer = dot_transposed(jnp.concatenate([upper, lower], axis=0), g_plus).astype(narrow)
+        part = slice(k * orbitals, (k + 2) * orbitals)
+        held[part] = outer
+        out[0, part] = outer
+        if last is not None:
+            last[0, part] = outer
 
 
 def sweep(first, layers, group, live, lead, sigma, green, couplings, whole=None):

time: 352 us -> 353 us (level)
  no operation moved by 1% of the time
where the time goes in v7:
time: 353 us; the launch traced here: 351 us
  blocking collectives  171 us (48%)
  waiting for transfers between devices  89.7 us (25%)
  Pallas kernels  51.1 us (14%)
  starting transfers between devices  28.6 us (8%)
  local copies, waits for them, and re-layouts  5.2 us (1%)
  other arithmetic  4.65 us (1%)
    all_to_all x2, blocking collectives, exchange(): lax.all_to_all(block, 'layer', split_axis=0, concat_axis=0, tiled=True)  171 us
    all_to_all x3, waiting for transfers between devices, exchange(): lax.all_to_all(block, 'layer', split_axis=0, concat_axis=0, tiled=True)  49.7 us
    pallas_call x2, Pallas kernels, sweep(): pl.pallas_call(functools.partial(sweep_kernel, first), grid_spec=pltpu.Pr...  26.4 us
    ppermute x2, waiting for transfers between devices, halo_of(): high = lax.ppermute(block[:SHIFT_MAX], 'energy', backward)  19.1 us
    pallas_call x2, Pallas kernels, self_energy(): pl.pallas_call(sigma_kernel, grid=(rows // share,), in_specs=[pl.BlockSpe...  16.3 us
    all_to_all x3, starting transfers between devices, exchange(): lax.all_to_all(block, 'layer', split_axis=0, concat_axis=0, tiled=True)  14.8 us
    ppermute x3, waiting for transfers between devices, all_couplings(): other = lax.ppermute(held, 'energy', [(i, i ^ bit) for i in range(count)])  14.1 us
  transfers between devices with their start and end apart: 10, of which 9 were waited for; matrix products, arithmetic and copies ran while one was open for 3% of the time, Pallas kernels for 9%

profile of v7, /device:TPU:8, one launch (start us, length us, event | category | flops | bytes accessed | tf_op | source)
XLA Modules:
  0.0 351.4 jit_solution(5767384147255692517)
XLA Ops:
  0.7 5.0 %pick.1 = (bf16[16,640,256]{2,1,0:T(8,128)(2,1)S(1)}, bf16[16,424,256]{2,1,0:T(8,128)(2,1)}) custom-call(bf16[16,16,64,256]{3,2,1,0:T(8,128)(2,1)} %bitcast.16, bf16[1,256,256]{2,1,0:T(8,128)(2,1)} %coupling.1, bf16[8,256]{1,0:T(8,128)(2,1)S(1)} %broadcast_in_dim.20.live), custom_call_target="tpu_custom_call" | custom-call | bytes 16777216 | tf_op jit(solution)/shard_map/pick/pallas_call | solution.py:221
  5.7 69.9 %all_to_all.25.here = bf16[16,640,256]{2,1,0:T(8,128)(2,1)} all-to-all(bf16[16,640,256]{2,1,0:T(8,128)(2,1)S(1)} %get-tuple-element.14), channel_id=1, replica_groups=mesh['energy'=8,'layer'=16] {'layer'}, dimensions={0} | all-to-all | bytes 10485760 | tf_op jit(solution)/shard_map/all_to_all | solution.py:267
  75.6 4.2 %all-to-all-start = ((bf16[16,424,256]{2,1,0:T(8,128)(2,1)}), bf16[16,424,256]{2,1,0:T(8,128)(2,1)S(1)}, u32[]{:S(2)}, u32[]{:S(2)}) async-start(bf16[16,424,256]{2,1,0:T(8,128)(2,1)} %get-tuple-element.12), calls=%async_computation | async-start | bytes 6946816 | tf_op jit(solution)/shard_map/all_to_all | solution.py:267
  79.9 3.4 fusion.4
  88.7 11.9 %collective-permute-done.6.high = bf16[4,640,256]{2,1,0:T(8,128)(2,1)} collective-permute-done((bf16[4,640,256]{2,1,0:T(8,128)(2,1)}, bf16[4,640,256]{2,1,0:T(8,128)(2,1)}, u32[]{:S(2)}, u32[]{:S(2)}) %collective-permute-start.6) | collective-permute-done | bytes 1310752 | tf_op jit(solution)/shard_map/ppermute | solution.py:283
  100.6 3.8 %collective-permute-done.5.low = bf16[4,640,256]{2,1,0:T(8,128)(2,1)} collective-permute-done((bf16[4,640,256]{2,1,0:T(8,128)(2,1)}, bf16[4,640,256]{2,1,0:T(8,128)(2,1)}, u32[]{:S(2)}, u32[]{:S(2)}) %collective-permute-start.5) | collective-permute-done | bytes 1310752 | tf_op jit(solution)/shard_map/ppermute | solution.py:282
  104.4 9.6 %self_energy_0.1 = bf16[16,640,256]{2,1,0:T(8,128)(2,1)} custom-call(f32[8]{0:T(128)} %dynamic-slice_bitcast_fusion.weights, bf16[4,640,256]{2,1,0:T(8,128)(2,1)} %collective-permute-done.5.low, bf16[16,640,256]{2,1,0:T(8,128)(2,1)} %all_to_all.25.here, bf16[4,640,256]{2,1,0:T(8,128)(2,1)} %collective-permute-done.6.high), custom_call_target="tpu_custom_call" | custom-call | flops 41943040 | bytes 13107200 | tf_op jit(solution)/shard_map/self_energy_0/pallas_call | solution.py:63
  114.0 11.6 %all-to-all-done.here = bf16[16,424,256]{2,1,0:T(8,128)(2,1)S(1)} async-done(((bf16[16,424,256]{2,1,0:T(8,128)(2,1)}), bf16[16,424,256]{2,1,0:T(8,128)(2,1)S(1)}, u32[]{:S(2)}, u32[]{:S(2)}) %all-to-all-start) | async-done | bytes 3473440 | tf_op jit(solution)/shard_map/all_to_all | solution.py:267
  125.6 4.6 %all-to-all-start.2 = ((bf16[16,640,256]{2,1,0:T(8,128)(2,1)}), bf16[16,640,256]{2,1,0:T(8,128)(2,1)}, u32[]{:S(2)}, u32[]{:S(2)}) async-start(bf16[16,640,256]{2,1,0:T(8,128)(2,1)} %self_energy_0.1), calls=%async_computation.2 | async-start | bytes 10485760 | tf_op jit(solution)/shard_map/all_to_all | solution.py:267
  130.7 7.0 %collective-permute-done.2 = bf16[1,16,32,256]{3,2,1,0:T(8,128)(2,1)S(1)} collective-permute-done((bf16[1,16,32,256]{3,2,1,0:T(8,128)(2,1)S(1)}, bf16[1,16,32,256]{3,2,1,0:T(8,128)(2,1)S(1)}, u32[]{:S(2)}, u32[]{:S(2)}) %collective-permute-start.2) | collective-permute-done | bytes 262176 | tf_op jit(solution)/shard_map/ppermute | solution.py:291
  137.8 4.1 %collective-permute-start.3 = (bf16[2,16,32,256]{3,2,1,0:T(8,128)(2,1)S(1)}, bf16[2,16,32,256]{3,2,1,0:T(8,128)(2,1)S(1)}, u32[]{:S(2)}, u32[]{:S(2)}) collective-permute-start(bf16[2,16,32,256]{3,2,1,0:T(8,128)(2,1)S(1)} %pad_maximum_fusion.2), channel_id=1, source_target_pairs={{0,64},{16,80},{32,96},{48,112},{64,0},{80,16},{96,32},{112,48},{1... | collective-permute-start | bytes 1572872 | tf_op jit(solution)/shard_map/ppermute | solution.py:291
  141.9 7.2 %collective-permute-done.3 = bf16[2,16,32,256]{3,2,1,0:T(8,128)(2,1)S(1)} collective-permute-done((bf16[2,16,32,256]{3,2,1,0:T(8,128)(2,1)S(1)}, bf16[2,16,32,256]{3,2,1,0:T(8,128)(2,1)S(1)}, u32[]{:S(2)}, u32[]{:S(2)}) %collective-permute-start.3) | collective-permute-done | bytes 524320 | tf_op jit(solution)/shard_map/ppermute | solution.py:291
  150.3 2.9 collective-permute-start.1
  155.6 7.2 %collective-permute-done.1.high = bf16[4,384,256]{2,1,0:T(8,128)(2,1)S(1)} collective-permute-done((bf16[4,384,256]{2,1,0:T(8,128)(2,1)S(1)}, bf16[4,384,256]{2,1,0:T(8,128)(2,1)S(1)}, u32[]{:S(2)}, u32[]{:S(2)}) %collective-permute-start.1) | collective-permute-done | bytes 786464 | tf_op jit(solution)/shard_map/ppermute | solution.py:283
  163.6 3.0 collective-permute-done.low
  166.7 6.7 %self_energy_1.1 = bf16[16,384,256]{2,1,0:T(8,128)(2,1)} custom-call(f32[8]{0:T(128)} %dynamic-slice_bitcast_fusion.weights, bf16[4,384,256]{2,1,0:T(8,128)(2,1)} %collective-permute-done.low, bf16[16,424,256]{2,1,0:T(8,128)(2,1)} %copy-done, bf16[4,384,256]{2,1,0:T(8,128)(2,1)} %copy-done.7), custom_call_target="tpu_custom_call" | custom-call | flops 25165824 | bytes 7864320 | tf_op jit(solution)/shard_map/self_energy_1/pallas_call | solution.py:63
  173.4 2.8 pad_maximum_fusion.coupling
  176.2 16.9 %all-to-all-done.2.sigma = bf16[16,640,256]{2,1,0:T(8,128)(2,1)} async-done(((bf16[16,640,256]{2,1,0:T(8,128)(2,1)}), bf16[16,640,256]{2,1,0:T(8,128)(2,1)}, u32[]{:S(2)}, u32[]{:S(2)}) %all-to-all-start.2) | async-done | bytes 5242912 | tf_op jit(solution)/shard_map/all_to_all | solution.py:267
  193.1 6.0 %all-to-all-start.3 = ((bf16[16,384,256]{2,1,0:T(8,128)(2,1)}), bf16[16,384,256]{2,1,0:T(8,128)(2,1)S(1)}, u32[]{:S(2)}, u32[]{:S(2)}) async-start(bf16[16,384,256]{2,1,0:T(8,128)(2,1)} %self_energy_1.1), calls=%async_computation.3 | async-start | bytes 6291456 | tf_op jit(solution)/shard_map/all_to_all | solution.py:267
  199.1 16.0 %sweep_0.1 = (bf16[16,1024,256]{2,1,0:T(8,128)(2,1)}, bf16[1,1024,256]{2,1,0:T(8,128)(2,1)}) custom-call(s32[1]{0:T(128)} %bitcast.group, s32[16]{0:T(128)S(1)} %fusion.live, bf16[16,1024,256]{2,1,0:T(8,128)(2,1)} %bitcast.17, bf16[16,640,256]{2,1,0:T(8,128)(2,1)} %all-to-all-done.2.sigma, bf16[16,2,256,256]{3,2,1,0:T(8,128)(2,1)} %bitcast.18, ...), custom_call_target="tpu_custom_call" | custom-call | flops 8053063680 | bytes 18350080 | tf_op jit(solution)/shard_map/sweep_0/pallas_call | solution.py:155
  215.1 21.2 %all-to-all-done.3.sigma = bf16[16,384,256]{2,1,0:T(8,128)(2,1)S(1)} async-done(((bf16[16,384,256]{2,1,0:T(8,128)(2,1)}), bf16[16,384,256]{2,1,0:T(8,128)(2,1)S(1)}, u32[]{:S(2)}, u32[]{:S(2)}) %all-to-all-start.3) | async-done | bytes 3145760 | tf_op jit(solution)/shard_map/all_to_all | solution.py:267
  236.3 10.4 %sweep_10.1 = bf16[16,1024,256]{2,1,0:T(8,128)(2,1)} custom-call(s32[1]{0:T(128)} %bitcast.group, s32[16]{0:T(128)S(1)} %fusion.live, bf16[1,1024,256]{2,1,0:T(8,128)(2,1)} %get-tuple-element.16.lead, bf16[16,384,256]{2,1,0:T(8,128)(2,1)S(1)} %all-to-all-done.3.sigma, bf16[16,2,256,256]{3,2,1,0:T(8,128)(2,1)} %bitcast.19, ...), custom_call_target="tpu_custom_call", output_to_operand_aliasing={{}: (6, {})} | custom-call | flops 4831838208 | bytes 11010048 | tf_op jit(solution)/shard_map/sweep_10/pallas_call | solution.py:155
  246.7 101.3 %all_to_all.26.source = bf16[16,1024,256]{2,1,0:T(8,128)(2,1)S(1)} all-to-all(bf16[16,1024,256]{2,1,0:T(8,128)(2,1)} %sweep_10.1), channel_id=1, replica_groups=mesh['energy'=8,'layer'=16] {'layer'}, dimensions={0} | all-to-all | bytes 16777216 | tf_op jit(solution)/shard_map/all_to_all | solution.py:267
  348.0 3.4 settle.1
  (41 shorter events, 10.4 us)
Async XLA Ops:
  75.6 49.9 %all-to-all-start = ((bf16[16,424,256]{2,1,0:T(8,128)(2,1)}), bf16[16,424,256]{2,1,0:T(8,128)(2,1)S(1)}, u32[]{:S(2)}, u32[]{:S(2)}) async-start(bf16[16,424,256]{2,1,0:T(8,128)(2,1)} %get-tuple-element.12), calls=%async_computation | async-start | bytes 6946816 | tf_op jit(solution)/shard_map/all_to_all | solution.py:267
  79.8 7.8 %copy-start.8 = (s32[4]{0:T(128)S(1)}, s32[4]{0:T(128)}, u32[]{:S(2)}) copy-start(s32[4]{0:T(128)} %param.9) | copy-start | bytes 52
  79.9 7.8 %copy-start.9 = (f32[4]{0:T(128)S(1)}, f32[4]{0:T(128)}, u32[]{:S(2)}) copy-start(f32[4]{0:T(128)} %param.10) | copy-start | bytes 52
  83.3 17.3 %collective-permute-start.6 = (bf16[4,640,256]{2,1,0:T(8,128)(2,1)}, bf16[4,640,256]{2,1,0:T(8,128)(2,1)}, u32[]{:S(2)}, u32[]{:S(2)}) collective-permute-start(bf16[4,640,256]{2,1,0:T(8,128)(2,1)} %get-tuple-element.23), channel_id=1, source_target_pairs={{16,0},{32,16},{48,32},{64,48},{80,64},{96,80},{112,96},{17,1},{33... | collective-permute-start | bytes 3932168 | tf_op jit(solution)/shard_map/ppermute | solution.py:283
  85.2 19.2 %collective-permute-start.5 = (bf16[4,640,256]{2,1,0:T(8,128)(2,1)}, bf16[4,640,256]{2,1,0:T(8,128)(2,1)}, u32[]{:S(2)}, u32[]{:S(2)}) collective-permute-start(bf16[4,640,256]{2,1,0:T(8,128)(2,1)} %get-tuple-element.24), channel_id=1, source_target_pairs={{0,16},{16,32},{32,48},{48,64},{64,80},{80,96},{96,112},{1,17},{17... | collective-permute-start | bytes 3932168 | tf_op jit(solution)/shard_map/ppermute | solution.py:282
  125.6 29.6 %copy-start = (bf16[16,424,256]{2,1,0:T(8,128)(2,1)}, bf16[16,424,256]{2,1,0:T(8,128)(2,1)S(1)}, u32[]{:S(2)}) copy-start(bf16[16,424,256]{2,1,0:T(8,128)(2,1)S(1)} %all-to-all-done.here) | copy-start | bytes 10420228
  125.6 67.5 %all-to-all-start.2 = ((bf16[16,640,256]{2,1,0:T(8,128)(2,1)}), bf16[16,640,256]{2,1,0:T(8,128)(2,1)}, u32[]{:S(2)}, u32[]{:S(2)}) async-start(bf16[16,640,256]{2,1,0:T(8,128)(2,1)} %self_energy_0.1), calls=%async_computation.2 | async-start | bytes 10485760 | tf_op jit(solution)/shard_map/all_to_all | solution.py:267
  130.2 25.4 %copy-start.1 = (bf16[1,16,32,256]{3,2,1,0:T(8,128)(2,1)}, bf16[1,16,32,256]{3,2,1,0:T(8,128)(2,1)S(1)}, u32[]{:S(2)}) copy-start(bf16[1,16,32,256]{3,2,1,0:T(8,128)(2,1)S(1)} %slice_bitcast_fusion) | copy-start | bytes 786436
  130.2 7.5 %collective-permute-start.2 = (bf16[1,16,32,256]{3,2,1,0:T(8,128)(2,1)S(1)}, bf16[1,16,32,256]{3,2,1,0:T(8,128)(2,1)S(1)}, u32[]{:S(2)}, u32[]{:S(2)}) collective-permute-start(bf16[1,16,32,256]{3,2,1,0:T(8,128)(2,1)S(1)} %slice_bitcast_fusion), channel_id=1, source_target_pairs={{0,32},{16,48},{32,0},{48,16},{64,96},{80,112},{96,64},{112,80},{1... | collective-permute-start | bytes 786440 | tf_op jit(solution)/shard_map/ppermute | solution.py:291
  137.7 25.0 %copy-start.3 = (bf16[1,16,32,256]{3,2,1,0:T(8,128)(2,1)}, bf16[1,16,32,256]{3,2,1,0:T(8,128)(2,1)S(1)}, u32[]{:S(2)}) copy-start(bf16[1,16,32,256]{3,2,1,0:T(8,128)(2,1)S(1)} %collective-permute-done.2) | copy-start | bytes 786436
  137.8 11.3 %collective-permute-start.3 = (bf16[2,16,32,256]{3,2,1,0:T(8,128)(2,1)S(1)}, bf16[2,16,32,256]{3,2,1,0:T(8,128)(2,1)S(1)}, u32[]{:S(2)}, u32[]{:S(2)}) collective-permute-start(bf16[2,16,32,256]{3,2,1,0:T(8,128)(2,1)S(1)} %pad_maximum_fusion.2), channel_id=1, source_target_pairs={{0,64},{16,80},{32,96},{48,112},{64,0},{80,16},{96,32},{112,48},{1... | collective-permute-start | bytes 1572872 | tf_op jit(solution)/shard_map/ppermute | solution.py:291
  149.1 13.7 %copy-start.5 = (bf16[2,16,32,256]{3,2,1,0:T(8,128)(2,1)}, bf16[2,16,32,256]{3,2,1,0:T(8,128)(2,1)S(1)}, u32[]{:S(2)}) copy-start(bf16[2,16,32,256]{3,2,1,0:T(8,128)(2,1)S(1)} %collective-permute-done.3) | copy-start | bytes 1572868
  150.2 23.2 %collective-permute-start.4 = (bf16[4,16,32,256]{3,2,1,0:T(8,128)(2,1)}, bf16[4,16,32,256]{3,2,1,0:T(8,128)(2,1)}, u32[]{:S(2)}, u32[]{:S(2)}) collective-permute-start(bf16[4,16,32,256]{3,2,1,0:T(8,128)(2,1)} %pad_maximum_fusion.1), channel_id=1, source_target_pairs={{0,16},{16,0},{32,48},{48,32},{64,80},{80,64},{96,112},{112,96},{1... | collective-permute-start | bytes 3145736 | tf_op jit(solution)/shard_map/ppermute | solution.py:291
  150.3 12.4 %collective-permute-start.1 = (bf16[4,384,256]{2,1,0:T(8,128)(2,1)S(1)}, bf16[4,384,256]{2,1,0:T(8,128)(2,1)S(1)}, u32[]{:S(2)}, u32[]{:S(2)}) collective-permute-start(bf16[4,384,256]{2,1,0:T(8,128)(2,1)S(1)} %get-tuple-element.25), channel_id=1, source_target_pairs={{16,0},{32,16},{48,32},{64,48},{80,64},{96,80},{112,96},{17,1},{33... | collective-permute-start | bytes 2359304 | tf_op jit(solution)/shard_map/ppermute | solution.py:283
  153.3 13.4 %collective-permute-start = (bf16[4,384,256]{2,1,0:T(8,128)(2,1)S(1)}, bf16[4,384,256]{2,1,0:T(8,128)(2,1)}, u32[]{:S(2)}, u32[]{:S(2)}) collective-permute-start(bf16[4,384,256]{2,1,0:T(8,128)(2,1)S(1)} %get-tuple-element.26), channel_id=1, source_target_pairs={{0,16},{16,32},{32,48},{48,64},{64,80},{80,96},{96,112},{1,17},{17... | collective-permute-start | bytes 2359304 | tf_op jit(solution)/shard_map/ppermute | solution.py:282
  162.7 0.9 copy-start.7
  163.6 9.7 %copy-start.2 = (bf16[1,16,32,256]{3,2,1,0:T(8,128)(2,1)S(1)}, bf16[1,16,32,256]{3,2,1,0:T(8,128)(2,1)}, u32[]{:S(2)}) copy-start(bf16[1,16,32,256]{3,2,1,0:T(8,128)(2,1)} %copy-done.1) | copy-start | bytes 786436
  166.7 6.7 %copy-start.4 = (bf16[1,16,32,256]{3,2,1,0:T(8,128)(2,1)S(1)}, bf16[1,16,32,256]{3,2,1,0:T(8,128)(2,1)}, u32[]{:S(2)}) copy-start(bf16[1,16,32,256]{3,2,1,0:T(8,128)(2,1)} %copy-done.3) | copy-start | bytes 786436
  166.7 6.7 %copy-start.6 = (bf16[2,16,32,256]{3,2,1,0:T(8,128)(2,1)S(1)}, bf16[2,16,32,256]{3,2,1,0:T(8,128)(2,1)}, u32[]{:S(2)}) copy-start(bf16[2,16,32,256]{3,2,1,0:T(8,128)(2,1)} %copy-done.5) | copy-start | bytes 1572868
  193.1 43.2 %all-to-all-start.3 = ((bf16[16,384,256]{2,1,0:T(8,128)(2,1)}), bf16[16,384,256]{2,1,0:T(8,128)(2,1)S(1)}, u32[]{:S(2)}, u32[]{:S(2)}) async-start(bf16[16,384,256]{2,1,0:T(8,128)(2,1)} %self_energy_1.1), calls=%async_computation.3 | async-start | bytes 6291456 | tf_op jit(solution)/shard_map/all_to_all | solution.py:267
